TPU v7x, 512 devices: a whole 4x8x8 slice. The times are simulated.
512 devices in a mesh: gx: 32 (over z, x), gy: 16 (over y, core).
Axes of the slice: x: 4, y: 8, z: 8, core: 2. Of those that a mesh axis runs over, the one named last changes fastest.
Arguments:
- rhs_field: float32 [256, 128, 128], P('gx', 'gy'), may hold values from -6 to 6
- accumulation: float32 [256, 128, 128], P('gx', 'gy'), may hold values from 0.05 to 0.5
- trans_x: float32 [256, 128, 128], P('gx', 'gy'), may hold values from 0.1 to 10
- trans_y: float32 [256, 128, 128], P('gx', 'gy'), may hold values from 0.1 to 10
- trans_z: float32 [256, 128, 128], P('gx', 'gy'), may hold values from 0.02 to 2
- held_cells: int32 [4, 32, 32, 128], P(None, 'gx', 'gy'), may hold values from 0 to 8191
- perf_host: int32 [32, 32, 128], P('gx', 'gy'), may hold values from 0 to 3, as said below
- well_index: float32 [32, 32, 128], P('gx', 'gy'), may hold values from 0.1 to 2
- seg_cond: float32 [32, 32, 128], P('gx', 'gy'), may hold values from 0.5 to 4
- seg_rate: float32 [32, 32, 128], P('gx', 'gy'), may hold values from -6 to 6
Outputs:
- pressure: float32 [256, 128, 128], P('gx', 'gy')
- seg_pressure: float32 [32, 32, 128], P('gx', 'gy')
Inputs may be any that keep to these rules, and one draw needn't show every extreme that they name: `held_cells`: local cell numbers, x-major then y then layer. `perf_host`: nondecreasing along a well's slots, starting at 0 in slot 0 and ending at 3 in the last slot: the perforations on each device form one run of slots.
All inputs are finite; a program needn't handle non-finite values.
Results may differ from a plain program's by a relative error of at most 0.00002.
Values sent between devices are 32-bit elements; how exact they have to be, the bound alone decides.
No kernel may reach another device: no remote copies, remote signals or barrier semaphores. Data moves between devices by JAX's collectives and lax.ppermute only.
A program may use at most 64 MiB of HBM per device.

v0:
```python
import jax
import jax.numpy as jnp
from jax import lax
from jax.experimental import pallas as pl
from jax.experimental.pallas import tpu as pltpu
from jax.sharding import PartitionSpec as P

SWEEPS = 6
F32 = jnp.float32
BF16 = jnp.bfloat16


def split3(value):
    high = value.astype(BF16)
    rest = value - high.astype(F32)
    middle = rest.astype(BF16)
    low = (rest - middle.astype(F32)).astype(BF16)
    return high, middle, low


def iota(shape, dim):
    return lax.broadcasted_iota(jnp.int32, shape, dim)


def lane_onehot(idx, lanes):
    lane_of = idx & (lanes - 1)
    pieces = []
    for row in range(idx.shape[0]):
        hit = iota((lanes, idx.shape[1]), 0) == lane_of[row : row + 1, :]
        pieces.append(jnp.where(hit, F32(1.0), F32(0.0)).astype(BF16))
    return jnp.concatenate(pieces, axis=1)


def row_hit(idx, row, lanes, count):
    shift = lanes.bit_length() - 1
    row_of = lax.shift_right_logical(idx[row : row + 1, :], shift)
    return iota((count, idx.shape[1]), 0) == row_of


def scatter(flux, idx, lane_hot, count, lanes):
    parts = [part.astype(F32) for part in split3(flux)]
    columns = []
    for row in range(idx.shape[0]):
        hit = row_hit(idx, row, lanes, count)
        columns.append(
            jnp.concatenate(
                [jnp.where(hit, part[row : row + 1, :], F32(0.0)).astype(BF16) for part in parts],
                axis=0,
            )
        )
    spread = jnp.concatenate(columns, axis=1)
    out = lax.dot_general(
        spread, lane_hot, (((1,), (1,)), ((), ())), preferred_element_type=F32
    )
    return out[:count] + out[count : 2 * count] + out[2 * count :]


def gather(cells, idx, lane_hot, lanes):
    count = cells.shape[0]
    stacked = jnp.concatenate(split3(cells), axis=0)
    picked = lax.dot_general(
        stacked, lane_hot, (((1,), (0,)), ((), ())), preferred_element_type=F32
    )
    picked = picked[:count] + picked[count : 2 * count] + picked[2 * count :]
    slots = idx.shape[1]
    out = jnp.zeros(idx.shape, F32)
    for row in range(idx.shape[0]):
        part = jnp.where(
            row_hit(idx, row, lanes, count), picked[:, row * slots : (row + 1) * slots], F32(0.0)
        )
        total = jnp.sum(part, axis=0, keepdims=True)
        out = jnp.where(iota(idx.shape, 0) == row, total, out)
    return out


def well_update(rate, index, fm, seg, cell_p):
    slots = seg.shape[1]
    fp = pltpu.roll(fm, slots - 1, 1)
    seg_prev = pltpu.roll(seg, 1, 1)
    seg_next = pltpu.roll(seg, slots - 1, 1)
    seg_res = rate - (
        index * (seg - cell_p) + fm * (seg - seg_prev) + fp * (seg - seg_next)
    )
    return seg + F32(0.8) * seg_res / (index + fm + fp)


def y_shifted(block, edge, step):
    planes = []
    size = block.shape[1]
    for x in range(block.shape[0]):
        moved = pltpu.roll(block[x], (-step) % size, 0)
        at = size - 1 if step > 0 else 0
        planes.append(jnp.where(iota(moved.shape, 0) == at, edge[x : x + 1, :], moved))
    return planes


def z_shifted(plane, step):
    size = plane.shape[1]
    moved = pltpu.roll(plane, (-step) % size, 1)
    at = size - 1 if step > 0 else 0
    return jnp.where(iota(plane.shape, 1) == at, F32(0.0), moved)


def send_out(pos, ring, vals, p, send_ref, ylo_ref, yhi_ref, reach):
    width = p.shape[0]
    rows = vals.shape[0]
    send_ref[...] = jnp.zeros(send_ref.shape, F32)
    for d in range(1 - reach, reach):
        send_ref[lax.rem(pos + d + ring, ring), :rows, :] = vals
    send_ref[lax.rem(pos + 1, ring), rows:, :] = p[width - 1]
    send_ref[lax.rem(pos + ring - 1, ring), rows:, :] = p[0]
    for x in range(width):
        ylo_ref[x : x + 1, :] = p[x][:1, :]
        yhi_ref[x : x + 1, :] = p[x][-1:, :]


def pack_kernel(pos_ref, tx_ref, ty_ref, host_ref, index_ref, cond_ref, rate_ref, send_ref, yhi_ref, *, reach):
    pos = pos_ref[0]
    ring = send_ref.shape[0]
    width = tx_ref.shape[0]
    pack = jnp.concatenate(
        [host_ref[0].astype(F32), index_ref[0], cond_ref[0], rate_ref[0]], axis=0
    )
    rows = pack.shape[0]
    send_ref[...] = jnp.zeros(send_ref.shape, F32)
    for d in range(reach):
        send_ref[lax.rem(pos + d, ring), :rows, :] = pack
    send_ref[lax.rem(pos + 1, ring), rows:, :] = tx_ref[width - 1]
    for x in range(width):
        yhi_ref[x : x + 1, :] = ty_ref[x, ty_ref.shape[1] - 1 :, :]


def first_kernel(
    pos_ref, rhs_ref, acc_ref, tx_ref, ty_ref, tz_ref, recv_ref, wy_ref, held_ref,
    p_ref, gain_ref, wx_ref, seg_ref, well_ref, send_ref, ylo_ref, yhi_ref, *, reach, wells,
):
    pos = pos_ref[0]
    ring = recv_ref.shape[0]
    width, depth, lanes = rhs_ref.shape
    rows = reach * wells
    slots = lanes
    groups = []
    for array in range(4):
        whole = jnp.zeros((rows, slots), F32)
        for q in range(reach):
            piece = recv_ref[lax.rem(pos + ring - q, ring), :rows, :]
            moved = pltpu.roll(piece, (wells * (q - array)) % rows, 0) if q != array else piece
            whole = jnp.where(iota((rows, slots), 0) // wells == q, moved, whole)
        groups.append(whole)
    host, index, cond, rate = groups
    fm = jnp.where(iota((rows, slots), 1) > 0, cond, F32(0.0))
    well_ref[0], well_ref[1], well_ref[2], well_ref[3] = host, index, fm, rate
    zero = jnp.zeros((rows, slots), F32)
    seg = well_update(rate, index, fm, zero, zero)
    seg_ref[...] = seg
    flux = F32(0.0) - index * seg
    idx = held_ref[...].reshape(rows, slots)
    own = (iota((rows, slots), 0) // wells).astype(F32)
    flux = jnp.where(host == own, flux, F32(0.0))
    hot = lane_onehot(idx, lanes)
    count = width * depth
    well_term = scatter(flux, idx, hot, count, lanes).reshape(width, depth, lanes)
    west = jnp.where(pos == 0, F32(0.0), recv_ref[lax.rem(pos + ring - 1, ring), rows:, :])
    wx_ref[...] = west
    wy = y_shifted(ty_ref[...], wy_ref[...], -1)
    planes = []
    for x in range(width):
        tz = tz_ref[x]
        diag = acc_ref[x] + tx_ref[x] + (west if x == 0 else tx_ref[x - 1])
        diag = diag + ty_ref[x] + wy[x] + tz + z_shifted(tz, -1)
        gain = F32(0.7) / diag
        gain_ref[x] = gain
        planes.append(gain * (rhs_ref[x] - well_term[x]))
    for x in range(width):
        p_ref[x] = planes[x]
    cells = jnp.concatenate(planes, axis=0)
    vals = gather(cells, idx, hot, lanes)
    send_out(pos, ring, vals, planes_array(planes), send_ref, ylo_ref, yhi_ref, reach)


class planes_array:
    def __init__(self, planes):
        self.planes = planes
        self.shape = (len(planes), *planes[0].shape)

    def __getitem__(self, x):
        return self.planes[x]


def sweep_kernel(
    pos_ref, p_in, rhs_ref, tx_ref, ty_ref, tz_ref, gain_ref, wx_ref, wy_ref, recv_ref, south_ref, north_ref,
    seg_in, well_ref, held_ref, p_ref, seg_ref, *rest, reach, wells, last,
):
    pos = pos_ref[0]
    ring = recv_ref.shape[0]
    width, depth, lanes = rhs_ref.shape
    rows = reach * wells
    slots = lanes
    host, index, fm, rate = well_ref[0], well_ref[1], well_ref[2], well_ref[3]
    own_row = iota((rows, slots), 0) // wells
    cell_p = jnp.zeros((rows, slots), F32)
    for d in range(1 - reach, reach):
        piece = recv_ref[lax.rem(pos + d + ring, ring), :rows, :]
        moved = pltpu.roll(piece, (-wells * d) % rows, 0) if d else piece
        cell_p = jnp.where(host == (own_row + d).astype(F32), moved, cell_p)
    seg = well_update(rate, index, fm, seg_in[...], cell_p)
    if last:
        seg_ref[0] = seg[:wells]
    else:
        seg_ref[...] = seg
    flux = index * (cell_p - seg)
    flux = jnp.where(host == own_row.astype(F32), flux, F32(0.0))
    idx = held_ref[...].reshape(rows, slots)
    hot = lane_onehot(idx, lanes)
    count = width * depth
    well_term = scatter(flux, idx, hot, count, lanes).reshape(width, depth, lanes)
    west = jnp.where(pos == 0, F32(0.0), recv_ref[lax.rem(pos + ring - 1, ring), rows:, :])
    east = jnp.where(pos == ring - 1, F32(0.0), recv_ref[lax.rem(pos + 1, ring), rows:, :])
    block = p_in[...]
    wy = y_shifted(ty_ref[...], wy_ref[...], -1)
    south = y_shifted(block, south_ref[...], -1)
    north = y_shifted(block, north_ref[...], 1)
    planes = []
    for x in range(width):
        tz = tz_ref[x]
        total = rhs_ref[x] - well_term[x]
        total = total + tx_ref[x] * (east if x == width - 1 else block[x + 1])
        total = total + (wx_ref[...] * west if x == 0 else tx_ref[x - 1] * block[x - 1])
        total = total + ty_ref[x] * north[x] + wy[x] * south[x]
        total = total + tz * z_shifted(block[x], 1) + z_shifted(tz, -1) * z_shifted(block[x], -1)
        planes.append(F32(0.3) * block[x] + gain_ref[x] * total)
    for x in range(width):
        p_ref[x] = planes[x]
    if not last:
        send_ref, ylo_ref, yhi_ref = rest
        vals = gather(jnp.concatenate(planes, axis=0), idx, hot, lanes)
        send_out(pos, ring, vals, planes_array(planes), send_ref, ylo_ref, yhi_ref, reach)


def shards(
    rhs_field,
    accumulation,
    trans_x,
    trans_y,
    trans_z,
    held_cells,
    perf_host,
    well_index,
    seg_cond,
    seg_rate,
):
    width, depth, layers = rhs_field.shape
    reach = held_cells.shape[0]
    wells = well_index.shape[1]
    slots = well_index.shape[2]
    rows = reach * wells
    ring = lax.axis_size("gx")
    county = lax.axis_size("gy")
    up = [(j, j + 1) for j in range(county - 1)]
    down = [(target, source) for source, target in up]
    pos = lax.axis_index("gx").astype(jnp.int32).reshape(1)

    def shape(*dims):
        return jax.ShapeDtypeStruct(dims, F32)

    smem = pl.BlockSpec(memory_space=pltpu.SMEM)
    vmem = pl.BlockSpec(memory_space=pltpu.VMEM)

    def call(body, outs, *args, **static):
        return pl.pallas_call(
            lambda *refs: body(*refs, **static),
            out_shape=outs,
            in_specs=[smem] + [vmem] * (len(args) - 1),
            out_specs=[vmem] * len(outs),
        )(*args)

    message = shape(ring, rows + depth, slots)
    edge = shape(width, layers)
    block = shape(width, depth, layers)

    def exchanged(send):
        return lax.all_to_all(send, "gx", 0, 0, tiled=True)

    send, yhi = call(
        pack_kernel, [message, edge], pos, trans_x, trans_y, perf_host, well_index, seg_cond, seg_rate,
        reach=reach,
    )
    wy = lax.ppermute(yhi, "gy", up)
    recv = exchanged(send)
    p, gain, wx, seg, well, send, ylo, yhi = call(
        first_kernel,
        [block, block, shape(depth, layers), shape(rows, slots), shape(4, rows, slots), message, edge, edge],
        pos, rhs_field, accumulation, trans_x, trans_y, trans_z, recv, wy, held_cells,
        reach=reach, wells=wells,
    )
    for sweep in range(1, SWEEPS):
        last = sweep == SWEEPS - 1
        south = lax.ppermute(yhi, "gy", up)
        north = lax.ppermute(ylo, "gy", down)
        recv = exchanged(send)
        outs = [block, shape(1, wells, slots) if last else shape(rows, slots)]
        if not last:
            outs += [message, edge, edge]
        got = call(
            sweep_kernel, outs, pos, p, rhs_field, trans_x, trans_y, trans_z, gain, wx, wy, recv, south, north,
            seg, well, held_cells, reach=reach, wells=wells, last=last,
        )
        p, seg = got[:2]
        if not last:
            send, ylo, yhi = got[2:]
    return (p, seg)


def solution(mesh):
    return jax.shard_map(
        shards,
        mesh=mesh,
        in_specs=(
            P("gx", "gy", None),
            P("gx", "gy", None),
            P("gx", "gy", None),
            P("gx", "gy", None),
            P("gx", "gy", None),
            P(None, "gx", "gy", None),
            P("gx", "gy", None),
            P("gx", "gy", None),
            P("gx", "gy", None),
            P("gx", "gy", None),
        ),
        out_specs=(P("gx", "gy", None), P("gx", "gy", None)),
        check_vma=False,
    )
```

profile of v0, /device:TPU:25, one launch (start us, length us, event | category | flops | bytes accessed | tf_op | source)
XLA Modules:
  0.0 136.9 jit_solution(18076108743524349385)
XLA Ops:
  2.2 13.0 %all-to-all-start = ((f32[32,16,128]{2,1,0:T(8,128)}), f32[32,16,128]{2,1,0:T(8,128)S(1)}, u32[]{:S(2)}, u32[]{:S(2)}) async-start(f32[32,16,128]{2,1,0:T(8,128)} %get-tuple-element.32), calls=%async_computation | async-start | bytes 524288 | tf_op jit(solution)/shard_map/all_to_all | solution.py:282
  15.2 5.3 %collective-permute-start = (f32[8,128]{1,0:T(8,128)S(1)}, f32[8,128]{1,0:T(8,128)S(1)}, u32[]{:S(2)}, u32[]{:S(2)}) collective-permute-start(f32[8,128]{1,0:T(8,128)S(1)} %copy-done.27), channel_id=1, source_target_pairs={{0,1},{1,2},{2,3},{3,4},{4,5},{5,6},{6,7},{7,8},{8,9},{9,10},{10,1... | collective-permute-start | bytes 12296 | tf_op jit(solution)/shard_map/ppermute | solution.py:288
  21.2 5.2 %all-to-all-done.refs_6_ = f32[32,16,128]{2,1,0:T(8,128)S(1)} async-done(((f32[32,16,128]{2,1,0:T(8,128)}), f32[32,16,128]{2,1,0:T(8,128)S(1)}, u32[]{:S(2)}, u32[]{:S(2)}) %all-to-all-start) | async-done | bytes 262176 | tf_op jit(solution)/shard_map/all_to_all | solution.py:282
  27.1 2.4 %shard_map.114 = (f32[8,8,128]{2,1,0:T(8,128)}, f32[8,8,128]{2,1,0:T(8,128)}, f32[8,128]{1,0:T(8,128)}, f32[8,128]{1,0:T(8,128)}, f32[4,8,128]{2,1,0:T(8,128)}, ...) custom-call(s32[1]{0:T(128)} %bitcast.refs_0_, f32[8,8,128]{2,1,0:T(8,128)} %refs_2_.13, ...), custom_call_target="tpu_custom_call" | custom-call | tf_op jit(solution)/shard_map/pallas_call | solution.py:270
  29.5 4.9 %all-to-all-start.1 = ((f32[32,16,128]{2,1,0:T(8,128)}), f32[32,16,128]{2,1,0:T(8,128)S(1)}, u32[]{:S(2)}, u32[]{:S(2)}) async-start(f32[32,16,128]{2,1,0:T(8,128)} %get-tuple-element.37), calls=%async_computation.1 | async-start | bytes 524288 | tf_op jit(solution)/shard_map/all_to_all | solution.py:282
  34.5 5.9 %collective-permute-start.1 = (f32[8,128]{1,0:T(8,128)S(1)}, f32[8,128]{1,0:T(8,128)S(1)}, u32[]{:S(2)}, u32[]{:S(2)}) collective-permute-start(f32[8,128]{1,0:T(8,128)S(1)} %copy-done.26), channel_id=1, source_target_pairs={{0,1},{1,2},{2,3},{3,4},{4,5},{5,6},{6,7},{7,8},{8,9},{9,10},{10,1... | collective-permute-start | bytes 12296 | tf_op jit(solution)/shard_map/ppermute | solution.py:298
  42.4 4.5 %collective-permute-done.2.refs_11_ = f32[8,128]{1,0:T(8,128)S(1)} collective-permute-done((f32[8,128]{1,0:T(8,128)S(1)}, f32[8,128]{1,0:T(8,128)S(1)}, u32[]{:S(2)}, u32[]{:S(2)}) %collective-permute-start.2) | collective-permute-done | bytes 4128 | tf_op jit(solution)/shard_map/ppermute | solution.py:299
  47.6 2.5 %shard_map.115 = (f32[8,8,128]{2,1,0:T(8,128)}, f32[8,128]{1,0:T(8,128)}, f32[32,16,128]{2,1,0:T(8,128)}, f32[8,128]{1,0:T(8,128)}, f32[8,128]{1,0:T(8,128)}) custom-call(s32[1]{0:T(128)} %bitcast.refs_0_, f32[8,8,128]{2,1,0:T(8,128)} %get-tuple-element.34.refs_1_, f32[8,8,128]{2,1,0:T(8,128)} %refs_2_.13, f32[8,8,128]{2,1,0:T(8,128)} %refs_3_.13, ...), custom_call_target="tpu_custom_call" | custom-call | tf_op jit(solution)/shard_map/pallas_call | solution.py:270
  50.1 9.2 %all-to-all-start.2 = ((f32[32,16,128]{2,1,0:T(8,128)}), f32[32,16,128]{2,1,0:T(8,128)S(1)}, u32[]{:S(2)}, u32[]{:S(2)}) async-start(f32[32,16,128]{2,1,0:T(8,128)} %get-tuple-element.43), calls=%async_computation.2 | async-start | bytes 524288 | tf_op jit(solution)/shard_map/all_to_all | solution.py:282
  59.4 2.2 %collective-permute-start.3 = (f32[8,128]{1,0:T(8,128)S(1)}, f32[8,128]{1,0:T(8,128)S(1)}, u32[]{:S(2)}, u32[]{:S(2)}) collective-permute-start(f32[8,128]{1,0:T(8,128)S(1)} %copy-done.22), channel_id=1, source_target_pairs={{0,1},{1,2},{2,3},{3,4},{4,5},{5,6},{6,7},{7,8},{8,9},{9,10},{10,1... | collective-permute-start | bytes 12296 | tf_op jit(solution)/shard_map/ppermute | solution.py:298
  63.7 4.0 %collective-permute-done.4.refs_11_ = f32[8,128]{1,0:T(8,128)S(1)} collective-permute-done((f32[8,128]{1,0:T(8,128)S(1)}, f32[8,128]{1,0:T(8,128)S(1)}, u32[]{:S(2)}, u32[]{:S(2)}) %collective-permute-start.4) | collective-permute-done | bytes 4128 | tf_op jit(solution)/shard_map/ppermute | solution.py:299
  67.8 2.7 %all-to-all-done.2.refs_9_ = f32[32,16,128]{2,1,0:T(8,128)S(1)} async-done(((f32[32,16,128]{2,1,0:T(8,128)}), f32[32,16,128]{2,1,0:T(8,128)S(1)}, u32[]{:S(2)}, u32[]{:S(2)}) %all-to-all-start.2) | async-done | bytes 262176 | tf_op jit(solution)/shard_map/all_to_all | solution.py:282
  71.2 2.5 %shard_map.116 = (f32[8,8,128]{2,1,0:T(8,128)}, f32[8,128]{1,0:T(8,128)}, f32[32,16,128]{2,1,0:T(8,128)}, f32[8,128]{1,0:T(8,128)}, f32[8,128]{1,0:T(8,128)}) custom-call(s32[1]{0:T(128)} %bitcast.refs_0_, f32[8,8,128]{2,1,0:T(8,128)} %get-tuple-element.42.refs_1_, f32[8,8,128]{2,1,0:T(8,128)} %refs_2_.13, f32[8,8,128]{2,1,0:T(8,128)} %refs_3_.13, ...), custom_call_target="tpu_custom_call" | custom-call | tf_op jit(solution)/shard_map/pallas_call | solution.py:270
  73.8 6.8 %all-to-all-start.3 = ((f32[32,16,128]{2,1,0:T(8,128)}), f32[32,16,128]{2,1,0:T(8,128)S(1)}, u32[]{:S(2)}, u32[]{:S(2)}) async-start(f32[32,16,128]{2,1,0:T(8,128)} %get-tuple-element.48), calls=%async_computation.3 | async-start | bytes 524288 | tf_op jit(solution)/shard_map/all_to_all | solution.py:282
  84.9 4.1 %collective-permute-done.6.refs_11_ = f32[8,128]{1,0:T(8,128)S(1)} collective-permute-done((f32[8,128]{1,0:T(8,128)S(1)}, f32[8,128]{1,0:T(8,128)S(1)}, u32[]{:S(2)}, u32[]{:S(2)}) %collective-permute-start.6) | collective-permute-done | bytes 4128 | tf_op jit(solution)/shard_map/ppermute | solution.py:299
  89.0 2.8 %all-to-all-done.3.refs_9_ = f32[32,16,128]{2,1,0:T(8,128)S(1)} async-done(((f32[32,16,128]{2,1,0:T(8,128)}), f32[32,16,128]{2,1,0:T(8,128)S(1)}, u32[]{:S(2)}, u32[]{:S(2)}) %all-to-all-start.3) | async-done | bytes 262176 | tf_op jit(solution)/shard_map/all_to_all | solution.py:282
  92.5 2.5 %shard_map.117 = (f32[8,8,128]{2,1,0:T(8,128)}, f32[8,128]{1,0:T(8,128)}, f32[32,16,128]{2,1,0:T(8,128)}, f32[8,128]{1,0:T(8,128)}, f32[8,128]{1,0:T(8,128)}) custom-call(s32[1]{0:T(128)} %bitcast.refs_0_, f32[8,8,128]{2,1,0:T(8,128)} %get-tuple-element.47.refs_1_, f32[8,8,128]{2,1,0:T(8,128)} %refs_2_.13, f32[8,8,128]{2,1,0:T(8,128)} %refs_3_.13, ...), custom_call_target="tpu_custom_call" | custom-call | tf_op jit(solution)/shard_map/pallas_call | solution.py:270
  95.0 6.7 %all-to-all-start.4 = ((f32[32,16,128]{2,1,0:T(8,128)}), f32[32,16,128]{2,1,0:T(8,128)S(1)}, u32[]{:S(2)}, u32[]{:S(2)}) async-start(f32[32,16,128]{2,1,0:T(8,128)} %get-tuple-element.53), calls=%async_computation.4 | async-start | bytes 524288 | tf_op jit(solution)/shard_map/all_to_all | solution.py:282
  106.1 4.1 %collective-permute-done.8.refs_11_ = f32[8,128]{1,0:T(8,128)S(1)} collective-permute-done((f32[8,128]{1,0:T(8,128)S(1)}, f32[8,128]{1,0:T(8,128)S(1)}, u32[]{:S(2)}, u32[]{:S(2)}) %collective-permute-start.8) | collective-permute-done | bytes 4128 | tf_op jit(solution)/shard_map/ppermute | solution.py:299
  110.2 2.8 %all-to-all-done.4.refs_9_ = f32[32,16,128]{2,1,0:T(8,128)S(1)} async-done(((f32[32,16,128]{2,1,0:T(8,128)}), f32[32,16,128]{2,1,0:T(8,128)S(1)}, u32[]{:S(2)}, u32[]{:S(2)}) %all-to-all-start.4) | async-done | bytes 262176 | tf_op jit(solution)/shard_map/all_to_all | solution.py:282
  113.6 2.5 %shard_map.118 = (f32[8,8,128]{2,1,0:T(8,128)}, f32[8,128]{1,0:T(8,128)}, f32[32,16,128]{2,1,0:T(8,128)}, f32[8,128]{1,0:T(8,128)}, f32[8,128]{1,0:T(8,128)}) custom-call(s32[1]{0:T(128)} %bitcast.refs_0_, f32[8,8,128]{2,1,0:T(8,128)} %get-tuple-element.52.refs_1_, f32[8,8,128]{2,1,0:T(8,128)} %refs_2_.13, f32[8,8,128]{2,1,0:T(8,128)} %refs_3_.13, ...), custom_call_target="tpu_custom_call" | custom-call | tf_op jit(solution)/shard_map/pallas_call | solution.py:270
  116.2 6.7 %all-to-all-start.5 = ((f32[32,16,128]{2,1,0:T(8,128)}), f32[32,16,128]{2,1,0:T(8,128)S(1)}, u32[]{:S(2)}, u32[]{:S(2)}) async-start(f32[32,16,128]{2,1,0:T(8,128)} %get-tuple-element.58), calls=%async_computation.5 | async-start | bytes 524288 | tf_op jit(solution)/shard_map/all_to_all | solution.py:282
  127.3 4.1 %collective-permute-done.10.refs_11_ = f32[8,128]{1,0:T(8,128)S(1)} collective-permute-done((f32[8,128]{1,0:T(8,128)S(1)}, f32[8,128]{1,0:T(8,128)S(1)}, u32[]{:S(2)}, u32[]{:S(2)}) %collective-permute-start.10) | collective-permute-done | bytes 4128 | tf_op jit(solution)/shard_map/ppermute | solution.py:299
  131.3 2.8 %all-to-all-done.5.refs_9_ = f32[32,16,128]{2,1,0:T(8,128)S(1)} async-done(((f32[32,16,128]{2,1,0:T(8,128)}), f32[32,16,128]{2,1,0:T(8,128)S(1)}, u32[]{:S(2)}, u32[]{:S(2)}) %all-to-all-start.5) | async-done | bytes 262176 | tf_op jit(solution)/shard_map/all_to_all | solution.py:282
  (73 shorter events, 25.6 us)
Async XLA Ops:
  2.2 13.0 %copy-start.27 = (f32[8,128]{1,0:T(8,128)S(1)}, f32[8,128]{1,0:T(8,128)}, u32[]{:S(2)}) copy-start(f32[8,128]{1,0:T(8,128)} %get-tuple-element.33) | copy-start | bytes 12292
  2.2 24.2 %all-to-all-start = ((f32[32,16,128]{2,1,0:T(8,128)}), f32[32,16,128]{2,1,0:T(8,128)S(1)}, u32[]{:S(2)}, u32[]{:S(2)}) async-start(f32[32,16,128]{2,1,0:T(8,128)} %get-tuple-element.32), calls=%async_computation | async-start | bytes 524288 | tf_op jit(solution)/shard_map/all_to_all | solution.py:282
  15.2 6.0 %collective-permute-start = (f32[8,128]{1,0:T(8,128)S(1)}, f32[8,128]{1,0:T(8,128)S(1)}, u32[]{:S(2)}, u32[]{:S(2)}) collective-permute-start(f32[8,128]{1,0:T(8,128)S(1)} %copy-done.27), channel_id=1, source_target_pairs={{0,1},{1,2},{2,3},{3,4},{4,5},{5,6},{6,7},{7,8},{8,9},{9,10},{10,1... | collective-permute-start | bytes 12296 | tf_op jit(solution)/shard_map/ppermute | solution.py:288
  29.5 10.9 %copy-start.21 = (f32[8,128]{1,0:T(8,128)S(1)}, f32[8,128]{1,0:T(8,128)}, u32[]{:S(2)}) copy-start(f32[8,128]{1,0:T(8,128)} %get-tuple-element.39) | copy-start | bytes 12292
  29.5 17.3 %all-to-all-start.1 = ((f32[32,16,128]{2,1,0:T(8,128)}), f32[32,16,128]{2,1,0:T(8,128)S(1)}, u32[]{:S(2)}, u32[]{:S(2)}) async-start(f32[32,16,128]{2,1,0:T(8,128)} %get-tuple-element.37), calls=%async_computation.1 | async-start | bytes 524288 | tf_op jit(solution)/shard_map/all_to_all | solution.py:282
  34.5 7.9 %collective-permute-start.1 = (f32[8,128]{1,0:T(8,128)S(1)}, f32[8,128]{1,0:T(8,128)S(1)}, u32[]{:S(2)}, u32[]{:S(2)}) collective-permute-start(f32[8,128]{1,0:T(8,128)S(1)} %copy-done.26), channel_id=1, source_target_pairs={{0,1},{1,2},{2,3},{3,4},{4,5},{5,6},{6,7},{7,8},{8,9},{9,10},{10,1... | collective-permute-start | bytes 12296 | tf_op jit(solution)/shard_map/ppermute | solution.py:298
  40.4 6.4 %collective-permute-start.2 = (f32[8,128]{1,0:T(8,128)S(1)}, f32[8,128]{1,0:T(8,128)S(1)}, u32[]{:S(2)}, u32[]{:S(2)}) collective-permute-start(f32[8,128]{1,0:T(8,128)S(1)} %copy-done.21), channel_id=1, source_target_pairs={{1,0},{2,1},{3,2},{4,3},{5,4},{6,5},{7,6},{8,7},{9,8},{10,9},{11,1... | collective-permute-start | bytes 12296 | tf_op jit(solution)/shard_map/ppermute | solution.py:299
  50.1 9.2 %copy-start.22 = (f32[8,128]{1,0:T(8,128)S(1)}, f32[8,128]{1,0:T(8,128)}, u32[]{:S(2)}) copy-start(f32[8,128]{1,0:T(8,128)} %get-tuple-element.44) | copy-start | bytes 12292
  50.1 11.5 %copy-start.17 = (f32[8,128]{1,0:T(8,128)S(1)}, f32[8,128]{1,0:T(8,128)}, u32[]{:S(2)}) copy-start(f32[8,128]{1,0:T(8,128)} %get-tuple-element.45) | copy-start | bytes 12292
  50.1 20.4 %all-to-all-start.2 = ((f32[32,16,128]{2,1,0:T(8,128)}), f32[32,16,128]{2,1,0:T(8,128)S(1)}, u32[]{:S(2)}, u32[]{:S(2)}) async-start(f32[32,16,128]{2,1,0:T(8,128)} %get-tuple-element.43), calls=%async_computation.2 | async-start | bytes 524288 | tf_op jit(solution)/shard_map/all_to_all | solution.py:282
  59.4 4.4 %collective-permute-start.3 = (f32[8,128]{1,0:T(8,128)S(1)}, f32[8,128]{1,0:T(8,128)S(1)}, u32[]{:S(2)}, u32[]{:S(2)}) collective-permute-start(f32[8,128]{1,0:T(8,128)S(1)} %copy-done.22), channel_id=1, source_target_pairs={{0,1},{1,2},{2,3},{3,4},{4,5},{5,6},{6,7},{7,8},{8,9},{9,10},{10,1... | collective-permute-start | bytes 12296 | tf_op jit(solution)/shard_map/ppermute | solution.py:298
  61.6 6.1 %collective-permute-start.4 = (f32[8,128]{1,0:T(8,128)S(1)}, f32[8,128]{1,0:T(8,128)S(1)}, u32[]{:S(2)}, u32[]{:S(2)}) collective-permute-start(f32[8,128]{1,0:T(8,128)S(1)} %copy-done.17), channel_id=1, source_target_pairs={{1,0},{2,1},{3,2},{4,3},{5,4},{6,5},{7,6},{8,7},{9,8},{10,9},{11,1... | collective-permute-start | bytes 12296 | tf_op jit(solution)/shard_map/ppermute | solution.py:299
  73.7 9.0 %copy-start.18 = (f32[8,128]{1,0:T(8,128)S(1)}, f32[8,128]{1,0:T(8,128)}, u32[]{:S(2)}) copy-start(f32[8,128]{1,0:T(8,128)} %get-tuple-element.50) | copy-start | bytes 12292
  73.8 18.0 %all-to-all-start.3 = ((f32[32,16,128]{2,1,0:T(8,128)}), f32[32,16,128]{2,1,0:T(8,128)S(1)}, u32[]{:S(2)}, u32[]{:S(2)}) async-start(f32[32,16,128]{2,1,0:T(8,128)} %get-tuple-element.48), calls=%async_computation.3 | async-start | bytes 524288 | tf_op jit(solution)/shard_map/all_to_all | solution.py:282
  80.5 4.4 %collective-permute-start.5 = (f32[8,128]{1,0:T(8,128)S(1)}, f32[8,128]{1,0:T(8,128)S(1)}, u32[]{:S(2)}, u32[]{:S(2)}) collective-permute-start(f32[8,128]{1,0:T(8,128)S(1)} %copy-done.23), channel_id=1, source_target_pairs={{0,1},{1,2},{2,3},{3,4},{4,5},{5,6},{6,7},{7,8},{8,9},{9,10},{10,1... | collective-permute-start | bytes 12296 | tf_op jit(solution)/shard_map/ppermute | solution.py:298
  82.8 6.2 %collective-permute-start.6 = (f32[8,128]{1,0:T(8,128)S(1)}, f32[8,128]{1,0:T(8,128)S(1)}, u32[]{:S(2)}, u32[]{:S(2)}) collective-permute-start(f32[8,128]{1,0:T(8,128)S(1)} %copy-done.18), channel_id=1, source_target_pairs={{1,0},{2,1},{3,2},{4,3},{5,4},{6,5},{7,6},{8,7},{9,8},{10,9},{11,1... | collective-permute-start | bytes 12296 | tf_op jit(solution)/shard_map/ppermute | solution.py:299
  95.0 9.0 %copy-start.19 = (f32[8,128]{1,0:T(8,128)S(1)}, f32[8,128]{1,0:T(8,128)}, u32[]{:S(2)}) copy-start(f32[8,128]{1,0:T(8,128)} %get-tuple-element.55) | copy-start | bytes 12292
  95.0 17.9 %all-to-all-start.4 = ((f32[32,16,128]{2,1,0:T(8,128)}), f32[32,16,128]{2,1,0:T(8,128)S(1)}, u32[]{:S(2)}, u32[]{:S(2)}) async-start(f32[32,16,128]{2,1,0:T(8,128)} %get-tuple-element.53), calls=%async_computation.4 | async-start | bytes 524288 | tf_op jit(solution)/shard_map/all_to_all | solution.py:282
  101.7 4.4 %collective-permute-start.7 = (f32[8,128]{1,0:T(8,128)S(1)}, f32[8,128]{1,0:T(8,128)S(1)}, u32[]{:S(2)}, u32[]{:S(2)}) collective-permute-start(f32[8,128]{1,0:T(8,128)S(1)} %copy-done.24), channel_id=1, source_target_pairs={{0,1},{1,2},{2,3},{3,4},{4,5},{5,6},{6,7},{7,8},{8,9},{9,10},{10,1... | collective-permute-start | bytes 12296 | tf_op jit(solution)/shard_map/ppermute | solution.py:298
  104.0 6.2 %collective-permute-start.8 = (f32[8,128]{1,0:T(8,128)S(1)}, f32[8,128]{1,0:T(8,128)S(1)}, u32[]{:S(2)}, u32[]{:S(2)}) collective-permute-start(f32[8,128]{1,0:T(8,128)S(1)} %copy-done.19), channel_id=1, source_target_pairs={{1,0},{2,1},{3,2},{4,3},{5,4},{6,5},{7,6},{8,7},{9,8},{10,9},{11,1... | collective-permute-start | bytes 12296 | tf_op jit(solution)/shard_map/ppermute | solution.py:299
  116.2 9.0 %copy-start.20 = (f32[8,128]{1,0:T(8,128)S(1)}, f32[8,128]{1,0:T(8,128)}, u32[]{:S(2)}) copy-start(f32[8,128]{1,0:T(8,128)} %get-tuple-element.60) | copy-start | bytes 12292
  116.2 17.9 %all-to-all-start.5 = ((f32[32,16,128]{2,1,0:T(8,128)}), f32[32,16,128]{2,1,0:T(8,128)S(1)}, u32[]{:S(2)}, u32[]{:S(2)}) async-start(f32[32,16,128]{2,1,0:T(8,128)} %get-tuple-element.58), calls=%async_computation.5 | async-start | bytes 524288 | tf_op jit(solution)/shard_map/all_to_all | solution.py:282
  122.9 4.4 %collective-permute-start.9 = (f32[8,128]{1,0:T(8,128)S(1)}, f32[8,128]{1,0:T(8,128)S(1)}, u32[]{:S(2)}, u32[]{:S(2)}) collective-permute-start(f32[8,128]{1,0:T(8,128)S(1)} %copy-done.25), channel_id=1, source_target_pairs={{0,1},{1,2},{2,3},{3,4},{4,5},{5,6},{6,7},{7,8},{8,9},{9,10},{10,1... | collective-permute-start | bytes 12296 | tf_op jit(solution)/shard_map/ppermute | solution.py:298
  125.2 6.2 %collective-permute-start.10 = (f32[8,128]{1,0:T(8,128)S(1)}, f32[8,128]{1,0:T(8,128)S(1)}, u32[]{:S(2)}, u32[]{:S(2)}) collective-permute-start(f32[8,128]{1,0:T(8,128)S(1)} %copy-done.20), channel_id=1, source_target_pairs={{1,0},{2,1},{3,2},{4,3},{5,4},{6,5},{7,6},{8,7},{9,8},{10,9},{11,1... | collective-permute-start | bytes 12296 | tf_op jit(solution)/shard_map/ppermute | solution.py:299
  (21 other events, 78.1 us)
where the time goes:
time: 138 us; the launch traced here: 137 us
  starting transfers between devices  77.7 us (56%)
  waiting for transfers between devices  37.7 us (27%)
  Pallas kernels  16.1 us (12%)
  local copies, waits for them, and re-layouts  4.33 us (3%)
    all_to_all x6, starting transfers between devices, exchanged(): return lax.all_to_all(send, 'gx', 0, 0, tiled=True)  47.3 us
    ppermute x5, waiting for transfers between devices, shards(): north = lax.ppermute(ylo, 'gy', down)  20.7 us
    all_to_all x6, waiting for transfers between devices, exchanged(): return lax.all_to_all(send, 'gx', 0, 0, tiled=True)  16.3 us
    pallas_call x7, Pallas kernels, call(): pl.pallas_call(lambda *refs: body(*refs, **static), out_shape=outs, in_sp...  16.1 us
    ppermute x5, starting transfers between devices, shards(): south = lax.ppermute(yhi, 'gy', up)  14.9 us
    ppermute x5, starting transfers between devices, shards(): north = lax.ppermute(ylo, 'gy', down)  10.3 us
    ppermute x1, starting transfers between devices, shards(): wy = lax.ppermute(yhi, 'gy', up)  5.26 us
    unnamed x56, local copies, waits for them, and re-layouts  4.33 us
  transfers between devices with their start and end apart: 17, of which 11 were waited for; matrix products, arithmetic and copies ran while one was open for 0% of the time, Pallas kernels for 0%

commit v1 on v0

--- a/solution.py
+++ b/solution.py
@@ -261,7 +261,13 @@
     pos = lax.axis_index("gx").astype(jnp.int32).reshape(1)
 
     def shape(*dims):
+        return pltpu.VMEM(dims, F32)
+
+    def result(*dims):
         return jax.ShapeDtypeStruct(dims, F32)
+
+    def near(value):
+        return pltpu.with_memory_space_constraint(value, pltpu.VMEM)
 
     smem = pl.BlockSpec(memory_space=pltpu.SMEM)
     vmem = pl.BlockSpec(memory_space=pltpu.VMEM)
@@ -272,7 +278,7 @@
             out_shape=outs,
             in_specs=[smem] + [vmem] * (len(args) - 1),
             out_specs=[vmem] * len(outs),
-        )(*args)
+        )(args[0], *map(near, args[1:]))
 
     message = shape(ring, rows + depth, slots)
     edge = shape(width, layers)
@@ -298,7 +304,7 @@
         south = lax.ppermute(yhi, "gy", up)
         north = lax.ppermute(ylo, "gy", down)
         recv = exchanged(send)
-        outs = [block, shape(1, wells, slots) if last else shape(rows, slots)]
+        outs = [result(width, depth, layers), result(1, wells, slots)] if last else [block, shape(rows, slots)]
         if not last:
             outs += [message, edge, edge]
         got = call(

time: 138 us -> 128 us (0.928)
  Pallas kernels: 16.1 us -> 8.86 us
  local copies, waits for them, and re-layouts: 4.33 us -> 2.22 us
    pallas_call x7, Pallas kernels: 16.1 us -> 8.86 us  [call(): pl.pallas_call(lambda *refs: body(*refs, **static), out_shape=outs, in_sp...]
    unnamed x56 -> x20, local copies, waits for them, and re-layouts: 4.33 us -> 2.22 us
where the time goes in v1:
time: 128 us; the launch traced here: 127 us
  starting transfers between devices  77.6 us (61%)
  waiting for transfers between devices  37.8 us (30%)
  Pallas kernels  8.86 us (7%)
  local copies, waits for them, and re-layouts  2.22 us (2%)
    all_to_all x6, starting transfers between devices, exchanged(): return lax.all_to_all(send, 'gx', 0, 0, tiled=True)  47 us
    ppermute x5, waiting for transfers between devices, shards(): north = lax.ppermute(ylo, 'gy', down)  20.8 us
    all_to_all x6, waiting for transfers between devices, exchanged(): return lax.all_to_all(send, 'gx', 0, 0, tiled=True)  16.3 us
    ppermute x5, starting transfers between devices, shards(): south = lax.ppermute(yhi, 'gy', up)  15 us
    ppermute x5, starting transfers between devices, shards(): north = lax.ppermute(ylo, 'gy', down)  10.3 us
    pallas_call x7, Pallas kernels, call(): pl.pallas_call(lambda *refs: body(*refs, **static), out_shape=outs, in_sp...  8.86 us
    ppermute x1, starting transfers between devices, shards(): wy = lax.ppermute(yhi, 'gy', up)  5.26 us
  transfers between devices with their start and end apart: 17, of which 11 were waited for; matrix products, arithmetic and copies ran while one was open for 0% of the time, Pallas kernels for 0%

profile of v1, /device:TPU:25, one launch (start us, length us, event | category | flops | bytes accessed | tf_op | source)
XLA Modules:
  0.0 127.4 jit_solution(11732257824049961974)
XLA Ops:
  3.6 13.0 %all-to-all-start = ((f32[32,16,128]{2,1,0:T(8,128)}), f32[32,16,128]{2,1,0:T(8,128)S(1)}, u32[]{:S(2)}, u32[]{:S(2)}) async-start(f32[32,16,128]{2,1,0:T(8,128)} %get-tuple-element.32), calls=%async_computation | async-start | bytes 524288 | tf_op jit(solution)/shard_map/all_to_all | solution.py:288
  16.7 5.3 %collective-permute-start = (f32[8,128]{1,0:T(8,128)S(1)}, f32[8,128]{1,0:T(8,128)S(1)}, u32[]{:S(2)}, u32[]{:S(2)}) collective-permute-start(f32[8,128]{1,0:T(8,128)S(1)} %get-tuple-element.33), channel_id=1, source_target_pairs={{0,1},{1,2},{2,3},{3,4},{4,5},{5,6},{6,7},{7,8},{8,9},{9,10},{10,1... | collective-permute-start | bytes 12296 | tf_op jit(solution)/shard_map/ppermute | solution.py:294
  22.7 5.2 %all-to-all-done.refs_6_ = f32[32,16,128]{2,1,0:T(8,128)S(1)} async-done(((f32[32,16,128]{2,1,0:T(8,128)}), f32[32,16,128]{2,1,0:T(8,128)S(1)}, u32[]{:S(2)}, u32[]{:S(2)}) %all-to-all-start) | async-done | bytes 262176 | tf_op jit(solution)/shard_map/all_to_all | solution.py:288
  29.3 4.8 %all-to-all-start.1 = ((f32[32,16,128]{2,1,0:T(8,128)}), f32[32,16,128]{2,1,0:T(8,128)S(1)}, u32[]{:S(2)}, u32[]{:S(2)}) async-start(f32[32,16,128]{2,1,0:T(8,128)} %get-tuple-element.37), calls=%async_computation.1 | async-start | bytes 524288 | tf_op jit(solution)/shard_map/all_to_all | solution.py:288
  34.1 6.1 %collective-permute-start.1 = (f32[8,128]{1,0:T(8,128)S(1)}, f32[8,128]{1,0:T(8,128)S(1)}, u32[]{:S(2)}, u32[]{:S(2)}) collective-permute-start(f32[8,128]{1,0:T(8,128)S(1)} %get-tuple-element.38), channel_id=1, source_target_pairs={{0,1},{1,2},{2,3},{3,4},{4,5},{5,6},{6,7},{7,8},{8,9},{9,10},{10,1... | collective-permute-start | bytes 12296 | tf_op jit(solution)/shard_map/ppermute | solution.py:304
  42.1 4.5 %collective-permute-done.2.refs_11_ = f32[8,128]{1,0:T(8,128)S(1)} collective-permute-done((f32[8,128]{1,0:T(8,128)S(1)}, f32[8,128]{1,0:T(8,128)S(1)}, u32[]{:S(2)}, u32[]{:S(2)}) %collective-permute-start.2) | collective-permute-done | bytes 4128 | tf_op jit(solution)/shard_map/ppermute | solution.py:305
  48.1 9.2 %all-to-all-start.2 = ((f32[32,16,128]{2,1,0:T(8,128)}), f32[32,16,128]{2,1,0:T(8,128)S(1)}, u32[]{:S(2)}, u32[]{:S(2)}) async-start(f32[32,16,128]{2,1,0:T(8,128)} %get-tuple-element.43), calls=%async_computation.2 | async-start | bytes 524288 | tf_op jit(solution)/shard_map/all_to_all | solution.py:288
  57.3 2.2 %collective-permute-start.3 = (f32[8,128]{1,0:T(8,128)S(1)}, f32[8,128]{1,0:T(8,128)S(1)}, u32[]{:S(2)}, u32[]{:S(2)}) collective-permute-start(f32[8,128]{1,0:T(8,128)S(1)} %get-tuple-element.44), channel_id=1, source_target_pairs={{0,1},{1,2},{2,3},{3,4},{4,5},{5,6},{6,7},{7,8},{8,9},{9,10},{10,1... | collective-permute-start | bytes 12296 | tf_op jit(solution)/shard_map/ppermute | solution.py:304
  59.5 2.1 %collective-permute-start.4 = (f32[8,128]{1,0:T(8,128)S(1)}, f32[8,128]{1,0:T(8,128)S(1)}, u32[]{:S(2)}, u32[]{:S(2)}) collective-permute-start(f32[8,128]{1,0:T(8,128)S(1)} %get-tuple-element.45), channel_id=1, source_target_pairs={{1,0},{2,1},{3,2},{4,3},{5,4},{6,5},{7,6},{8,7},{9,8},{10,9},{11,1... | collective-permute-start | bytes 12296 | tf_op jit(solution)/shard_map/ppermute | solution.py:305
  61.6 4.0 %collective-permute-done.4.refs_11_ = f32[8,128]{1,0:T(8,128)S(1)} collective-permute-done((f32[8,128]{1,0:T(8,128)S(1)}, f32[8,128]{1,0:T(8,128)S(1)}, u32[]{:S(2)}, u32[]{:S(2)}) %collective-permute-start.4) | collective-permute-done | bytes 4128 | tf_op jit(solution)/shard_map/ppermute | solution.py:305
  65.6 2.8 %all-to-all-done.2.refs_9_ = f32[32,16,128]{2,1,0:T(8,128)S(1)} async-done(((f32[32,16,128]{2,1,0:T(8,128)}), f32[32,16,128]{2,1,0:T(8,128)S(1)}, u32[]{:S(2)}, u32[]{:S(2)}) %all-to-all-start.2) | async-done | bytes 262176 | tf_op jit(solution)/shard_map/all_to_all | solution.py:288
  69.8 6.7 %all-to-all-start.3 = ((f32[32,16,128]{2,1,0:T(8,128)}), f32[32,16,128]{2,1,0:T(8,128)S(1)}, u32[]{:S(2)}, u32[]{:S(2)}) async-start(f32[32,16,128]{2,1,0:T(8,128)} %get-tuple-element.48), calls=%async_computation.3 | async-start | bytes 524288 | tf_op jit(solution)/shard_map/all_to_all | solution.py:288
  76.6 2.2 %collective-permute-start.5 = (f32[8,128]{1,0:T(8,128)S(1)}, f32[8,128]{1,0:T(8,128)S(1)}, u32[]{:S(2)}, u32[]{:S(2)}) collective-permute-start(f32[8,128]{1,0:T(8,128)S(1)} %get-tuple-element.49), channel_id=1, source_target_pairs={{0,1},{1,2},{2,3},{3,4},{4,5},{5,6},{6,7},{7,8},{8,9},{9,10},{10,1... | collective-permute-start | bytes 12296 | tf_op jit(solution)/shard_map/ppermute | solution.py:304
  78.8 2.1 %collective-permute-start.6 = (f32[8,128]{1,0:T(8,128)S(1)}, f32[8,128]{1,0:T(8,128)S(1)}, u32[]{:S(2)}, u32[]{:S(2)}) collective-permute-start(f32[8,128]{1,0:T(8,128)S(1)} %get-tuple-element.50), channel_id=1, source_target_pairs={{1,0},{2,1},{3,2},{4,3},{5,4},{6,5},{7,6},{8,7},{9,8},{10,9},{11,1... | collective-permute-start | bytes 12296 | tf_op jit(solution)/shard_map/ppermute | solution.py:305
  80.9 4.1 %collective-permute-done.6.refs_11_ = f32[8,128]{1,0:T(8,128)S(1)} collective-permute-done((f32[8,128]{1,0:T(8,128)S(1)}, f32[8,128]{1,0:T(8,128)S(1)}, u32[]{:S(2)}, u32[]{:S(2)}) %collective-permute-start.6) | collective-permute-done | bytes 4128 | tf_op jit(solution)/shard_map/ppermute | solution.py:305
  85.0 2.8 %all-to-all-done.3.refs_9_ = f32[32,16,128]{2,1,0:T(8,128)S(1)} async-done(((f32[32,16,128]{2,1,0:T(8,128)}), f32[32,16,128]{2,1,0:T(8,128)S(1)}, u32[]{:S(2)}, u32[]{:S(2)}) %all-to-all-start.3) | async-done | bytes 262176 | tf_op jit(solution)/shard_map/all_to_all | solution.py:288
  89.2 6.7 %all-to-all-start.4 = ((f32[32,16,128]{2,1,0:T(8,128)}), f32[32,16,128]{2,1,0:T(8,128)S(1)}, u32[]{:S(2)}, u32[]{:S(2)}) async-start(f32[32,16,128]{2,1,0:T(8,128)} %get-tuple-element.53), calls=%async_computation.4 | async-start | bytes 524288 | tf_op jit(solution)/shard_map/all_to_all | solution.py:288
  95.9 2.2 %collective-permute-start.7 = (f32[8,128]{1,0:T(8,128)S(1)}, f32[8,128]{1,0:T(8,128)S(1)}, u32[]{:S(2)}, u32[]{:S(2)}) collective-permute-start(f32[8,128]{1,0:T(8,128)S(1)} %get-tuple-element.54), channel_id=1, source_target_pairs={{0,1},{1,2},{2,3},{3,4},{4,5},{5,6},{6,7},{7,8},{8,9},{9,10},{10,1... | collective-permute-start | bytes 12296 | tf_op jit(solution)/shard_map/ppermute | solution.py:304
  100.2 4.1 %collective-permute-done.8.refs_11_ = f32[8,128]{1,0:T(8,128)S(1)} collective-permute-done((f32[8,128]{1,0:T(8,128)S(1)}, f32[8,128]{1,0:T(8,128)S(1)}, u32[]{:S(2)}, u32[]{:S(2)}) %collective-permute-start.8) | collective-permute-done | bytes 4128 | tf_op jit(solution)/shard_map/ppermute | solution.py:305
  104.3 2.8 %all-to-all-done.4.refs_9_ = f32[32,16,128]{2,1,0:T(8,128)S(1)} async-done(((f32[32,16,128]{2,1,0:T(8,128)}), f32[32,16,128]{2,1,0:T(8,128)S(1)}, u32[]{:S(2)}, u32[]{:S(2)}) %all-to-all-start.4) | async-done | bytes 262176 | tf_op jit(solution)/shard_map/all_to_all | solution.py:288
  108.5 6.7 %all-to-all-start.5 = ((f32[32,16,128]{2,1,0:T(8,128)}), f32[32,16,128]{2,1,0:T(8,128)S(1)}, u32[]{:S(2)}, u32[]{:S(2)}) async-start(f32[32,16,128]{2,1,0:T(8,128)} %get-tuple-element.58), calls=%async_computation.5 | async-start | bytes 524288 | tf_op jit(solution)/shard_map/all_to_all | solution.py:288
  115.2 2.2 %collective-permute-start.9 = (f32[8,128]{1,0:T(8,128)S(1)}, f32[8,128]{1,0:T(8,128)S(1)}, u32[]{:S(2)}, u32[]{:S(2)}) collective-permute-start(f32[8,128]{1,0:T(8,128)S(1)} %get-tuple-element.59), channel_id=1, source_target_pairs={{0,1},{1,2},{2,3},{3,4},{4,5},{5,6},{6,7},{7,8},{8,9},{9,10},{10,1... | collective-permute-start | bytes 12296 | tf_op jit(solution)/shard_map/ppermute | solution.py:304
  119.6 4.1 %collective-permute-done.10.refs_11_ = f32[8,128]{1,0:T(8,128)S(1)} collective-permute-done((f32[8,128]{1,0:T(8,128)S(1)}, f32[8,128]{1,0:T(8,128)S(1)}, u32[]{:S(2)}, u32[]{:S(2)}) %collective-permute-start.10) | collective-permute-done | bytes 4128 | tf_op jit(solution)/shard_map/ppermute | solution.py:305
  123.6 2.8 %all-to-all-done.5.refs_9_ = f32[32,16,128]{2,1,0:T(8,128)S(1)} async-done(((f32[32,16,128]{2,1,0:T(8,128)}), f32[32,16,128]{2,1,0:T(8,128)S(1)}, u32[]{:S(2)}, u32[]{:S(2)}) %all-to-all-start.5) | async-done | bytes 262176 | tf_op jit(solution)/shard_map/all_to_all | solution.py:288
  (37 shorter events, 17.9 us)
Async XLA Ops:
  0.7 0.7 copy-start.6
  1.4 0.8 copy-start
  2.1 0.8 copy-start.1
  3.6 24.2 %copy-start.2 = (f32[8,8,128]{2,1,0:T(8,128)S(1)}, f32[8,8,128]{2,1,0:T(8,128)}, u32[]{:S(2)}) copy-start(f32[8,8,128]{2,1,0:T(8,128)} %refs_2_.13) | copy-start | bytes 98308
  3.6 24.2 %copy-start.3 = (f32[8,8,128]{2,1,0:T(8,128)S(1)}, f32[8,8,128]{2,1,0:T(8,128)}, u32[]{:S(2)}) copy-start(f32[8,8,128]{2,1,0:T(8,128)} %refs_5_.13) | copy-start | bytes 98308
  3.6 24.2 %copy-start.4 = (s32[4,1,2,128]{3,2,1,0:T(2,128)S(1)}, s32[4,1,2,128]{3,2,1,0:T(2,128)}, u32[]{:S(2)}) copy-start(s32[4,1,2,128]{3,2,1,0:T(2,128)} %refs_14_.9) | copy-start | bytes 12292
  3.6 24.2 %copy-start.5 = (f32[8,8,128]{2,1,0:T(8,128)S(1)}, f32[8,8,128]{2,1,0:T(8,128)}, u32[]{:S(2)}) copy-start(f32[8,8,128]{2,1,0:T(8,128)} %refs_2_.8) | copy-start | bytes 98308
  3.6 24.2 %all-to-all-start = ((f32[32,16,128]{2,1,0:T(8,128)}), f32[32,16,128]{2,1,0:T(8,128)S(1)}, u32[]{:S(2)}, u32[]{:S(2)}) async-start(f32[32,16,128]{2,1,0:T(8,128)} %get-tuple-element.32), calls=%async_computation | async-start | bytes 524288 | tf_op jit(solution)/shard_map/all_to_all | solution.py:288
  16.7 6.0 %collective-permute-start = (f32[8,128]{1,0:T(8,128)S(1)}, f32[8,128]{1,0:T(8,128)S(1)}, u32[]{:S(2)}, u32[]{:S(2)}) collective-permute-start(f32[8,128]{1,0:T(8,128)S(1)} %get-tuple-element.33), channel_id=1, source_target_pairs={{0,1},{1,2},{2,3},{3,4},{4,5},{5,6},{6,7},{7,8},{8,9},{9,10},{10,1... | collective-permute-start | bytes 12296 | tf_op jit(solution)/shard_map/ppermute | solution.py:294
  29.3 17.3 %all-to-all-start.1 = ((f32[32,16,128]{2,1,0:T(8,128)}), f32[32,16,128]{2,1,0:T(8,128)S(1)}, u32[]{:S(2)}, u32[]{:S(2)}) async-start(f32[32,16,128]{2,1,0:T(8,128)} %get-tuple-element.37), calls=%async_computation.1 | async-start | bytes 524288 | tf_op jit(solution)/shard_map/all_to_all | solution.py:288
  34.1 8.0 %collective-permute-start.1 = (f32[8,128]{1,0:T(8,128)S(1)}, f32[8,128]{1,0:T(8,128)S(1)}, u32[]{:S(2)}, u32[]{:S(2)}) collective-permute-start(f32[8,128]{1,0:T(8,128)S(1)} %get-tuple-element.38), channel_id=1, source_target_pairs={{0,1},{1,2},{2,3},{3,4},{4,5},{5,6},{6,7},{7,8},{8,9},{9,10},{10,1... | collective-permute-start | bytes 12296 | tf_op jit(solution)/shard_map/ppermute | solution.py:304
  40.2 6.4 %collective-permute-start.2 = (f32[8,128]{1,0:T(8,128)S(1)}, f32[8,128]{1,0:T(8,128)S(1)}, u32[]{:S(2)}, u32[]{:S(2)}) collective-permute-start(f32[8,128]{1,0:T(8,128)S(1)} %get-tuple-element.39), channel_id=1, source_target_pairs={{1,0},{2,1},{3,2},{4,3},{5,4},{6,5},{7,6},{8,7},{9,8},{10,9},{11,1... | collective-permute-start | bytes 12296 | tf_op jit(solution)/shard_map/ppermute | solution.py:305
  48.1 20.4 %all-to-all-start.2 = ((f32[32,16,128]{2,1,0:T(8,128)}), f32[32,16,128]{2,1,0:T(8,128)S(1)}, u32[]{:S(2)}, u32[]{:S(2)}) async-start(f32[32,16,128]{2,1,0:T(8,128)} %get-tuple-element.43), calls=%async_computation.2 | async-start | bytes 524288 | tf_op jit(solution)/shard_map/all_to_all | solution.py:288
  57.3 4.3 %collective-permute-start.3 = (f32[8,128]{1,0:T(8,128)S(1)}, f32[8,128]{1,0:T(8,128)S(1)}, u32[]{:S(2)}, u32[]{:S(2)}) collective-permute-start(f32[8,128]{1,0:T(8,128)S(1)} %get-tuple-element.44), channel_id=1, source_target_pairs={{0,1},{1,2},{2,3},{3,4},{4,5},{5,6},{6,7},{7,8},{8,9},{9,10},{10,1... | collective-permute-start | bytes 12296 | tf_op jit(solution)/shard_map/ppermute | solution.py:304
  59.5 6.1 %collective-permute-start.4 = (f32[8,128]{1,0:T(8,128)S(1)}, f32[8,128]{1,0:T(8,128)S(1)}, u32[]{:S(2)}, u32[]{:S(2)}) collective-permute-start(f32[8,128]{1,0:T(8,128)S(1)} %get-tuple-element.45), channel_id=1, source_target_pairs={{1,0},{2,1},{3,2},{4,3},{5,4},{6,5},{7,6},{8,7},{9,8},{10,9},{11,1... | collective-permute-start | bytes 12296 | tf_op jit(solution)/shard_map/ppermute | solution.py:305
  69.8 18.0 %all-to-all-start.3 = ((f32[32,16,128]{2,1,0:T(8,128)}), f32[32,16,128]{2,1,0:T(8,128)S(1)}, u32[]{:S(2)}, u32[]{:S(2)}) async-start(f32[32,16,128]{2,1,0:T(8,128)} %get-tuple-element.48), calls=%async_computation.3 | async-start | bytes 524288 | tf_op jit(solution)/shard_map/all_to_all | solution.py:288
  76.6 4.3 %collective-permute-start.5 = (f32[8,128]{1,0:T(8,128)S(1)}, f32[8,128]{1,0:T(8,128)S(1)}, u32[]{:S(2)}, u32[]{:S(2)}) collective-permute-start(f32[8,128]{1,0:T(8,128)S(1)} %get-tuple-element.49), channel_id=1, source_target_pairs={{0,1},{1,2},{2,3},{3,4},{4,5},{5,6},{6,7},{7,8},{8,9},{9,10},{10,1... | collective-permute-start | bytes 12296 | tf_op jit(solution)/shard_map/ppermute | solution.py:304
  78.8 6.2 %collective-permute-start.6 = (f32[8,128]{1,0:T(8,128)S(1)}, f32[8,128]{1,0:T(8,128)S(1)}, u32[]{:S(2)}, u32[]{:S(2)}) collective-permute-start(f32[8,128]{1,0:T(8,128)S(1)} %get-tuple-element.50), channel_id=1, source_target_pairs={{1,0},{2,1},{3,2},{4,3},{5,4},{6,5},{7,6},{8,7},{9,8},{10,9},{11,1... | collective-permute-start | bytes 12296 | tf_op jit(solution)/shard_map/ppermute | solution.py:305
  89.2 17.9 %all-to-all-start.4 = ((f32[32,16,128]{2,1,0:T(8,128)}), f32[32,16,128]{2,1,0:T(8,128)S(1)}, u32[]{:S(2)}, u32[]{:S(2)}) async-start(f32[32,16,128]{2,1,0:T(8,128)} %get-tuple-element.53), calls=%async_computation.4 | async-start | bytes 524288 | tf_op jit(solution)/shard_map/all_to_all | solution.py:288
  95.9 4.3 %collective-permute-start.7 = (f32[8,128]{1,0:T(8,128)S(1)}, f32[8,128]{1,0:T(8,128)S(1)}, u32[]{:S(2)}, u32[]{:S(2)}) collective-permute-start(f32[8,128]{1,0:T(8,128)S(1)} %get-tuple-element.54), channel_id=1, source_target_pairs={{0,1},{1,2},{2,3},{3,4},{4,5},{5,6},{6,7},{7,8},{8,9},{9,10},{10,1... | collective-permute-start | bytes 12296 | tf_op jit(solution)/shard_map/ppermute | solution.py:304
  98.1 6.2 %collective-permute-start.8 = (f32[8,128]{1,0:T(8,128)S(1)}, f32[8,128]{1,0:T(8,128)S(1)}, u32[]{:S(2)}, u32[]{:S(2)}) collective-permute-start(f32[8,128]{1,0:T(8,128)S(1)} %get-tuple-element.55), channel_id=1, source_target_pairs={{1,0},{2,1},{3,2},{4,3},{5,4},{6,5},{7,6},{8,7},{9,8},{10,9},{11,1... | collective-permute-start | bytes 12296 | tf_op jit(solution)/shard_map/ppermute | solution.py:305
  108.5 17.9 %all-to-all-start.5 = ((f32[32,16,128]{2,1,0:T(8,128)}), f32[32,16,128]{2,1,0:T(8,128)S(1)}, u32[]{:S(2)}, u32[]{:S(2)}) async-start(f32[32,16,128]{2,1,0:T(8,128)} %get-tuple-element.58), calls=%async_computation.5 | async-start | bytes 524288 | tf_op jit(solution)/shard_map/all_to_all | solution.py:288
  115.2 4.3 %collective-permute-start.9 = (f32[8,128]{1,0:T(8,128)S(1)}, f32[8,128]{1,0:T(8,128)S(1)}, u32[]{:S(2)}, u32[]{:S(2)}) collective-permute-start(f32[8,128]{1,0:T(8,128)S(1)} %get-tuple-element.59), channel_id=1, source_target_pairs={{0,1},{1,2},{2,3},{3,4},{4,5},{5,6},{6,7},{7,8},{8,9},{9,10},{10,1... | collective-permute-start | bytes 12296 | tf_op jit(solution)/shard_map/ppermute | solution.py:304
  117.4 6.2 %collective-permute-start.10 = (f32[8,128]{1,0:T(8,128)S(1)}, f32[8,128]{1,0:T(8,128)S(1)}, u32[]{:S(2)}, u32[]{:S(2)}) collective-permute-start(f32[8,128]{1,0:T(8,128)S(1)} %get-tuple-element.60), channel_id=1, source_target_pairs={{1,0},{2,1},{3,2},{4,3},{5,4},{6,5},{7,6},{8,7},{9,8},{10,9},{11,1... | collective-permute-start | bytes 12296 | tf_op jit(solution)/shard_map/ppermute | solution.py:305
  (3 other events, 2.1 us)

commit v2 on v1

--- a/solution.py
+++ b/solution.py
@@ -101,7 +101,7 @@
     return jnp.where(iota(plane.shape, 1) == at, F32(0.0), moved)
 
 
-def send_out(pos, ring, vals, p, send_ref, ylo_ref, yhi_ref, reach):
+def send_out(pos, odd, ring, vals, p, send_ref, face_ref, mate_ref, reach):
     width = p.shape[0]
     rows = vals.shape[0]
     send_ref[...] = jnp.zeros(send_ref.shape, F32)
@@ -110,8 +110,9 @@
     send_ref[lax.rem(pos + 1, ring), rows:, :] = p[width - 1]
     send_ref[lax.rem(pos + ring - 1, ring), rows:, :] = p[0]
     for x in range(width):
-        ylo_ref[x : x + 1, :] = p[x][:1, :]
-        yhi_ref[x : x + 1, :] = p[x][-1:, :]
+        low, high = p[x][:1, :], p[x][-1:, :]
+        face_ref[x : x + 1, :] = jnp.where(odd, high, low)
+        mate_ref[x : x + 1, :] = jnp.where(odd, low, high)
 
 
 def pack_kernel(pos_ref, tx_ref, ty_ref, host_ref, index_ref, cond_ref, rate_ref, send_ref, yhi_ref, *, reach):
@@ -132,9 +133,10 @@
 
 def first_kernel(
     pos_ref, rhs_ref, acc_ref, tx_ref, ty_ref, tz_ref, recv_ref, wy_ref, held_ref,
-    p_ref, gain_ref, wx_ref, seg_ref, well_ref, send_ref, ylo_ref, yhi_ref, *, reach, wells,
+    p_ref, gain_ref, wx_ref, seg_ref, well_ref, send_ref, face_ref, mate_ref, *, reach, wells,
 ):
     pos = pos_ref[0]
+    odd = pos_ref[1] == 1
     ring = recv_ref.shape[0]
     width, depth, lanes = rhs_ref.shape
     rows = reach * wells
@@ -175,7 +177,7 @@
         p_ref[x] = planes[x]
     cells = jnp.concatenate(planes, axis=0)
     vals = gather(cells, idx, hot, lanes)
-    send_out(pos, ring, vals, planes_array(planes), send_ref, ylo_ref, yhi_ref, reach)
+    send_out(pos, odd, ring, vals, planes_array(planes), send_ref, face_ref, mate_ref, reach)
 
 
 class planes_array:
@@ -188,10 +190,11 @@
 
 
 def sweep_kernel(
-    pos_ref, p_in, rhs_ref, tx_ref, ty_ref, tz_ref, gain_ref, wx_ref, wy_ref, recv_ref, south_ref, north_ref,
+    pos_ref, p_in, rhs_ref, tx_ref, ty_ref, tz_ref, gain_ref, wx_ref, wy_ref, recv_ref, face_in, mate_in,
     seg_in, well_ref, held_ref, p_ref, seg_ref, *rest, reach, wells, last,
 ):
     pos = pos_ref[0]
+    odd = pos_ref[1] == 1
     ring = recv_ref.shape[0]
     width, depth, lanes = rhs_ref.shape
     rows = reach * wells
@@ -218,8 +221,9 @@
     east = jnp.where(pos == ring - 1, F32(0.0), recv_ref[lax.rem(pos + 1, ring), rows:, :])
     block = p_in[...]
     wy = y_shifted(ty_ref[...], wy_ref[...], -1)
-    south = y_shifted(block, south_ref[...], -1)
-    north = y_shifted(block, north_ref[...], 1)
+    face, mate = face_in[...], mate_in[...]
+    south = y_shifted(block, jnp.where(odd, mate, face), -1)
+    north = y_shifted(block, jnp.where(odd, face, mate), 1)
     planes = []
     for x in range(width):
         tz = tz_ref[x]
@@ -232,9 +236,9 @@
     for x in range(width):
         p_ref[x] = planes[x]
     if not last:
-        send_ref, ylo_ref, yhi_ref = rest
+        send_ref, face_ref, mate_ref = rest
         vals = gather(jnp.concatenate(planes, axis=0), idx, hot, lanes)
-        send_out(pos, ring, vals, planes_array(planes), send_ref, ylo_ref, yhi_ref, reach)
+        send_out(pos, odd, ring, vals, planes_array(planes), send_ref, face_ref, mate_ref, reach)
 
 
 def shards(
@@ -257,8 +261,10 @@
     ring = lax.axis_size("gx")
     county = lax.axis_size("gy")
     up = [(j, j + 1) for j in range(county - 1)]
-    down = [(target, source) for source, target in up]
-    pos = lax.axis_index("gx").astype(jnp.int32).reshape(1)
+    facing = [(j, j + 1) for j in range(1, county - 1, 2)]
+    facing += [(target, source) for source, target in facing]
+    mates = [(j, j ^ 1) for j in range(county)]
+    pos = jnp.stack([lax.axis_index("gx"), lax.axis_index("gy") & 1]).astype(jnp.int32)
 
     def shape(*dims):
         return pltpu.VMEM(dims, F32)
@@ -293,7 +299,7 @@
     )
     wy = lax.ppermute(yhi, "gy", up)
     recv = exchanged(send)
-    p, gain, wx, seg, well, send, ylo, yhi = call(
+    p, gain, wx, seg, well, send, face, mate = call(
         first_kernel,
         [block, block, shape(depth, layers), shape(rows, slots), shape(4, rows, slots), message, edge, edge],
         pos, rhs_field, accumulation, trans_x, trans_y, trans_z, recv, wy, held_cells,
@@ -301,19 +307,19 @@
     )
     for sweep in range(1, SWEEPS):
         last = sweep == SWEEPS - 1
-        south = lax.ppermute(yhi, "gy", up)
-        north = lax.ppermute(ylo, "gy", down)
+        face_in = lax.ppermute(face, "gy", facing)
+        mate_in = lax.ppermute(mate, "gy", mates)
         recv = exchanged(send)
         outs = [result(width, depth, layers), result(1, wells, slots)] if last else [block, shape(rows, slots)]
         if not last:
             outs += [message, edge, edge]
         got = call(
-            sweep_kernel, outs, pos, p, rhs_field, trans_x, trans_y, trans_z, gain, wx, wy, recv, south, north,
+            sweep_kernel, outs, pos, p, rhs_field, trans_x, trans_y, trans_z, gain, wx, wy, recv, face_in, mate_in,
             seg, well, held_cells, reach=reach, wells=wells, last=last,
         )
         p, seg = got[:2]
         if not last:
-            send, ylo, yhi = got[2:]
+            send, face, mate = got[2:]
     return (p, seg)
 
 

time: 128 us -> 128 us (level)
  the two profiles are of different devices: /device:TPU:25 before, /device:TPU:16 now
where the time goes in v2:
time: 128 us; the launch traced here: 127 us
  starting transfers between devices  63.5 us (50%)
  waiting for transfers between devices  46.9 us (37%)
  Pallas kernels  13.5 us (11%)
  local copies, waits for them, and re-layouts  1.57 us (1%)
    all_to_all x6, waiting for transfers between devices, exchanged(): return lax.all_to_all(send, 'gx', 0, 0, tiled=True)  39.9 us
    all_to_all x6, starting transfers between devices, exchanged(): return lax.all_to_all(send, 'gx', 0, 0, tiled=True)  32.9 us
    ppermute x5, starting transfers between devices, shards(): mate_in = lax.ppermute(mate, 'gy', mates)  19.1 us
    pallas_call x7, Pallas kernels, call(): pl.pallas_call(lambda *refs: body(*refs, **static), out_shape=outs, in_sp...  13.5 us
    ppermute x5, starting transfers between devices, shards(): face_in = lax.ppermute(face, 'gy', facing)  9.6 us
    ppermute x5, waiting for transfers between devices, shards(): mate_in = lax.ppermute(mate, 'gy', mates)  3.44 us
    ppermute x1, waiting for transfers between devices, shards(): wy = lax.ppermute(yhi, 'gy', up)  3 us
  transfers between devices with their start and end apart: 17, of which 13 were waited for; matrix products, arithmetic and copies ran while one was open for 0% of the time, Pallas kernels for 0%

profile of v2, /device:TPU:16, one launch (start us, length us, event | category | flops | bytes accessed | tf_op | source)
XLA Modules:
  0.0 127.0 jit_solution(7879730978684731466)
XLA Ops:
  4.3 13.3 %all-to-all-start = ((f32[32,16,128]{2,1,0:T(8,128)}), f32[32,16,128]{2,1,0:T(8,128)S(1)}, u32[]{:S(2)}, u32[]{:S(2)}) async-start(f32[32,16,128]{2,1,0:T(8,128)} %get-tuple-element.32), calls=%async_computation | async-start | bytes 524288 | tf_op jit(solution)/shard_map/all_to_all | solution.py:294
  17.6 1.9 %collective-permute-start = (f32[8,128]{1,0:T(8,128)S(1)}, f32[8,128]{1,0:T(8,128)S(1)}, u32[]{:S(2)}, u32[]{:S(2)}) collective-permute-start(f32[8,128]{1,0:T(8,128)S(1)} %get-tuple-element.33), channel_id=1, source_target_pairs={{0,1},{1,2},{2,3},{3,4},{4,5},{5,6},{6,7},{7,8},{8,9},{9,10},{10,1... | collective-permute-start | bytes 12296 | tf_op jit(solution)/shard_map/ppermute | solution.py:300
  19.5 3.0 %collective-permute-done.refs_7_.refs_8_ = f32[8,128]{1,0:T(8,128)S(1)} collective-permute-done((f32[8,128]{1,0:T(8,128)S(1)}, f32[8,128]{1,0:T(8,128)S(1)}, u32[]{:S(2)}, u32[]{:S(2)}) %collective-permute-start) | collective-permute-done | bytes 4128 | tf_op jit(solution)/shard_map/ppermute | solution.py:300
  22.5 7.8 %all-to-all-done.refs_6_ = f32[32,16,128]{2,1,0:T(8,128)S(1)} async-done(((f32[32,16,128]{2,1,0:T(8,128)}), f32[32,16,128]{2,1,0:T(8,128)S(1)}, u32[]{:S(2)}, u32[]{:S(2)}) %all-to-all-start) | async-done | bytes 262176 | tf_op jit(solution)/shard_map/all_to_all | solution.py:294
  30.3 2.1 %shard_map.114 = (f32[8,8,128]{2,1,0:T(8,128)S(1)}, f32[8,8,128]{2,1,0:T(8,128)S(1)}, f32[8,128]{1,0:T(8,128)S(1)}, f32[8,128]{1,0:T(8,128)S(1)}, f32[4,8,128]{2...) custom-call(s32[2]{0:T(128)} %pad_add_fusion.refs_0_, ...), custom_call_target="tpu_custom_call" | custom-call | tf_op jit(solution)/shard_map/pallas_call | solution.py:282
  32.4 4.1 %all-to-all-start.1 = ((f32[32,16,128]{2,1,0:T(8,128)}), f32[32,16,128]{2,1,0:T(8,128)S(1)}, u32[]{:S(2)}, u32[]{:S(2)}) async-start(f32[32,16,128]{2,1,0:T(8,128)} %get-tuple-element.37), calls=%async_computation.1 | async-start | bytes 524288 | tf_op jit(solution)/shard_map/all_to_all | solution.py:294
  38.4 3.6 %collective-permute-start.2 = (f32[8,128]{1,0:T(8,128)S(1)}, f32[8,128]{1,0:T(8,128)S(1)}, u32[]{:S(2)}, u32[]{:S(2)}) collective-permute-start(f32[8,128]{1,0:T(8,128)S(1)} %get-tuple-element.39), channel_id=1, source_target_pairs={{0,1},{1,0},{2,3},{3,2},{4,5},{5,4},{6,7},{7,6},{8,9},{9,8},{10,11... | collective-permute-start | bytes 12296 | tf_op jit(solution)/shard_map/ppermute | solution.py:311
  42.8 6.1 %all-to-all-done.1.refs_9_ = f32[32,16,128]{2,1,0:T(8,128)S(1)} async-done(((f32[32,16,128]{2,1,0:T(8,128)}), f32[32,16,128]{2,1,0:T(8,128)S(1)}, u32[]{:S(2)}, u32[]{:S(2)}) %all-to-all-start.1) | async-done | bytes 262176 | tf_op jit(solution)/shard_map/all_to_all | solution.py:294
  48.9 2.1 %shard_map.115 = (f32[8,8,128]{2,1,0:T(8,128)S(1)}, f32[8,128]{1,0:T(8,128)S(1)}, f32[32,16,128]{2,1,0:T(8,128)}, f32[8,128]{1,0:T(8,128)S(1)}, f32[8,128]{1,0:T(8,128)S(1)}) custom-call(s32[2]{0:T(128)} %pad_add_fusion.refs_0_, f32[8,8,128]{2,1,0:T(8,128)S(1)} %get-tuple-element.34.refs_1_, f32[8,8,128]{2,1,0:T(8,128)S(1)} %copy-done.2, ...), custom_call_target="tpu_custom_call" | custom-call | tf_op jit(solution)/shard_map/pallas_call | solution.py:282
  51.0 3.9 %all-to-all-start.2 = ((f32[32,16,128]{2,1,0:T(8,128)}), f32[32,16,128]{2,1,0:T(8,128)S(1)}, u32[]{:S(2)}, u32[]{:S(2)}) async-start(f32[32,16,128]{2,1,0:T(8,128)} %get-tuple-element.43), calls=%async_computation.2 | async-start | bytes 524288 | tf_op jit(solution)/shard_map/all_to_all | solution.py:294
  56.8 4.7 %collective-permute-start.4 = (f32[8,128]{1,0:T(8,128)S(1)}, f32[8,128]{1,0:T(8,128)S(1)}, u32[]{:S(2)}, u32[]{:S(2)}) collective-permute-start(f32[8,128]{1,0:T(8,128)S(1)} %get-tuple-element.45), channel_id=1, source_target_pairs={{0,1},{1,0},{2,3},{3,2},{4,5},{5,4},{6,7},{7,6},{8,9},{9,8},{10,11... | collective-permute-start | bytes 12296 | tf_op jit(solution)/shard_map/ppermute | solution.py:311
  62.3 6.0 %all-to-all-done.2.refs_9_ = f32[32,16,128]{2,1,0:T(8,128)S(1)} async-done(((f32[32,16,128]{2,1,0:T(8,128)}), f32[32,16,128]{2,1,0:T(8,128)S(1)}, u32[]{:S(2)}, u32[]{:S(2)}) %all-to-all-start.2) | async-done | bytes 262176 | tf_op jit(solution)/shard_map/all_to_all | solution.py:294
  68.3 2.1 %shard_map.116 = (f32[8,8,128]{2,1,0:T(8,128)S(1)}, f32[8,128]{1,0:T(8,128)S(1)}, f32[32,16,128]{2,1,0:T(8,128)}, f32[8,128]{1,0:T(8,128)S(1)}, f32[8,128]{1,0:T(8,128)S(1)}) custom-call(s32[2]{0:T(128)} %pad_add_fusion.refs_0_, f32[8,8,128]{2,1,0:T(8,128)S(1)} %get-tuple-element.42.refs_1_, f32[8,8,128]{2,1,0:T(8,128)S(1)} %copy-done.2, ...), custom_call_target="tpu_custom_call" | custom-call | tf_op jit(solution)/shard_map/pallas_call | solution.py:282
  70.3 3.9 %all-to-all-start.3 = ((f32[32,16,128]{2,1,0:T(8,128)}), f32[32,16,128]{2,1,0:T(8,128)S(1)}, u32[]{:S(2)}, u32[]{:S(2)}) async-start(f32[32,16,128]{2,1,0:T(8,128)} %get-tuple-element.48), calls=%async_computation.3 | async-start | bytes 524288 | tf_op jit(solution)/shard_map/all_to_all | solution.py:294
  76.2 4.8 %collective-permute-start.6 = (f32[8,128]{1,0:T(8,128)S(1)}, f32[8,128]{1,0:T(8,128)S(1)}, u32[]{:S(2)}, u32[]{:S(2)}) collective-permute-start(f32[8,128]{1,0:T(8,128)S(1)} %get-tuple-element.50), channel_id=1, source_target_pairs={{0,1},{1,0},{2,3},{3,2},{4,5},{5,4},{6,7},{7,6},{8,9},{9,8},{10,11... | collective-permute-start | bytes 12296 | tf_op jit(solution)/shard_map/ppermute | solution.py:311
  81.8 5.9 %all-to-all-done.3.refs_9_ = f32[32,16,128]{2,1,0:T(8,128)S(1)} async-done(((f32[32,16,128]{2,1,0:T(8,128)}), f32[32,16,128]{2,1,0:T(8,128)S(1)}, u32[]{:S(2)}, u32[]{:S(2)}) %all-to-all-start.3) | async-done | bytes 262176 | tf_op jit(solution)/shard_map/all_to_all | solution.py:294
  87.7 2.1 %shard_map.117 = (f32[8,8,128]{2,1,0:T(8,128)S(1)}, f32[8,128]{1,0:T(8,128)S(1)}, f32[32,16,128]{2,1,0:T(8,128)}, f32[8,128]{1,0:T(8,128)S(1)}, f32[8,128]{1,0:T(8,128)S(1)}) custom-call(s32[2]{0:T(128)} %pad_add_fusion.refs_0_, f32[8,8,128]{2,1,0:T(8,128)S(1)} %get-tuple-element.47.refs_1_, f32[8,8,128]{2,1,0:T(8,128)S(1)} %copy-done.2, ...), custom_call_target="tpu_custom_call" | custom-call | tf_op jit(solution)/shard_map/pallas_call | solution.py:282
  89.8 3.9 %all-to-all-start.4 = ((f32[32,16,128]{2,1,0:T(8,128)}), f32[32,16,128]{2,1,0:T(8,128)S(1)}, u32[]{:S(2)}, u32[]{:S(2)}) async-start(f32[32,16,128]{2,1,0:T(8,128)} %get-tuple-element.53), calls=%async_computation.4 | async-start | bytes 524288 | tf_op jit(solution)/shard_map/all_to_all | solution.py:294
  95.6 3.6 %collective-permute-start.8 = (f32[8,128]{1,0:T(8,128)S(1)}, f32[8,128]{1,0:T(8,128)S(1)}, u32[]{:S(2)}, u32[]{:S(2)}) collective-permute-start(f32[8,128]{1,0:T(8,128)S(1)} %get-tuple-element.55), channel_id=1, source_target_pairs={{0,1},{1,0},{2,3},{3,2},{4,5},{5,4},{6,7},{7,6},{8,9},{9,8},{10,11... | collective-permute-start | bytes 12296 | tf_op jit(solution)/shard_map/ppermute | solution.py:311
  100.0 7.2 %all-to-all-done.4.refs_9_ = f32[32,16,128]{2,1,0:T(8,128)S(1)} async-done(((f32[32,16,128]{2,1,0:T(8,128)}), f32[32,16,128]{2,1,0:T(8,128)S(1)}, u32[]{:S(2)}, u32[]{:S(2)}) %all-to-all-start.4) | async-done | bytes 262176 | tf_op jit(solution)/shard_map/all_to_all | solution.py:294
  107.2 2.1 %shard_map.118 = (f32[8,8,128]{2,1,0:T(8,128)S(1)}, f32[8,128]{1,0:T(8,128)S(1)}, f32[32,16,128]{2,1,0:T(8,128)}, f32[8,128]{1,0:T(8,128)S(1)}, f32[8,128]{1,0:T(8,128)S(1)}) custom-call(s32[2]{0:T(128)} %pad_add_fusion.refs_0_, f32[8,8,128]{2,1,0:T(8,128)S(1)} %get-tuple-element.52.refs_1_, f32[8,8,128]{2,1,0:T(8,128)S(1)} %copy-done.2, ...), custom_call_target="tpu_custom_call" | custom-call | tf_op jit(solution)/shard_map/pallas_call | solution.py:282
  109.3 3.9 %all-to-all-start.5 = ((f32[32,16,128]{2,1,0:T(8,128)}), f32[32,16,128]{2,1,0:T(8,128)S(1)}, u32[]{:S(2)}, u32[]{:S(2)}) async-start(f32[32,16,128]{2,1,0:T(8,128)} %get-tuple-element.58), calls=%async_computation.5 | async-start | bytes 524288 | tf_op jit(solution)/shard_map/all_to_all | solution.py:294
  115.1 2.5 %collective-permute-start.10 = (f32[8,128]{1,0:T(8,128)S(1)}, f32[8,128]{1,0:T(8,128)S(1)}, u32[]{:S(2)}, u32[]{:S(2)}) collective-permute-start(f32[8,128]{1,0:T(8,128)S(1)} %get-tuple-element.60), channel_id=1, source_target_pairs={{0,1},{1,0},{2,3},{3,2},{4,5},{5,4},{6,7},{7,6},{8,9},{9,8},{10,11... | collective-permute-start | bytes 12296 | tf_op jit(solution)/shard_map/ppermute | solution.py:311
  118.4 7.0 %all-to-all-done.5.refs_9_ = f32[32,16,128]{2,1,0:T(8,128)S(1)} async-done(((f32[32,16,128]{2,1,0:T(8,128)}), f32[32,16,128]{2,1,0:T(8,128)S(1)}, u32[]{:S(2)}, u32[]{:S(2)}) %all-to-all-start.5) | async-done | bytes 262176 | tf_op jit(solution)/shard_map/all_to_all | solution.py:294
  (38 shorter events, 18.8 us)
Async XLA Ops:
  0.7 0.7 copy-start.6
  1.4 0.8 copy-start
  2.1 0.8 copy-start.1
  4.3 26.0 %copy-start.2 = (f32[8,8,128]{2,1,0:T(8,128)S(1)}, f32[8,8,128]{2,1,0:T(8,128)}, u32[]{:S(2)}) copy-start(f32[8,8,128]{2,1,0:T(8,128)} %refs_2_.13) | copy-start | bytes 98308
  4.3 26.0 %copy-start.3 = (f32[8,8,128]{2,1,0:T(8,128)S(1)}, f32[8,8,128]{2,1,0:T(8,128)}, u32[]{:S(2)}) copy-start(f32[8,8,128]{2,1,0:T(8,128)} %refs_5_.13) | copy-start | bytes 98308
  4.3 26.0 %copy-start.4 = (s32[4,1,2,128]{3,2,1,0:T(2,128)S(1)}, s32[4,1,2,128]{3,2,1,0:T(2,128)}, u32[]{:S(2)}) copy-start(s32[4,1,2,128]{3,2,1,0:T(2,128)} %refs_14_.9) | copy-start | bytes 12292
  4.3 26.0 %copy-start.5 = (f32[8,8,128]{2,1,0:T(8,128)S(1)}, f32[8,8,128]{2,1,0:T(8,128)}, u32[]{:S(2)}) copy-start(f32[8,8,128]{2,1,0:T(8,128)} %refs_2_.8) | copy-start | bytes 98308
  4.3 26.0 %all-to-all-start = ((f32[32,16,128]{2,1,0:T(8,128)}), f32[32,16,128]{2,1,0:T(8,128)S(1)}, u32[]{:S(2)}, u32[]{:S(2)}) async-start(f32[32,16,128]{2,1,0:T(8,128)} %get-tuple-element.32), calls=%async_computation | async-start | bytes 524288 | tf_op jit(solution)/shard_map/all_to_all | solution.py:294
  17.6 4.9 %collective-permute-start = (f32[8,128]{1,0:T(8,128)S(1)}, f32[8,128]{1,0:T(8,128)S(1)}, u32[]{:S(2)}, u32[]{:S(2)}) collective-permute-start(f32[8,128]{1,0:T(8,128)S(1)} %get-tuple-element.33), channel_id=1, source_target_pairs={{0,1},{1,2},{2,3},{3,4},{4,5},{5,6},{6,7},{7,8},{8,9},{9,10},{10,1... | collective-permute-start | bytes 12296 | tf_op jit(solution)/shard_map/ppermute | solution.py:300
  32.4 16.5 %all-to-all-start.1 = ((f32[32,16,128]{2,1,0:T(8,128)}), f32[32,16,128]{2,1,0:T(8,128)S(1)}, u32[]{:S(2)}, u32[]{:S(2)}) async-start(f32[32,16,128]{2,1,0:T(8,128)} %get-tuple-element.37), calls=%async_computation.1 | async-start | bytes 524288 | tf_op jit(solution)/shard_map/all_to_all | solution.py:294
  36.5 5.5 %collective-permute-start.1 = (f32[8,128]{1,0:T(8,128)S(1)}, f32[8,128]{1,0:T(8,128)S(1)}, u32[]{:S(2)}, u32[]{:S(2)}) collective-permute-start(f32[8,128]{1,0:T(8,128)S(1)} %get-tuple-element.38), channel_id=1, source_target_pairs={{1,2},{3,4},{5,6},{7,8},{9,10},{11,12},{13,14},{2,1},{4,3},{6,5},{... | collective-permute-start | bytes 12296 | tf_op jit(solution)/shard_map/ppermute | solution.py:310
  38.4 4.4 %collective-permute-start.2 = (f32[8,128]{1,0:T(8,128)S(1)}, f32[8,128]{1,0:T(8,128)S(1)}, u32[]{:S(2)}, u32[]{:S(2)}) collective-permute-start(f32[8,128]{1,0:T(8,128)S(1)} %get-tuple-element.39), channel_id=1, source_target_pairs={{0,1},{1,0},{2,3},{3,2},{4,5},{5,4},{6,7},{7,6},{8,9},{9,8},{10,11... | collective-permute-start | bytes 12296 | tf_op jit(solution)/shard_map/ppermute | solution.py:311
  51.0 17.3 %all-to-all-start.2 = ((f32[32,16,128]{2,1,0:T(8,128)}), f32[32,16,128]{2,1,0:T(8,128)S(1)}, u32[]{:S(2)}, u32[]{:S(2)}) async-start(f32[32,16,128]{2,1,0:T(8,128)} %get-tuple-element.43), calls=%async_computation.2 | async-start | bytes 524288 | tf_op jit(solution)/shard_map/all_to_all | solution.py:294
  54.9 6.6 %collective-permute-start.3 = (f32[8,128]{1,0:T(8,128)S(1)}, f32[8,128]{1,0:T(8,128)S(1)}, u32[]{:S(2)}, u32[]{:S(2)}) collective-permute-start(f32[8,128]{1,0:T(8,128)S(1)} %get-tuple-element.44), channel_id=1, source_target_pairs={{1,2},{3,4},{5,6},{7,8},{9,10},{11,12},{13,14},{2,1},{4,3},{6,5},{... | collective-permute-start | bytes 12296 | tf_op jit(solution)/shard_map/ppermute | solution.py:310
  56.8 5.5 %collective-permute-start.4 = (f32[8,128]{1,0:T(8,128)S(1)}, f32[8,128]{1,0:T(8,128)S(1)}, u32[]{:S(2)}, u32[]{:S(2)}) collective-permute-start(f32[8,128]{1,0:T(8,128)S(1)} %get-tuple-element.45), channel_id=1, source_target_pairs={{0,1},{1,0},{2,3},{3,2},{4,5},{5,4},{6,7},{7,6},{8,9},{9,8},{10,11... | collective-permute-start | bytes 12296 | tf_op jit(solution)/shard_map/ppermute | solution.py:311
  70.3 17.3 %all-to-all-start.3 = ((f32[32,16,128]{2,1,0:T(8,128)}), f32[32,16,128]{2,1,0:T(8,128)S(1)}, u32[]{:S(2)}, u32[]{:S(2)}) async-start(f32[32,16,128]{2,1,0:T(8,128)} %get-tuple-element.48), calls=%async_computation.3 | async-start | bytes 524288 | tf_op jit(solution)/shard_map/all_to_all | solution.py:294
  74.2 6.7 %collective-permute-start.5 = (f32[8,128]{1,0:T(8,128)S(1)}, f32[8,128]{1,0:T(8,128)S(1)}, u32[]{:S(2)}, u32[]{:S(2)}) collective-permute-start(f32[8,128]{1,0:T(8,128)S(1)} %get-tuple-element.49), channel_id=1, source_target_pairs={{1,2},{3,4},{5,6},{7,8},{9,10},{11,12},{13,14},{2,1},{4,3},{6,5},{... | collective-permute-start | bytes 12296 | tf_op jit(solution)/shard_map/ppermute | solution.py:310
  76.2 5.6 %collective-permute-start.6 = (f32[8,128]{1,0:T(8,128)S(1)}, f32[8,128]{1,0:T(8,128)S(1)}, u32[]{:S(2)}, u32[]{:S(2)}) collective-permute-start(f32[8,128]{1,0:T(8,128)S(1)} %get-tuple-element.50), channel_id=1, source_target_pairs={{0,1},{1,0},{2,3},{3,2},{4,5},{5,4},{6,7},{7,6},{8,9},{9,8},{10,11... | collective-permute-start | bytes 12296 | tf_op jit(solution)/shard_map/ppermute | solution.py:311
  89.8 17.4 %all-to-all-start.4 = ((f32[32,16,128]{2,1,0:T(8,128)}), f32[32,16,128]{2,1,0:T(8,128)S(1)}, u32[]{:S(2)}, u32[]{:S(2)}) async-start(f32[32,16,128]{2,1,0:T(8,128)} %get-tuple-element.53), calls=%async_computation.4 | async-start | bytes 524288 | tf_op jit(solution)/shard_map/all_to_all | solution.py:294
  93.6 5.6 %collective-permute-start.7 = (f32[8,128]{1,0:T(8,128)S(1)}, f32[8,128]{1,0:T(8,128)S(1)}, u32[]{:S(2)}, u32[]{:S(2)}) collective-permute-start(f32[8,128]{1,0:T(8,128)S(1)} %get-tuple-element.54), channel_id=1, source_target_pairs={{1,2},{3,4},{5,6},{7,8},{9,10},{11,12},{13,14},{2,1},{4,3},{6,5},{... | collective-permute-start | bytes 12296 | tf_op jit(solution)/shard_map/ppermute | solution.py:310
  95.6 4.4 %collective-permute-start.8 = (f32[8,128]{1,0:T(8,128)S(1)}, f32[8,128]{1,0:T(8,128)S(1)}, u32[]{:S(2)}, u32[]{:S(2)}) collective-permute-start(f32[8,128]{1,0:T(8,128)S(1)} %get-tuple-element.55), channel_id=1, source_target_pairs={{0,1},{1,0},{2,3},{3,2},{4,5},{5,4},{6,7},{7,6},{8,9},{9,8},{10,11... | collective-permute-start | bytes 12296 | tf_op jit(solution)/shard_map/ppermute | solution.py:311
  109.3 16.1 %all-to-all-start.5 = ((f32[32,16,128]{2,1,0:T(8,128)}), f32[32,16,128]{2,1,0:T(8,128)S(1)}, u32[]{:S(2)}, u32[]{:S(2)}) async-start(f32[32,16,128]{2,1,0:T(8,128)} %get-tuple-element.58), calls=%async_computation.5 | async-start | bytes 524288 | tf_op jit(solution)/shard_map/all_to_all | solution.py:294
  113.2 4.9 %collective-permute-start.9 = (f32[8,128]{1,0:T(8,128)S(1)}, f32[8,128]{1,0:T(8,128)S(1)}, u32[]{:S(2)}, u32[]{:S(2)}) collective-permute-start(f32[8,128]{1,0:T(8,128)S(1)} %get-tuple-element.59), channel_id=1, source_target_pairs={{1,2},{3,4},{5,6},{7,8},{9,10},{11,12},{13,14},{2,1},{4,3},{6,5},{... | collective-permute-start | bytes 12296 | tf_op jit(solution)/shard_map/ppermute | solution.py:310
  115.1 3.3 %collective-permute-start.10 = (f32[8,128]{1,0:T(8,128)S(1)}, f32[8,128]{1,0:T(8,128)S(1)}, u32[]{:S(2)}, u32[]{:S(2)}) collective-permute-start(f32[8,128]{1,0:T(8,128)S(1)} %get-tuple-element.60), channel_id=1, source_target_pairs={{0,1},{1,0},{2,3},{3,2},{4,5},{5,4},{6,7},{7,6},{8,9},{9,8},{10,11... | collective-permute-start | bytes 12296 | tf_op jit(solution)/shard_map/ppermute | solution.py:311
  (3 other events, 2.1 us)

commit v3 on v2

--- a/solution.py
+++ b/solution.py
@@ -115,8 +115,8 @@
         mate_ref[x : x + 1, :] = jnp.where(odd, low, high)
 
 
-def pack_kernel(pos_ref, tx_ref, ty_ref, host_ref, index_ref, cond_ref, rate_ref, send_ref, yhi_ref, *, reach):
-    pos = pos_ref[0]
+def pack_kernel(tx_ref, ty_ref, host_ref, index_ref, cond_ref, rate_ref, send_ref, yhi_ref, *, reach):
+    pos = lax.axis_index("gx")
     ring = send_ref.shape[0]
     width = tx_ref.shape[0]
     pack = jnp.concatenate(
@@ -132,11 +132,11 @@
 
 
 def first_kernel(
-    pos_ref, rhs_ref, acc_ref, tx_ref, ty_ref, tz_ref, recv_ref, wy_ref, held_ref,
+    rhs_ref, acc_ref, tx_ref, ty_ref, tz_ref, recv_ref, wy_ref, held_ref,
     p_ref, gain_ref, wx_ref, seg_ref, well_ref, send_ref, face_ref, mate_ref, *, reach, wells,
 ):
-    pos = pos_ref[0]
-    odd = pos_ref[1] == 1
+    pos = lax.axis_index("gx")
+    odd = (lax.axis_index("gy") & 1) == 1
     ring = recv_ref.shape[0]
     width, depth, lanes = rhs_ref.shape
     rows = reach * wells
@@ -190,11 +190,11 @@
 
 
 def sweep_kernel(
-    pos_ref, p_in, rhs_ref, tx_ref, ty_ref, tz_ref, gain_ref, wx_ref, wy_ref, recv_ref, face_in, mate_in,
+    p_in, rhs_ref, tx_ref, ty_ref, tz_ref, gain_ref, wx_ref, wy_ref, recv_ref, face_in, mate_in,
     seg_in, well_ref, held_ref, p_ref, seg_ref, *rest, reach, wells, last,
 ):
-    pos = pos_ref[0]
-    odd = pos_ref[1] == 1
+    pos = lax.axis_index("gx")
+    odd = (lax.axis_index("gy") & 1) == 1
     ring = recv_ref.shape[0]
     width, depth, lanes = rhs_ref.shape
     rows = reach * wells
@@ -264,7 +264,6 @@
     facing = [(j, j + 1) for j in range(1, county - 1, 2)]
     facing += [(target, source) for source, target in facing]
     mates = [(j, j ^ 1) for j in range(county)]
-    pos = jnp.stack([lax.axis_index("gx"), lax.axis_index("gy") & 1]).astype(jnp.int32)
 
     def shape(*dims):
         return pltpu.VMEM(dims, F32)
@@ -275,16 +274,15 @@
     def near(value):
         return pltpu.with_memory_space_constraint(value, pltpu.VMEM)
 
-    smem = pl.BlockSpec(memory_space=pltpu.SMEM)
     vmem = pl.BlockSpec(memory_space=pltpu.VMEM)
 
-    def call(body, outs, *args, **static):
+    def call(body, outs, *args, placed=near, **static):
         return pl.pallas_call(
             lambda *refs: body(*refs, **static),
             out_shape=outs,
-            in_specs=[smem] + [vmem] * (len(args) - 1),
+            in_specs=[vmem] * len(args),
             out_specs=[vmem] * len(outs),
-        )(args[0], *map(near, args[1:]))
+        )(*map(placed, args))
 
     message = shape(ring, rows + depth, slots)
     edge = shape(width, layers)
@@ -294,15 +292,15 @@
         return lax.all_to_all(send, "gx", 0, 0, tiled=True)
 
     send, yhi = call(
-        pack_kernel, [message, edge], pos, trans_x, trans_y, perf_host, well_index, seg_cond, seg_rate,
-        reach=reach,
+        pack_kernel, [message, edge], trans_x, trans_y, perf_host, well_index, seg_cond, seg_rate,
+        placed=lambda value: value, reach=reach,
     )
     wy = lax.ppermute(yhi, "gy", up)
     recv = exchanged(send)
     p, gain, wx, seg, well, send, face, mate = call(
         first_kernel,
         [block, block, shape(depth, layers), shape(rows, slots), shape(4, rows, slots), message, edge, edge],
-        pos, rhs_field, accumulation, trans_x, trans_y, trans_z, recv, wy, held_cells,
+        rhs_field, accumulation, trans_x, trans_y, trans_z, recv, wy, held_cells,
         reach=reach, wells=wells,
     )
     for sweep in range(1, SWEEPS):
@@ -314,7 +312,7 @@
         if not last:
             outs += [message, edge, edge]
         got = call(
-            sweep_kernel, outs, pos, p, rhs_field, trans_x, trans_y, trans_z, gain, wx, wy, recv, face_in, mate_in,
+            sweep_kernel, outs, p, rhs_field, trans_x, trans_y, trans_z, gain, wx, wy, recv, face_in, mate_in,
             seg, well, held_cells, reach=reach, wells=wells, last=last,
         )
         p, seg = got[:2]

time: 128 us -> 122 us (0.953)
  Pallas kernels: 13.5 us -> 9.61 us
  local copies, waits for them, and re-layouts: 1.57 us -> 0.03 us
    pallas_call x7, Pallas kernels: 13.5 us -> 9.61 us  [call(): pl.pallas_call(lambda *refs: body(*refs, **static), out_shape=outs, in_sp...]
    unnamed x20 -> x12, local copies, waits for them, and re-layouts: 1.57 us -> 0.03 us
where the time goes in v3:
time: 122 us; the launch traced here: 121 us
  starting transfers between devices  63.5 us (52%)
  waiting for transfers between devices  46.9 us (38%)
  Pallas kernels  9.61 us (8%)
    all_to_all x6, waiting for transfers between devices, exchanged(): return lax.all_to_all(send, 'gx', 0, 0, tiled=True)  39.9 us
    all_to_all x6, starting transfers between devices, exchanged(): return lax.all_to_all(send, 'gx', 0, 0, tiled=True)  32.9 us
    ppermute x5, starting transfers between devices, shards(): mate_in = lax.ppermute(mate, 'gy', mates)  19.1 us
    pallas_call x7, Pallas kernels, call(): pl.pallas_call(lambda *refs: body(*refs, **static), out_shape=outs, in_sp...  9.61 us
    ppermute x5, starting transfers between devices, shards(): face_in = lax.ppermute(face, 'gy', facing)  9.6 us
    ppermute x5, waiting for transfers between devices, shards(): mate_in = lax.ppermute(mate, 'gy', mates)  3.44 us
    ppermute x1, waiting for transfers between devices, shards(): wy = lax.ppermute(yhi, 'gy', up)  3 us
  transfers between devices with their start and end apart: 17, of which 13 were waited for; matrix products, arithmetic and copies ran while one was open for 0% of the time, Pallas kernels for 0%

profile of v3, /device:TPU:16, one launch (start us, length us, event | category | flops | bytes accessed | tf_op | source)
XLA Modules:
  0.0 120.9 jit_solution(9875309933676550102)
XLA Ops:
  2.2 13.3 %all-to-all-start = ((f32[32,16,128]{2,1,0:T(8,128)}), f32[32,16,128]{2,1,0:T(8,128)S(1)}, u32[]{:S(2)}, u32[]{:S(2)}) async-start(f32[32,16,128]{2,1,0:T(8,128)} %get-tuple-element.32), calls=%async_computation | async-start | bytes 524288 | tf_op jit(solution)/shard_map/all_to_all | solution.py:292
  15.5 1.9 %collective-permute-start = (f32[8,128]{1,0:T(8,128)S(1)}, f32[8,128]{1,0:T(8,128)S(1)}, u32[]{:S(2)}, u32[]{:S(2)}) collective-permute-start(f32[8,128]{1,0:T(8,128)S(1)} %get-tuple-element.33), channel_id=1, source_target_pairs={{0,1},{1,2},{2,3},{3,4},{4,5},{5,6},{6,7},{7,8},{8,9},{9,10},{10,1... | collective-permute-start | bytes 12296 | tf_op jit(solution)/shard_map/ppermute | solution.py:298
  17.4 3.0 %collective-permute-done.refs_6_.refs_7_ = f32[8,128]{1,0:T(8,128)S(1)} collective-permute-done((f32[8,128]{1,0:T(8,128)S(1)}, f32[8,128]{1,0:T(8,128)S(1)}, u32[]{:S(2)}, u32[]{:S(2)}) %collective-permute-start) | collective-permute-done | bytes 4128 | tf_op jit(solution)/shard_map/ppermute | solution.py:298
  20.4 7.8 %all-to-all-done.refs_5_ = f32[32,16,128]{2,1,0:T(8,128)S(1)} async-done(((f32[32,16,128]{2,1,0:T(8,128)}), f32[32,16,128]{2,1,0:T(8,128)S(1)}, u32[]{:S(2)}, u32[]{:S(2)}) %all-to-all-start) | async-done | bytes 262176 | tf_op jit(solution)/shard_map/all_to_all | solution.py:292
  29.7 4.1 %all-to-all-start.1 = ((f32[32,16,128]{2,1,0:T(8,128)}), f32[32,16,128]{2,1,0:T(8,128)S(1)}, u32[]{:S(2)}, u32[]{:S(2)}) async-start(f32[32,16,128]{2,1,0:T(8,128)} %get-tuple-element.37), calls=%async_computation.1 | async-start | bytes 524288 | tf_op jit(solution)/shard_map/all_to_all | solution.py:292
  33.8 1.9 %collective-permute-start.1 = (f32[8,128]{1,0:T(8,128)S(1)}, f32[8,128]{1,0:T(8,128)S(1)}, u32[]{:S(2)}, u32[]{:S(2)}) collective-permute-start(f32[8,128]{1,0:T(8,128)S(1)} %get-tuple-element.38), channel_id=1, source_target_pairs={{1,2},{3,4},{5,6},{7,8},{9,10},{11,12},{13,14},{2,1},{4,3},{6,5},{... | collective-permute-start | bytes 12296 | tf_op jit(solution)/shard_map/ppermute | solution.py:308
  35.7 3.6 %collective-permute-start.2 = (f32[8,128]{1,0:T(8,128)S(1)}, f32[8,128]{1,0:T(8,128)S(1)}, u32[]{:S(2)}, u32[]{:S(2)}) collective-permute-start(f32[8,128]{1,0:T(8,128)S(1)} %get-tuple-element.39), channel_id=1, source_target_pairs={{0,1},{1,0},{2,3},{3,2},{4,5},{5,4},{6,7},{7,6},{8,9},{9,8},{10,11... | collective-permute-start | bytes 12296 | tf_op jit(solution)/shard_map/ppermute | solution.py:309
  40.1 6.1 %all-to-all-done.1.refs_8_ = f32[32,16,128]{2,1,0:T(8,128)S(1)} async-done(((f32[32,16,128]{2,1,0:T(8,128)}), f32[32,16,128]{2,1,0:T(8,128)S(1)}, u32[]{:S(2)}, u32[]{:S(2)}) %all-to-all-start.1) | async-done | bytes 262176 | tf_op jit(solution)/shard_map/all_to_all | solution.py:292
  47.6 3.9 %all-to-all-start.2 = ((f32[32,16,128]{2,1,0:T(8,128)}), f32[32,16,128]{2,1,0:T(8,128)S(1)}, u32[]{:S(2)}, u32[]{:S(2)}) async-start(f32[32,16,128]{2,1,0:T(8,128)} %get-tuple-element.43), calls=%async_computation.2 | async-start | bytes 524288 | tf_op jit(solution)/shard_map/all_to_all | solution.py:292
  51.5 1.9 %collective-permute-start.3 = (f32[8,128]{1,0:T(8,128)S(1)}, f32[8,128]{1,0:T(8,128)S(1)}, u32[]{:S(2)}, u32[]{:S(2)}) collective-permute-start(f32[8,128]{1,0:T(8,128)S(1)} %get-tuple-element.44), channel_id=1, source_target_pairs={{1,2},{3,4},{5,6},{7,8},{9,10},{11,12},{13,14},{2,1},{4,3},{6,5},{... | collective-permute-start | bytes 12296 | tf_op jit(solution)/shard_map/ppermute | solution.py:308
  53.4 4.7 %collective-permute-start.4 = (f32[8,128]{1,0:T(8,128)S(1)}, f32[8,128]{1,0:T(8,128)S(1)}, u32[]{:S(2)}, u32[]{:S(2)}) collective-permute-start(f32[8,128]{1,0:T(8,128)S(1)} %get-tuple-element.45), channel_id=1, source_target_pairs={{0,1},{1,0},{2,3},{3,2},{4,5},{5,4},{6,7},{7,6},{8,9},{9,8},{10,11... | collective-permute-start | bytes 12296 | tf_op jit(solution)/shard_map/ppermute | solution.py:309
  58.9 6.0 %all-to-all-done.2.refs_8_ = f32[32,16,128]{2,1,0:T(8,128)S(1)} async-done(((f32[32,16,128]{2,1,0:T(8,128)}), f32[32,16,128]{2,1,0:T(8,128)S(1)}, u32[]{:S(2)}, u32[]{:S(2)}) %all-to-all-start.2) | async-done | bytes 262176 | tf_op jit(solution)/shard_map/all_to_all | solution.py:292
  66.3 3.9 %all-to-all-start.3 = ((f32[32,16,128]{2,1,0:T(8,128)}), f32[32,16,128]{2,1,0:T(8,128)S(1)}, u32[]{:S(2)}, u32[]{:S(2)}) async-start(f32[32,16,128]{2,1,0:T(8,128)} %get-tuple-element.48), calls=%async_computation.3 | async-start | bytes 524288 | tf_op jit(solution)/shard_map/all_to_all | solution.py:292
  70.2 1.9 %collective-permute-start.5 = (f32[8,128]{1,0:T(8,128)S(1)}, f32[8,128]{1,0:T(8,128)S(1)}, u32[]{:S(2)}, u32[]{:S(2)}) collective-permute-start(f32[8,128]{1,0:T(8,128)S(1)} %get-tuple-element.49), channel_id=1, source_target_pairs={{1,2},{3,4},{5,6},{7,8},{9,10},{11,12},{13,14},{2,1},{4,3},{6,5},{... | collective-permute-start | bytes 12296 | tf_op jit(solution)/shard_map/ppermute | solution.py:308
  72.1 4.8 %collective-permute-start.6 = (f32[8,128]{1,0:T(8,128)S(1)}, f32[8,128]{1,0:T(8,128)S(1)}, u32[]{:S(2)}, u32[]{:S(2)}) collective-permute-start(f32[8,128]{1,0:T(8,128)S(1)} %get-tuple-element.50), channel_id=1, source_target_pairs={{0,1},{1,0},{2,3},{3,2},{4,5},{5,4},{6,7},{7,6},{8,9},{9,8},{10,11... | collective-permute-start | bytes 12296 | tf_op jit(solution)/shard_map/ppermute | solution.py:309
  77.7 5.9 %all-to-all-done.3.refs_8_ = f32[32,16,128]{2,1,0:T(8,128)S(1)} async-done(((f32[32,16,128]{2,1,0:T(8,128)}), f32[32,16,128]{2,1,0:T(8,128)S(1)}, u32[]{:S(2)}, u32[]{:S(2)}) %all-to-all-start.3) | async-done | bytes 262176 | tf_op jit(solution)/shard_map/all_to_all | solution.py:292
  85.0 3.9 %all-to-all-start.4 = ((f32[32,16,128]{2,1,0:T(8,128)}), f32[32,16,128]{2,1,0:T(8,128)S(1)}, u32[]{:S(2)}, u32[]{:S(2)}) async-start(f32[32,16,128]{2,1,0:T(8,128)} %get-tuple-element.53), calls=%async_computation.4 | async-start | bytes 524288 | tf_op jit(solution)/shard_map/all_to_all | solution.py:292
  88.9 1.9 %collective-permute-start.7 = (f32[8,128]{1,0:T(8,128)S(1)}, f32[8,128]{1,0:T(8,128)S(1)}, u32[]{:S(2)}, u32[]{:S(2)}) collective-permute-start(f32[8,128]{1,0:T(8,128)S(1)} %get-tuple-element.54), channel_id=1, source_target_pairs={{1,2},{3,4},{5,6},{7,8},{9,10},{11,12},{13,14},{2,1},{4,3},{6,5},{... | collective-permute-start | bytes 12296 | tf_op jit(solution)/shard_map/ppermute | solution.py:308
  90.8 3.6 %collective-permute-start.8 = (f32[8,128]{1,0:T(8,128)S(1)}, f32[8,128]{1,0:T(8,128)S(1)}, u32[]{:S(2)}, u32[]{:S(2)}) collective-permute-start(f32[8,128]{1,0:T(8,128)S(1)} %get-tuple-element.55), channel_id=1, source_target_pairs={{0,1},{1,0},{2,3},{3,2},{4,5},{5,4},{6,7},{7,6},{8,9},{9,8},{10,11... | collective-permute-start | bytes 12296 | tf_op jit(solution)/shard_map/ppermute | solution.py:309
  95.3 7.2 %all-to-all-done.4.refs_8_ = f32[32,16,128]{2,1,0:T(8,128)S(1)} async-done(((f32[32,16,128]{2,1,0:T(8,128)}), f32[32,16,128]{2,1,0:T(8,128)S(1)}, u32[]{:S(2)}, u32[]{:S(2)}) %all-to-all-start.4) | async-done | bytes 262176 | tf_op jit(solution)/shard_map/all_to_all | solution.py:292
  103.9 3.9 %all-to-all-start.5 = ((f32[32,16,128]{2,1,0:T(8,128)}), f32[32,16,128]{2,1,0:T(8,128)S(1)}, u32[]{:S(2)}, u32[]{:S(2)}) async-start(f32[32,16,128]{2,1,0:T(8,128)} %get-tuple-element.58), calls=%async_computation.5 | async-start | bytes 524288 | tf_op jit(solution)/shard_map/all_to_all | solution.py:292
  107.7 1.9 %collective-permute-start.9 = (f32[8,128]{1,0:T(8,128)S(1)}, f32[8,128]{1,0:T(8,128)S(1)}, u32[]{:S(2)}, u32[]{:S(2)}) collective-permute-start(f32[8,128]{1,0:T(8,128)S(1)} %get-tuple-element.59), channel_id=1, source_target_pairs={{1,2},{3,4},{5,6},{7,8},{9,10},{11,12},{13,14},{2,1},{4,3},{6,5},{... | collective-permute-start | bytes 12296 | tf_op jit(solution)/shard_map/ppermute | solution.py:308
  109.7 2.5 %collective-permute-start.10 = (f32[8,128]{1,0:T(8,128)S(1)}, f32[8,128]{1,0:T(8,128)S(1)}, u32[]{:S(2)}, u32[]{:S(2)}) collective-permute-start(f32[8,128]{1,0:T(8,128)S(1)} %get-tuple-element.60), channel_id=1, source_target_pairs={{0,1},{1,0},{2,3},{3,2},{4,5},{5,4},{6,7},{7,6},{8,9},{9,8},{10,11... | collective-permute-start | bytes 12296 | tf_op jit(solution)/shard_map/ppermute | solution.py:309
  112.9 7.0 %all-to-all-done.5.refs_8_ = f32[32,16,128]{2,1,0:T(8,128)S(1)} async-done(((f32[32,16,128]{2,1,0:T(8,128)}), f32[32,16,128]{2,1,0:T(8,128)S(1)}, u32[]{:S(2)}, u32[]{:S(2)}) %all-to-all-start.5) | async-done | bytes 262176 | tf_op jit(solution)/shard_map/all_to_all | solution.py:292
  (29 shorter events, 13.6 us)
Async XLA Ops:
  2.1 26.1 %copy-start = (f32[8,8,128]{2,1,0:T(8,128)S(1)}, f32[8,8,128]{2,1,0:T(8,128)}, u32[]{:S(2)}) copy-start(f32[8,8,128]{2,1,0:T(8,128)} %refs_2_.13) | copy-start | bytes 98308
  2.1 26.1 %copy-start.1 = (f32[8,8,128]{2,1,0:T(8,128)S(1)}, f32[8,8,128]{2,1,0:T(8,128)}, u32[]{:S(2)}) copy-start(f32[8,8,128]{2,1,0:T(8,128)} %refs_3_.13) | copy-start | bytes 98308
  2.1 26.1 %copy-start.2 = (f32[8,8,128]{2,1,0:T(8,128)S(1)}, f32[8,8,128]{2,1,0:T(8,128)}, u32[]{:S(2)}) copy-start(f32[8,8,128]{2,1,0:T(8,128)} %refs_1_.13) | copy-start | bytes 98308
  2.2 26.1 %copy-start.3 = (f32[8,8,128]{2,1,0:T(8,128)S(1)}, f32[8,8,128]{2,1,0:T(8,128)}, u32[]{:S(2)}) copy-start(f32[8,8,128]{2,1,0:T(8,128)} %refs_4_.13) | copy-start | bytes 98308
  2.2 26.1 %copy-start.4 = (s32[4,1,2,128]{3,2,1,0:T(2,128)S(1)}, s32[4,1,2,128]{3,2,1,0:T(2,128)}, u32[]{:S(2)}) copy-start(s32[4,1,2,128]{3,2,1,0:T(2,128)} %refs_13_.9) | copy-start | bytes 12292
  2.2 26.1 %copy-start.5 = (f32[8,8,128]{2,1,0:T(8,128)S(1)}, f32[8,8,128]{2,1,0:T(8,128)}, u32[]{:S(2)}) copy-start(f32[8,8,128]{2,1,0:T(8,128)} %refs_1_.8) | copy-start | bytes 98308
  2.2 26.0 %all-to-all-start = ((f32[32,16,128]{2,1,0:T(8,128)}), f32[32,16,128]{2,1,0:T(8,128)S(1)}, u32[]{:S(2)}, u32[]{:S(2)}) async-start(f32[32,16,128]{2,1,0:T(8,128)} %get-tuple-element.32), calls=%async_computation | async-start | bytes 524288 | tf_op jit(solution)/shard_map/all_to_all | solution.py:292
  15.5 4.9 %collective-permute-start = (f32[8,128]{1,0:T(8,128)S(1)}, f32[8,128]{1,0:T(8,128)S(1)}, u32[]{:S(2)}, u32[]{:S(2)}) collective-permute-start(f32[8,128]{1,0:T(8,128)S(1)} %get-tuple-element.33), channel_id=1, source_target_pairs={{0,1},{1,2},{2,3},{3,4},{4,5},{5,6},{6,7},{7,8},{8,9},{9,10},{10,1... | collective-permute-start | bytes 12296 | tf_op jit(solution)/shard_map/ppermute | solution.py:298
  29.7 16.5 %all-to-all-start.1 = ((f32[32,16,128]{2,1,0:T(8,128)}), f32[32,16,128]{2,1,0:T(8,128)S(1)}, u32[]{:S(2)}, u32[]{:S(2)}) async-start(f32[32,16,128]{2,1,0:T(8,128)} %get-tuple-element.37), calls=%async_computation.1 | async-start | bytes 524288 | tf_op jit(solution)/shard_map/all_to_all | solution.py:292
  33.8 5.5 %collective-permute-start.1 = (f32[8,128]{1,0:T(8,128)S(1)}, f32[8,128]{1,0:T(8,128)S(1)}, u32[]{:S(2)}, u32[]{:S(2)}) collective-permute-start(f32[8,128]{1,0:T(8,128)S(1)} %get-tuple-element.38), channel_id=1, source_target_pairs={{1,2},{3,4},{5,6},{7,8},{9,10},{11,12},{13,14},{2,1},{4,3},{6,5},{... | collective-permute-start | bytes 12296 | tf_op jit(solution)/shard_map/ppermute | solution.py:308
  35.7 4.4 %collective-permute-start.2 = (f32[8,128]{1,0:T(8,128)S(1)}, f32[8,128]{1,0:T(8,128)S(1)}, u32[]{:S(2)}, u32[]{:S(2)}) collective-permute-start(f32[8,128]{1,0:T(8,128)S(1)} %get-tuple-element.39), channel_id=1, source_target_pairs={{0,1},{1,0},{2,3},{3,2},{4,5},{5,4},{6,7},{7,6},{8,9},{9,8},{10,11... | collective-permute-start | bytes 12296 | tf_op jit(solution)/shard_map/ppermute | solution.py:309
  47.6 17.3 %all-to-all-start.2 = ((f32[32,16,128]{2,1,0:T(8,128)}), f32[32,16,128]{2,1,0:T(8,128)S(1)}, u32[]{:S(2)}, u32[]{:S(2)}) async-start(f32[32,16,128]{2,1,0:T(8,128)} %get-tuple-element.43), calls=%async_computation.2 | async-start | bytes 524288 | tf_op jit(solution)/shard_map/all_to_all | solution.py:292
  51.5 6.6 %collective-permute-start.3 = (f32[8,128]{1,0:T(8,128)S(1)}, f32[8,128]{1,0:T(8,128)S(1)}, u32[]{:S(2)}, u32[]{:S(2)}) collective-permute-start(f32[8,128]{1,0:T(8,128)S(1)} %get-tuple-element.44), channel_id=1, source_target_pairs={{1,2},{3,4},{5,6},{7,8},{9,10},{11,12},{13,14},{2,1},{4,3},{6,5},{... | collective-permute-start | bytes 12296 | tf_op jit(solution)/shard_map/ppermute | solution.py:308
  53.4 5.5 %collective-permute-start.4 = (f32[8,128]{1,0:T(8,128)S(1)}, f32[8,128]{1,0:T(8,128)S(1)}, u32[]{:S(2)}, u32[]{:S(2)}) collective-permute-start(f32[8,128]{1,0:T(8,128)S(1)} %get-tuple-element.45), channel_id=1, source_target_pairs={{0,1},{1,0},{2,3},{3,2},{4,5},{5,4},{6,7},{7,6},{8,9},{9,8},{10,11... | collective-permute-start | bytes 12296 | tf_op jit(solution)/shard_map/ppermute | solution.py:309
  66.3 17.3 %all-to-all-start.3 = ((f32[32,16,128]{2,1,0:T(8,128)}), f32[32,16,128]{2,1,0:T(8,128)S(1)}, u32[]{:S(2)}, u32[]{:S(2)}) async-start(f32[32,16,128]{2,1,0:T(8,128)} %get-tuple-element.48), calls=%async_computation.3 | async-start | bytes 524288 | tf_op jit(solution)/shard_map/all_to_all | solution.py:292
  70.2 6.7 %collective-permute-start.5 = (f32[8,128]{1,0:T(8,128)S(1)}, f32[8,128]{1,0:T(8,128)S(1)}, u32[]{:S(2)}, u32[]{:S(2)}) collective-permute-start(f32[8,128]{1,0:T(8,128)S(1)} %get-tuple-element.49), channel_id=1, source_target_pairs={{1,2},{3,4},{5,6},{7,8},{9,10},{11,12},{13,14},{2,1},{4,3},{6,5},{... | collective-permute-start | bytes 12296 | tf_op jit(solution)/shard_map/ppermute | solution.py:308
  72.1 5.6 %collective-permute-start.6 = (f32[8,128]{1,0:T(8,128)S(1)}, f32[8,128]{1,0:T(8,128)S(1)}, u32[]{:S(2)}, u32[]{:S(2)}) collective-permute-start(f32[8,128]{1,0:T(8,128)S(1)} %get-tuple-element.50), channel_id=1, source_target_pairs={{0,1},{1,0},{2,3},{3,2},{4,5},{5,4},{6,7},{7,6},{8,9},{9,8},{10,11... | collective-permute-start | bytes 12296 | tf_op jit(solution)/shard_map/ppermute | solution.py:309
  85.0 17.4 %all-to-all-start.4 = ((f32[32,16,128]{2,1,0:T(8,128)}), f32[32,16,128]{2,1,0:T(8,128)S(1)}, u32[]{:S(2)}, u32[]{:S(2)}) async-start(f32[32,16,128]{2,1,0:T(8,128)} %get-tuple-element.53), calls=%async_computation.4 | async-start | bytes 524288 | tf_op jit(solution)/shard_map/all_to_all | solution.py:292
  88.9 5.6 %collective-permute-start.7 = (f32[8,128]{1,0:T(8,128)S(1)}, f32[8,128]{1,0:T(8,128)S(1)}, u32[]{:S(2)}, u32[]{:S(2)}) collective-permute-start(f32[8,128]{1,0:T(8,128)S(1)} %get-tuple-element.54), channel_id=1, source_target_pairs={{1,2},{3,4},{5,6},{7,8},{9,10},{11,12},{13,14},{2,1},{4,3},{6,5},{... | collective-permute-start | bytes 12296 | tf_op jit(solution)/shard_map/ppermute | solution.py:308
  90.8 4.4 %collective-permute-start.8 = (f32[8,128]{1,0:T(8,128)S(1)}, f32[8,128]{1,0:T(8,128)S(1)}, u32[]{:S(2)}, u32[]{:S(2)}) collective-permute-start(f32[8,128]{1,0:T(8,128)S(1)} %get-tuple-element.55), channel_id=1, source_target_pairs={{0,1},{1,0},{2,3},{3,2},{4,5},{5,4},{6,7},{7,6},{8,9},{9,8},{10,11... | collective-permute-start | bytes 12296 | tf_op jit(solution)/shard_map/ppermute | solution.py:309
  103.9 16.1 %all-to-all-start.5 = ((f32[32,16,128]{2,1,0:T(8,128)}), f32[32,16,128]{2,1,0:T(8,128)S(1)}, u32[]{:S(2)}, u32[]{:S(2)}) async-start(f32[32,16,128]{2,1,0:T(8,128)} %get-tuple-element.58), calls=%async_computation.5 | async-start | bytes 524288 | tf_op jit(solution)/shard_map/all_to_all | solution.py:292
  107.7 4.9 %collective-permute-start.9 = (f32[8,128]{1,0:T(8,128)S(1)}, f32[8,128]{1,0:T(8,128)S(1)}, u32[]{:S(2)}, u32[]{:S(2)}) collective-permute-start(f32[8,128]{1,0:T(8,128)S(1)} %get-tuple-element.59), channel_id=1, source_target_pairs={{1,2},{3,4},{5,6},{7,8},{9,10},{11,12},{13,14},{2,1},{4,3},{6,5},{... | collective-permute-start | bytes 12296 | tf_op jit(solution)/shard_map/ppermute | solution.py:308
  109.7 3.3 %collective-permute-start.10 = (f32[8,128]{1,0:T(8,128)S(1)}, f32[8,128]{1,0:T(8,128)S(1)}, u32[]{:S(2)}, u32[]{:S(2)}) collective-permute-start(f32[8,128]{1,0:T(8,128)S(1)} %get-tuple-element.60), channel_id=1, source_target_pairs={{0,1},{1,0},{2,3},{3,2},{4,5},{5,4},{6,7},{7,6},{8,9},{9,8},{10,11... | collective-permute-start | bytes 12296 | tf_op jit(solution)/shard_map/ppermute | solution.py:309

commit v4 on v3

v4 whole, which is shorter than its diff:
```python
import jax
import jax.numpy as jnp
from jax import lax
from jax.experimental import pallas as pl
from jax.experimental.pallas import tpu as pltpu
from jax.sharding import PartitionSpec as P

SWEEPS = 6
F32 = jnp.float32
BF16 = jnp.bfloat16


def split3(value):
    high = value.astype(BF16)
    rest = value - high.astype(F32)
    middle = rest.astype(BF16)
    low = (rest - middle.astype(F32)).astype(BF16)
    return high, middle, low


def iota(shape, dim):
    return lax.broadcasted_iota(jnp.int32, shape, dim)


def lane_onehot(idx, lanes):
    lane_of = idx & (lanes - 1)
    pieces = []
    for row in range(idx.shape[0]):
        hit = iota((lanes, idx.shape[1]), 0) == lane_of[row : row + 1, :]
        pieces.append(jnp.where(hit, F32(1.0), F32(0.0)).astype(BF16))
    return jnp.concatenate(pieces, axis=1)


def row_hit(idx, row, lanes, count):
    shift = lanes.bit_length() - 1
    row_of = lax.shift_right_logical(idx[row : row + 1, :], shift)
    return iota((count, idx.shape[1]), 0) == row_of


def scatter(flux, idx, lane_hot, count, lanes):
    parts = [part.astype(F32) for part in split3(flux)]
    columns = []
    for row in range(idx.shape[0]):
        hit = row_hit(idx, row, lanes, count)
        columns.append(
            jnp.concatenate(
                [jnp.where(hit, part[row : row + 1, :], F32(0.0)).astype(BF16) for part in parts],
                axis=0,
            )
        )
    spread = jnp.concatenate(columns, axis=1)
    out = lax.dot_general(
        spread, lane_hot, (((1,), (1,)), ((), ())), preferred_element_type=F32
    )
    return out[:count] + out[count : 2 * count] + out[2 * count :]


def gather(cells, idx, lane_hot, lanes):
    count = cells.shape[0]
    stacked = jnp.concatenate(split3(cells), axis=0)
    picked = lax.dot_general(
        stacked, lane_hot, (((1,), (0,)), ((), ())), preferred_element_type=F32
    )
    picked = picked[:count] + picked[count : 2 * count] + picked[2 * count :]
    slots = idx.shape[1]
    out = jnp.zeros(idx.shape, F32)
    for row in range(idx.shape[0]):
        part = jnp.where(
            row_hit(idx, row, lanes, count), picked[:, row * slots : (row + 1) * slots], F32(0.0)
        )
        total = jnp.sum(part, axis=0, keepdims=True)
        out = jnp.where(iota(idx.shape, 0) == row, total, out)
    return out


def well_update(rate, index, fm, seg, cell_p):
    slots = seg.shape[1]
    fp = pltpu.roll(fm, slots - 1, 1)
    seg_prev = pltpu.roll(seg, 1, 1)
    seg_next = pltpu.roll(seg, slots - 1, 1)
    seg_res = rate - (
        index * (seg - cell_p) + fm * (seg - seg_prev) + fp * (seg - seg_next)
    )
    return seg + F32(0.8) * seg_res / (index + fm + fp)


UNIT = 4
PARTS = 48


def z_shifted(plane, step):
    size = plane.shape[1]
    moved = pltpu.roll(plane, (-step) % size, 1)
    at = size - 1 if step > 0 else 0
    return jnp.where(iota(plane.shape, 1) == at, F32(0.0), moved)


def y_moved(plane, edge, step):
    size = plane.shape[0]
    at = size - 1 if step > 0 else 0
    return jnp.where(iota(plane.shape, 0) == at, edge, pltpu.roll(plane, (-step) % size, 0))


def places():
    unit = lax.axis_index("gx") // UNIT
    odd = unit & 1
    half = 4 * PARTS + 8 * UNIT
    return unit, odd * 2 * PARTS, odd * half + 2 * PARTS, (1 - odd) * half


def rows_at(recv_ref, start, count=8):
    return recv_ref[pl.ds(pl.multiple_of(start, 8), count), :]


def lifted(piece, shift):
    tall = jnp.concatenate([piece, jnp.zeros_like(piece)], axis=0)
    shift = shift % tall.shape[0]
    return pltpu.roll(tall, shift, 0) if shift else tall


def window(rows, y, block):
    start = 16 * y + 6 - 2 * block
    moved = pltpu.roll(rows, (-start) % rows.shape[0], 0) if start else rows
    return moved[:8]


def spread_wells(flux, host, held_ref, term_ref):
    hots = []
    for y in range(2):
        for block in range(UNIT):
            near_host = window(host, y, block)
            part = window(flux, y, block)
            part = jnp.where(near_host == (iota(part.shape, 0) // 2).astype(F32), part, F32(0.0))
            idx = held_ref[2 * block + y]
            hot = lane_onehot(idx, 128)
            hots.append(hot)
            term = scatter(part, idx, hot, 64, 128)
            term_ref[pl.ds(32 * y + 8 * block, 8)] = term.reshape(8, 8, 128)
    return hots


def send_out(p_ref, held_ref, hots, send_ref, face_ref):
    for y in range(2):
        for block in range(UNIT):
            cells = p_ref[pl.ds(32 * y + 8 * block, 8)].reshape(64, 128)
            vals = gather(cells, held_ref[2 * block + y], hots[UNIT * y + block], 128)
            send_ref[pl.ds(PARTS * y + 8 * block, 8), :] = vals
        send_ref[pl.ds(PARTS * y + 32, 8), :] = p_ref[32 * y]
        send_ref[pl.ds(PARTS * y + 40, 8), :] = p_ref[32 * y + 31]
    upper = (lax.axis_index("gy") & 1) == 1
    for x in range(32):
        face_ref[x : x + 1, :] = jnp.where(upper, p_ref[32 + x, 7:8, :], p_ref[x, 0:1, :])


def field(fields_ref, which, y, x):
    return fields_ref[2 * (x // 8) + y, pl.ds(64 * which + 8 * (x % 8), 8), :]


def pack_kernel(
    rhs_ref, acc_ref, tx_ref, ty_ref, tz_ref, held_ref, host_ref, index_ref, cond_ref, rate_ref, small_ref, large_ref
):
    members = large_ref.shape[0]
    pack = jnp.concatenate(
        [host_ref[0].astype(F32), index_ref[0], cond_ref[0], rate_ref[0]], axis=0
    )
    edge = jnp.concatenate([ty_ref[x, 7:8, :] for x in range(8)], axis=0)
    for m in range(members):
        small_ref[m, 0:8, :] = pack
        small_ref[m, 8:16, :] = tx_ref[7]
        small_ref[m, 16:24, :] = edge
    for which, ref in enumerate((rhs_ref, acc_ref, tx_ref, ty_ref, tz_ref)):
        whole = ref[...].reshape(64, 128)
        for m in range(members):
            large_ref[m, 64 * which : 64 * which + 64, :] = whole
    held = held_ref[...].reshape(8, 128).astype(F32)
    for m in range(members):
        large_ref[m, 320:328, :] = held


def share_kernel(small_ref, send_ref, face_ref):
    for y in range(2):
        for block in range(UNIT):
            send_ref[pl.ds(PARTS * y + 8 * block, 8), :] = small_ref[2 * block + y, 0:8, :]
        send_ref[pl.ds(PARTS * y + 32, 8), :] = jnp.zeros((8, 128), F32)
        send_ref[pl.ds(PARTS * y + 40, 8), :] = small_ref[2 * (UNIT - 1) + y, 8:16, :]
    for block in range(UNIT):
        face_ref[pl.ds(8 * block, 8), :] = small_ref[2 * block + 1, 16:24, :]


def first_kernel(
    fields_ref, recv_ref, p_ref, gain_ref, wx_ref, wy_ref, seg_ref, well_ref, held_ref, send_ref, face_ref, term_ref
):
    unit, here, after, before = places()
    own = iota((16, 128), 0) // 2
    groups = []
    for array in range(4):
        halves = []
        for y in range(2):
            whole = jnp.zeros((16, 128), F32)
            for owner in range(-UNIT, UNIT):
                base = here + 8 * owner if owner >= 0 else before + 8 * (owner + UNIT)
                place = UNIT - 1 - owner
                moved = lifted(rows_at(recv_ref, base + PARTS * y), 2 * place - 2 * array)
                whole = jnp.where(own == place, moved, whole)
            halves.append(whole)
        groups.append(jnp.concatenate(halves, axis=0))
    host, index, cond, rate = groups
    fm = jnp.where(iota(cond.shape, 1) > 0, cond, F32(0.0))
    well_ref[0], well_ref[1], well_ref[2], well_ref[3] = host, index, fm, rate
    zero = jnp.zeros(cond.shape, F32)
    seg = well_update(rate, index, fm, zero, zero)
    seg_ref[...] = seg
    for m in range(2 * UNIT):
        held_ref[m] = fields_ref[m, 320:328, :].astype(jnp.int32)
    hots = spread_wells(F32(0.0) - index * seg, host, held_ref, term_ref)
    wy_ref[...] = recv_ref[4 * PARTS : 4 * PARTS + 32, :]
    for y in range(2):
        west = rows_at(recv_ref, before + PARTS * y + 40)
        west = jnp.where(unit == 0, F32(0.0), west)
        wx_ref[y] = west
        for x in range(32):
            tx, ty, tz = (field(fields_ref, which, y, x) for which in (2, 3, 4))
            edge = field(fields_ref, 3, 0, x)[7:8, :] if y else wy_ref[x : x + 1, :]
            diag = field(fields_ref, 1, y, x) + tx + (field(fields_ref, 2, y, x - 1) if x else west)
            diag = diag + ty + y_moved(ty, edge, -1) + tz + z_shifted(tz, -1)
            gain = F32(0.7) / diag
            gain_ref[32 * y + x] = gain
            p_ref[32 * y + x] = gain * (field(fields_ref, 0, y, x) - term_ref[32 * y + x])
    send_out(p_ref, held_ref, hots, send_ref, face_ref)


def sweep_kernel(
    p_in, fields_ref, gain_ref, wx_ref, wy_ref, recv_ref, seg_in, well_ref, held_ref, *rest, last
):
    if last:
        out_ref, seg_out, p_ref, term_ref = rest
    else:
        p_ref, seg_ref, send_ref, face_ref, term_ref = rest
    unit, here, after, before = places()
    units = lax.axis_size("gx") // UNIT
    host, index, fm, rate = well_ref[0], well_ref[1], well_ref[2], well_ref[3]
    own = iota((16, 128), 0) // 2
    halves = []
    for y in range(2):
        cell = jnp.zeros((16, 128), F32)
        near_host = host[16 * y : 16 * y + 16]
        for block in range(1 - UNIT, 2 * UNIT - 1):
            base = here if 0 <= block < UNIT else after if block > 0 else before
            vals = rows_at(recv_ref, base + PARTS * y + 8 * (block % UNIT))
            hit = near_host == (own + block - 3).astype(F32)
            cell = jnp.where(hit, lifted(vals, 6 - 2 * block), cell)
        halves.append(cell)
    cell_p = jnp.concatenate(halves, axis=0)
    seg = well_update(rate, index, fm, seg_in[...], cell_p)
    hots = spread_wells(index * (cell_p - seg), host, held_ref, term_ref)
    half = 4 * PARTS + 32
    for y in range(2):
        west = rows_at(recv_ref, before + PARTS * y + 40)
        west = jnp.where(unit == 0, F32(0.0), west)
        east = rows_at(recv_ref, after + PARTS * y + 32)
        east = jnp.where(unit == units - 1, F32(0.0), east)
        for x in range(32):
            block = p_in[32 * y + x]
            tx, ty, tz = (field(fields_ref, which, y, x) for which in (2, 3, 4))
            if y:
                south, north = p_in[x, 7:8, :], recv_ref[half + 4 * PARTS + x : half + 4 * PARTS + x + 1, :]
                edge = field(fields_ref, 3, 0, x)[7:8, :]
            else:
                south, north = recv_ref[4 * PARTS + x : 4 * PARTS + x + 1, :], p_in[32 + x, 0:1, :]
                edge = wy_ref[x : x + 1, :]
            total = field(fields_ref, 0, y, x) - term_ref[32 * y + x]
            total = total + tx * (p_in[32 * y + x + 1] if x < 31 else east)
            if x:
                total = total + field(fields_ref, 2, y, x - 1) * p_in[32 * y + x - 1]
            else:
                total = total + wx_ref[y] * west
            total = total + ty * y_moved(block, north, 1) + y_moved(ty, edge, -1) * y_moved(block, south, -1)
            total = total + tz * z_shifted(block, 1) + z_shifted(tz, -1) * z_shifted(block, -1)
            p_ref[32 * y + x] = F32(0.3) * block + gain_ref[32 * y + x] * total
    if last:
        at = lax.axis_index("gx") % UNIT
        core = lax.axis_index("gy") & 1
        out_ref[...] = p_ref[pl.ds(32 * core + 8 * at, 8)]
        mine = seg[6:8]
        for y in range(2):
            for owner in range(UNIT):
                start = 16 * y + 2 * (UNIT - 1 - owner)
                mine = jnp.where((at == owner) & (core == y), seg[start : start + 2], mine)
        seg_out[0] = mine
    else:
        seg_ref[...] = seg
        send_out(p_ref, held_ref, hots, send_ref, face_ref)


def shards(
    rhs_field,
    accumulation,
    trans_x,
    trans_y,
    trans_z,
    held_cells,
    perf_host,
    well_index,
    seg_cond,
    seg_rate,
):
    ring = lax.axis_size("gx")
    county = lax.axis_size("gy")
    units = ring // UNIT
    facing = [(j, j + 1) for j in range(1, county - 1, 2)]
    facing += [(target, source) for source, target in facing]
    mates = [[j, j + 1] for j in range(0, county, 2)]
    chips = [
        [(UNIT * unit + x) * county + j + core for x in range(UNIT) for core in range(2)]
        for unit in range(units)
        for j in range(0, county, 2)
    ]
    columns = [
        [(((low + step + j % 2) % units) * UNIT + x) * county + j for step in range(2)]
        for j in range(county)
        for low in range(0, units, 2)
        for x in range(UNIT)
    ]

    def shape(*dims):
        return pltpu.VMEM(dims, F32)

    def result(*dims):
        return jax.ShapeDtypeStruct(dims, F32)

    def near(value):
        return pltpu.with_memory_space_constraint(value, pltpu.VMEM)

    vmem = pl.BlockSpec(memory_space=pltpu.VMEM)

    def call(body, outs, *args, placed=near, scratch=(), **static):
        return pl.pallas_call(
            lambda *refs: body(*refs, **static),
            out_shape=outs,
            in_specs=[vmem] * len(args),
            out_specs=[vmem] * len(outs),
            scratch_shapes=scratch,
        )(*map(placed, args))

    def exchanged(send, face):
        edge = lax.ppermute(face, "gy", facing)
        pair = lax.all_gather(send, ("gx", "gy"), axis_index_groups=columns, tiled=True)
        both = jnp.concatenate([pair, edge], axis=0)
        return lax.all_gather(both, "gy", axis_index_groups=mates, tiled=True)

    def among_chips(buffer):
        return lax.all_to_all(buffer, ("gx", "gy"), 0, 0, tiled=True, axis_index_groups=chips)

    small, large = call(
        pack_kernel, [result(8, 24, 128), result(8, 328, 128)], rhs_field, accumulation, trans_x, trans_y, trans_z,
        held_cells, perf_host, well_index, seg_cond, seg_rate, placed=lambda value: value,
    )
    fields = among_chips(large)
    message, edges, grid, wells = shape(96, 128), shape(32, 128), shape(64, 8, 128), shape(32, 128)
    send, face = call(share_kernel, [message, edges], among_chips(small))
    recv = exchanged(send, face)
    p, gain, wx, wy, seg, well, held, send, face = call(
        first_kernel,
        [grid, grid, shape(2, 8, 128), edges, wells, shape(4, 32, 128), pltpu.VMEM((8, 8, 128), jnp.int32), message, edges],
        fields, recv, scratch=[grid],
    )
    for sweep in range(1, SWEEPS):
        last = sweep == SWEEPS - 1
        recv = exchanged(send, face)
        outs = [result(8, 8, 128), result(1, 2, 128)] if last else [grid, wells, message, edges]
        got = call(
            sweep_kernel, outs, p, fields, gain, wx, wy, recv, seg, well, held,
            scratch=[grid, grid] if last else [grid], last=last,
        )
        p, seg = got[:2]
        if not last:
            send, face = got[2:]
    return (p, seg)


def solution(mesh):
    return jax.shard_map(
        shards,
        mesh=mesh,
        in_specs=(
            P("gx", "gy", None),
            P("gx", "gy", None),
            P("gx", "gy", None),
            P("gx", "gy", None),
            P("gx", "gy", None),
            P(None, "gx", "gy", None),
            P("gx", "gy", None),
            P("gx", "gy", None),
            P("gx", "gy", None),
            P("gx", "gy", None),
        ),
        out_specs=(P("gx", "gy", None), P("gx", "gy", None)),
        check_vma=False,
    )
```

time: 122 us -> 111 us (0.910)
  the two profiles are of different devices: /device:TPU:16 before, /device:TPU:25 now
where the time goes in v4:
time: 111 us; the launch traced here: 110 us
  blocking collectives  63.1 us (57%)
  starting transfers between devices  27.3 us (25%)
  Pallas kernels  15.8 us (14%)
  local copies, waits for them, and re-layouts  2.43 us (2%)
    all_gather x6, blocking collectives, exchanged(): lax.all_gather(send, ('gx', 'gy'), axis_index_groups=columns, tiled=True)  41.1 us
    ppermute x6, starting transfers between devices, exchanged(): edge = lax.ppermute(face, 'gy', facing)  23 us
    pallas_call x8, Pallas kernels, call(): pl.pallas_call(lambda *refs: body(*refs, **static), out_shape=outs, in_sp...  15.8 us
    all_gather x6, blocking collectives, exchanged(): return lax.all_gather(both, 'gy', axis_index_groups=mates, tiled=True)  12 us
    all_to_all x1, blocking collectives, among_chips(): lax.all_to_all(buffer, ('gx', 'gy'), 0, 0, tiled=True, axis_index_groups=...  9.95 us
    all_to_all x1, starting transfers between devices, among_chips(): lax.all_to_all(buffer, ('gx', 'gy'), 0, 0, tiled=True, axis_index_groups=...  4.29 us
    unnamed x4, local copies, waits for them, and re-layouts  2.43 us
  transfers between devices with their start and end apart: 7, of which 1 were waited for; matrix products, arithmetic and copies ran while one was open for 0% of the time, Pallas kernels for 0%

profile of v4, /device:TPU:25, one launch (start us, length us, event | category | flops | bytes accessed | tf_op | source)
XLA Modules:
  0.0 110.4 jit_solution(192001978041220353)
XLA Ops:
  0.6 2.1 %shard_map.113 = (f32[8,24,128]{2,1,0:T(8,128)}, f32[8,328,128]{2,1,0:T(8,128)}) custom-call(f32[8,8,128]{2,1,0:T(8,128)} %refs_0_.1, f32[8,8,128]{2,1,0:T(8,128)} %refs_1_.1, f32[8,8,128]{2,1,0:T(8,128)} %refs_2_.1, f32[8,8,128]{2,1,0:T(8,128)} %refs_3_.1, f32[8,8,128]{2,1,0:T(8,128)} %refs_4_.1, s32[4,1,2,128]{3,2,1,0:T(2,128)} %refs_5_.1, ...), custom_call_target="tpu_custom_call" | custom-call | tf_op jit(solution)/shard_map/pallas_call | solution.py:337
  2.7 9.9 %all_to_all.10.refs_0_ = f32[8,24,128]{2,1,0:T(8,128)S(1)} all-to-all(f32[8,24,128]{2,1,0:T(8,128)} %get-tuple-element.32), channel_id=1, replica_groups={{0,1,16,17,32,33,48,49},{2,3,18,19,34,35,50,51},{4,5,20,21,36,37,52,53}..., dimensions={0} | all-to-all | bytes 196608 | tf_op jit(solution)/shard_map/all_to_all | solution.py:352
  12.6 4.3 %all-to-all-start = ((f32[8,328,128]{2,1,0:T(8,128)}), f32[8,328,128]{2,1,0:T(8,128)S(1)}, u32[]{:S(2)}, u32[]{:S(2)}) async-start(f32[8,328,128]{2,1,0:T(8,128)} %get-tuple-element.31), calls=%async_computation | async-start | bytes 2686976 | tf_op jit(solution)/shard_map/all_to_all | solution.py:352
  16.9 4.4 %collective-permute-start = (f32[32,128]{1,0:T(8,128)S(1)}, f32[32,128]{1,0:T(8,128)S(1)}, u32[]{:S(2)}, u32[]{:S(2)}) collective-permute-start(f32[32,128]{1,0:T(8,128)S(1)} %get-tuple-element.34), channel_id=1, source_target_pairs={{1,2},{3,4},{5,6},{7,8},{9,10},{11,12},{13,14},{2,1},{4,3},{6,5},{... | collective-permute-start | bytes 49160 | tf_op jit(solution)/shard_map/ppermute | solution.py:346
  21.4 10.9 %all_gather.36 = f32[192,128]{1,0:T(8,128)S(1)} all-gather(f32[96,128]{1,0:T(8,128)S(1)} %get-tuple-element.33), channel_id=1, replica_groups={{0,64},{16,80},{32,96},{48,112},{128,192},{144,208},{160,224},{176,240}..., dimensions={0}, use_global_device_ids=true | all-gather | bytes 147456 | tf_op jit(solution)/shard_map/all_gather | solution.py:347
  32.3 2.0 %all_gather.37.refs_1_ = f32[448,128]{1,0:T(8,128)S(1)} all-gather(f32[224,128]{1,0:T(8,128)S(1)} %pad_maximum_fusion), channel_id=1, replica_groups={{0,1},{2,3},{4,5},{6,7},{8,9},{10,11},{12,13},{14,15},{16,17},{18,19},{..., dimensions={0}, use_global_device_ids=true | all-gather | bytes 344064 | tf_op jit(solution)/shard_map/all_gather | solution.py:349
  37.6 2.2 %shard_map.115 = (f32[64,8,128]{2,1,0:T(8,128)S(1)}, f32[64,8,128]{2,1,0:T(8,128)S(1)}, f32[2,8,128]{2,1,0:T(8,128)S(1)}, f32[32,128]{1,0:T(8,128)S(1)}, f32[32,...) custom-call(f32[8,328,128]{2,1,0:T(8,128)S(1)} %copy-done.1, ...), custom_call_target="tpu_custom_call" | custom-call | tf_op jit(solution)/shard_map/pallas_call | solution.py:337
  39.8 5.2 %collective-permute-start.1 = (f32[32,128]{1,0:T(8,128)S(1)}, f32[32,128]{1,0:T(8,128)S(1)}, u32[]{:S(2)}, u32[]{:S(2)}) collective-permute-start(f32[32,128]{1,0:T(8,128)S(1)} %get-tuple-element.40), channel_id=1, source_target_pairs={{1,2},{3,4},{5,6},{7,8},{9,10},{11,12},{13,14},{2,1},{4,3},{6,5},{... | collective-permute-start | bytes 49160 | tf_op jit(solution)/shard_map/ppermute | solution.py:346
  45.0 10.9 %all_gather.38 = f32[192,128]{1,0:T(8,128)S(1)} all-gather(f32[96,128]{1,0:T(8,128)S(1)} %get-tuple-element.39), channel_id=1, replica_groups={{0,64},{16,80},{32,96},{48,112},{128,192},{144,208},{160,224},{176,240}..., dimensions={0}, use_global_device_ids=true | all-gather | bytes 147456 | tf_op jit(solution)/shard_map/all_gather | solution.py:347
  55.9 2.0 %all_gather.39.refs_5_ = f32[448,128]{1,0:T(8,128)S(1)} all-gather(f32[224,128]{1,0:T(8,128)S(1)} %pad_maximum_fusion.1), channel_id=1, replica_groups={{0,1},{2,3},{4,5},{6,7},{8,9},{10,11},{12,13},{14,15},{16,17},{18,19},{..., dimensions={0}, use_global_device_ids=true | all-gather | bytes 344064 | tf_op jit(solution)/shard_map/all_gather | solution.py:349
  57.9 2.4 %shard_map.116 = (f32[64,8,128]{2,1,0:T(8,128)S(1)}, f32[32,128]{1,0:T(8,128)S(1)}, f32[96,128]{1,0:T(8,128)S(1)}, f32[32,128]{1,0:T(8,128)S(1)}) custom-call(f32[64,8,128]{2,1,0:T(8,128)S(1)} %get-tuple-element.35.refs_0_, f32[8,328,128]{2,1,0:T(8,128)S(1)} %copy-done.1, f32[64,8,128]{2,1,0:T(8,128)S(1)} %get-tuple-element.36.refs_2_, ...), custom_call_target="tpu_custom_call" | custom-call | tf_op jit(solution)/shard_map/pallas_call | solution.py:337
  60.3 2.3 %collective-permute-start.2 = (f32[32,128]{1,0:T(8,128)S(1)}, f32[32,128]{1,0:T(8,128)S(1)}, u32[]{:S(2)}, u32[]{:S(2)}) collective-permute-start(f32[32,128]{1,0:T(8,128)S(1)} %get-tuple-element.46), channel_id=1, source_target_pairs={{1,2},{3,4},{5,6},{7,8},{9,10},{11,12},{13,14},{2,1},{4,3},{6,5},{... | collective-permute-start | bytes 49160 | tf_op jit(solution)/shard_map/ppermute | solution.py:346
  62.7 4.8 %all_gather.40 = f32[192,128]{1,0:T(8,128)S(1)} all-gather(f32[96,128]{1,0:T(8,128)S(1)} %get-tuple-element.45), channel_id=1, replica_groups={{0,64},{16,80},{32,96},{48,112},{128,192},{144,208},{160,224},{176,240}..., dimensions={0}, use_global_device_ids=true | all-gather | bytes 147456 | tf_op jit(solution)/shard_map/all_gather | solution.py:347
  69.5 2.4 %shard_map.117 = (f32[64,8,128]{2,1,0:T(8,128)S(1)}, f32[32,128]{1,0:T(8,128)S(1)}, f32[96,128]{1,0:T(8,128)S(1)}, f32[32,128]{1,0:T(8,128)S(1)}) custom-call(f32[64,8,128]{2,1,0:T(8,128)S(1)} %get-tuple-element.44.refs_0_, f32[8,328,128]{2,1,0:T(8,128)S(1)} %copy-done.1, f32[64,8,128]{2,1,0:T(8,128)S(1)} %get-tuple-element.36.refs_2_, ...), custom_call_target="tpu_custom_call" | custom-call | tf_op jit(solution)/shard_map/pallas_call | solution.py:337
  71.9 4.4 %collective-permute-start.3 = (f32[32,128]{1,0:T(8,128)S(1)}, f32[32,128]{1,0:T(8,128)S(1)}, u32[]{:S(2)}, u32[]{:S(2)}) collective-permute-start(f32[32,128]{1,0:T(8,128)S(1)} %get-tuple-element.50), channel_id=1, source_target_pairs={{1,2},{3,4},{5,6},{7,8},{9,10},{11,12},{13,14},{2,1},{4,3},{6,5},{... | collective-permute-start | bytes 49160 | tf_op jit(solution)/shard_map/ppermute | solution.py:346
  76.3 4.8 %all_gather.42 = f32[192,128]{1,0:T(8,128)S(1)} all-gather(f32[96,128]{1,0:T(8,128)S(1)} %get-tuple-element.49), channel_id=1, replica_groups={{0,64},{16,80},{32,96},{48,112},{128,192},{144,208},{160,224},{176,240}..., dimensions={0}, use_global_device_ids=true | all-gather | bytes 147456 | tf_op jit(solution)/shard_map/all_gather | solution.py:347
  83.1 2.4 %shard_map.118 = (f32[64,8,128]{2,1,0:T(8,128)S(1)}, f32[32,128]{1,0:T(8,128)S(1)}, f32[96,128]{1,0:T(8,128)S(1)}, f32[32,128]{1,0:T(8,128)S(1)}) custom-call(f32[64,8,128]{2,1,0:T(8,128)S(1)} %get-tuple-element.48.refs_0_, f32[8,328,128]{2,1,0:T(8,128)S(1)} %copy-done.1, f32[64,8,128]{2,1,0:T(8,128)S(1)} %get-tuple-element.36.refs_2_, ...), custom_call_target="tpu_custom_call" | custom-call | tf_op jit(solution)/shard_map/pallas_call | solution.py:337
  85.5 2.3 %collective-permute-start.4 = (f32[32,128]{1,0:T(8,128)S(1)}, f32[32,128]{1,0:T(8,128)S(1)}, u32[]{:S(2)}, u32[]{:S(2)}) collective-permute-start(f32[32,128]{1,0:T(8,128)S(1)} %get-tuple-element.54), channel_id=1, source_target_pairs={{1,2},{3,4},{5,6},{7,8},{9,10},{11,12},{13,14},{2,1},{4,3},{6,5},{... | collective-permute-start | bytes 49160 | tf_op jit(solution)/shard_map/ppermute | solution.py:346
  87.9 4.8 %all_gather.44 = f32[192,128]{1,0:T(8,128)S(1)} all-gather(f32[96,128]{1,0:T(8,128)S(1)} %get-tuple-element.53), channel_id=1, replica_groups={{0,64},{16,80},{32,96},{48,112},{128,192},{144,208},{160,224},{176,240}..., dimensions={0}, use_global_device_ids=true | all-gather | bytes 147456 | tf_op jit(solution)/shard_map/all_gather | solution.py:347
  92.7 2.2 %all_gather.45.refs_5_ = f32[448,128]{1,0:T(8,128)S(1)} all-gather(f32[224,128]{1,0:T(8,128)S(1)} %pad_maximum_fusion.4), channel_id=1, replica_groups={{0,1},{2,3},{4,5},{6,7},{8,9},{10,11},{12,13},{14,15},{16,17},{18,19},{..., dimensions={0}, use_global_device_ids=true | all-gather | bytes 344064 | tf_op jit(solution)/shard_map/all_gather | solution.py:349
  94.9 2.4 %shard_map.119 = (f32[64,8,128]{2,1,0:T(8,128)S(1)}, f32[32,128]{1,0:T(8,128)S(1)}, f32[96,128]{1,0:T(8,128)S(1)}, f32[32,128]{1,0:T(8,128)S(1)}) custom-call(f32[64,8,128]{2,1,0:T(8,128)S(1)} %get-tuple-element.52.refs_0_, f32[8,328,128]{2,1,0:T(8,128)S(1)} %copy-done.1, f32[64,8,128]{2,1,0:T(8,128)S(1)} %get-tuple-element.36.refs_2_, ...), custom_call_target="tpu_custom_call" | custom-call | tf_op jit(solution)/shard_map/pallas_call | solution.py:337
  97.3 4.4 %collective-permute-start.5 = (f32[32,128]{1,0:T(8,128)S(1)}, f32[32,128]{1,0:T(8,128)S(1)}, u32[]{:S(2)}, u32[]{:S(2)}) collective-permute-start(f32[32,128]{1,0:T(8,128)S(1)} %get-tuple-element.58), channel_id=1, source_target_pairs={{1,2},{3,4},{5,6},{7,8},{9,10},{11,12},{13,14},{2,1},{4,3},{6,5},{... | collective-permute-start | bytes 49160 | tf_op jit(solution)/shard_map/ppermute | solution.py:346
  101.6 4.8 %all_gather.46 = f32[192,128]{1,0:T(8,128)S(1)} all-gather(f32[96,128]{1,0:T(8,128)S(1)} %get-tuple-element.57), channel_id=1, replica_groups={{0,64},{16,80},{32,96},{48,112},{128,192},{144,208},{160,224},{176,240}..., dimensions={0}, use_global_device_ids=true | all-gather | bytes 147456 | tf_op jit(solution)/shard_map/all_gather | solution.py:347
  106.5 2.0 %all_gather.47.refs_5_ = f32[448,128]{1,0:T(8,128)S(1)} all-gather(f32[224,128]{1,0:T(8,128)S(1)} %pad_maximum_fusion.5), channel_id=1, replica_groups={{0,1},{2,3},{4,5},{6,7},{8,9},{10,11},{12,13},{14,15},{16,17},{18,19},{..., dimensions={0}, use_global_device_ids=true | all-gather | bytes 344064 | tf_op jit(solution)/shard_map/all_gather | solution.py:349
  (21 shorter events, 9.3 us)
Async XLA Ops:
  12.6 22.6 %all-to-all-start = ((f32[8,328,128]{2,1,0:T(8,128)}), f32[8,328,128]{2,1,0:T(8,128)S(1)}, u32[]{:S(2)}, u32[]{:S(2)}) async-start(f32[8,328,128]{2,1,0:T(8,128)} %get-tuple-element.31), calls=%async_computation | async-start | bytes 2686976 | tf_op jit(solution)/shard_map/all_to_all | solution.py:352
  16.9 15.3 %collective-permute-start = (f32[32,128]{1,0:T(8,128)S(1)}, f32[32,128]{1,0:T(8,128)S(1)}, u32[]{:S(2)}, u32[]{:S(2)}) collective-permute-start(f32[32,128]{1,0:T(8,128)S(1)} %get-tuple-element.34), channel_id=1, source_target_pairs={{1,2},{3,4},{5,6},{7,8},{9,10},{11,12},{13,14},{2,1},{4,3},{6,5},{... | collective-permute-start | bytes 49160 | tf_op jit(solution)/shard_map/ppermute | solution.py:346
  35.2 1.1 copy-start
  36.3 1.3 %copy-start.1 = (f32[8,328,128]{2,1,0:T(8,128)S(1)}, f32[8,328,128]{2,1,0:T(8,128)}, u32[]{:S(2)}) copy-start(f32[8,328,128]{2,1,0:T(8,128)} %copy-done) | copy-start | bytes 4030468
  39.8 16.1 %collective-permute-start.1 = (f32[32,128]{1,0:T(8,128)S(1)}, f32[32,128]{1,0:T(8,128)S(1)}, u32[]{:S(2)}, u32[]{:S(2)}) collective-permute-start(f32[32,128]{1,0:T(8,128)S(1)} %get-tuple-element.40), channel_id=1, source_target_pairs={{1,2},{3,4},{5,6},{7,8},{9,10},{11,12},{13,14},{2,1},{4,3},{6,5},{... | collective-permute-start | bytes 49160 | tf_op jit(solution)/shard_map/ppermute | solution.py:346
  60.3 7.2 %collective-permute-start.2 = (f32[32,128]{1,0:T(8,128)S(1)}, f32[32,128]{1,0:T(8,128)S(1)}, u32[]{:S(2)}, u32[]{:S(2)}) collective-permute-start(f32[32,128]{1,0:T(8,128)S(1)} %get-tuple-element.46), channel_id=1, source_target_pairs={{1,2},{3,4},{5,6},{7,8},{9,10},{11,12},{13,14},{2,1},{4,3},{6,5},{... | collective-permute-start | bytes 49160 | tf_op jit(solution)/shard_map/ppermute | solution.py:346
  71.9 9.2 %collective-permute-start.3 = (f32[32,128]{1,0:T(8,128)S(1)}, f32[32,128]{1,0:T(8,128)S(1)}, u32[]{:S(2)}, u32[]{:S(2)}) collective-permute-start(f32[32,128]{1,0:T(8,128)S(1)} %get-tuple-element.50), channel_id=1, source_target_pairs={{1,2},{3,4},{5,6},{7,8},{9,10},{11,12},{13,14},{2,1},{4,3},{6,5},{... | collective-permute-start | bytes 49160 | tf_op jit(solution)/shard_map/ppermute | solution.py:346
  85.5 7.2 %collective-permute-start.4 = (f32[32,128]{1,0:T(8,128)S(1)}, f32[32,128]{1,0:T(8,128)S(1)}, u32[]{:S(2)}, u32[]{:S(2)}) collective-permute-start(f32[32,128]{1,0:T(8,128)S(1)} %get-tuple-element.54), channel_id=1, source_target_pairs={{1,2},{3,4},{5,6},{7,8},{9,10},{11,12},{13,14},{2,1},{4,3},{6,5},{... | collective-permute-start | bytes 49160 | tf_op jit(solution)/shard_map/ppermute | solution.py:346
  97.3 9.2 %collective-permute-start.5 = (f32[32,128]{1,0:T(8,128)S(1)}, f32[32,128]{1,0:T(8,128)S(1)}, u32[]{:S(2)}, u32[]{:S(2)}) collective-permute-start(f32[32,128]{1,0:T(8,128)S(1)} %get-tuple-element.58), channel_id=1, source_target_pairs={{1,2},{3,4},{5,6},{7,8},{9,10},{11,12},{13,14},{2,1},{4,3},{6,5},{... | collective-permute-start | bytes 49160 | tf_op jit(solution)/shard_map/ppermute | solution.py:346

commit v5 on v4

--- a/solution.py
+++ b/solution.py
@@ -124,17 +124,21 @@
     return moved[:8]
 
 
+def spread_block(flux, host, held_ref, y, block):
+    near_host = window(host, y, block)
+    part = window(flux, y, block)
+    part = jnp.where(near_host == (iota(part.shape, 0) // 2).astype(F32), part, F32(0.0))
+    idx = held_ref[2 * block + y]
+    hot = lane_onehot(idx, 128)
+    return scatter(part, idx, hot, 64, 128), hot
+
+
 def spread_wells(flux, host, held_ref, term_ref):
     hots = []
     for y in range(2):
         for block in range(UNIT):
-            near_host = window(host, y, block)
-            part = window(flux, y, block)
-            part = jnp.where(near_host == (iota(part.shape, 0) // 2).astype(F32), part, F32(0.0))
-            idx = held_ref[2 * block + y]
-            hot = lane_onehot(idx, 128)
+            term, hot = spread_block(flux, host, held_ref, y, block)
             hots.append(hot)
-            term = scatter(part, idx, hot, 64, 128)
             term_ref[pl.ds(32 * y + 8 * block, 8)] = term.reshape(8, 8, 128)
     return hots
 
@@ -188,7 +192,7 @@
 
 
 def first_kernel(
-    fields_ref, recv_ref, p_ref, gain_ref, wx_ref, wy_ref, seg_ref, well_ref, held_ref, send_ref, face_ref, term_ref
+    fields_ref, recv_ref, p_ref, coef_ref, wx_ref, wy_ref, seg_ref, well_ref, held_ref, send_ref, face_ref, term_ref
 ):
     unit, here, after, before = places()
     own = iota((16, 128), 0) // 2
@@ -214,26 +218,30 @@
         held_ref[m] = fields_ref[m, 320:328, :].astype(jnp.int32)
     hots = spread_wells(F32(0.0) - index * seg, host, held_ref, term_ref)
     wy_ref[...] = recv_ref[4 * PARTS : 4 * PARTS + 32, :]
+    top = iota((8, 128), 1) == 127
     for y in range(2):
         west = rows_at(recv_ref, before + PARTS * y + 40)
         west = jnp.where(unit == 0, F32(0.0), west)
         wx_ref[y] = west
         for x in range(32):
             tx, ty, tz = (field(fields_ref, which, y, x) for which in (2, 3, 4))
-            edge = field(fields_ref, 3, 0, x)[7:8, :] if y else wy_ref[x : x + 1, :]
-            diag = field(fields_ref, 1, y, x) + tx + (field(fields_ref, 2, y, x - 1) if x else west)
-            diag = diag + ty + y_moved(ty, edge, -1) + tz + z_shifted(tz, -1)
-            gain = F32(0.7) / diag
-            gain_ref[32 * y + x] = gain
-            p_ref[32 * y + x] = gain * (field(fields_ref, 0, y, x) - term_ref[32 * y + x])
+            edge = field(fields_ref, 3, 0, x)[7:8, :] if y else recv_ref[4 * PARTS + x : 4 * PARTS + x + 1, :]
+            wx = field(fields_ref, 2, y, x - 1) if x else west
+            wy = y_moved(ty, edge, -1)
+            inner = jnp.where(top, F32(0.0), tz)
+            wz = pltpu.roll(inner, 1, 1)
+            gain = F32(0.7) / (field(fields_ref, 1, y, x) + tx + wx + ty + wy + tz + wz)
+            base = gain * field(fields_ref, 0, y, x)
+            at = 32 * y + x
+            for which, value in enumerate((tx, ty, inner, gain, base)):
+                coef_ref[which, at] = value
+            p_ref[at] = base - gain * term_ref[at]
     send_out(p_ref, held_ref, hots, send_ref, face_ref)
 
 
-def sweep_kernel(
-    p_in, fields_ref, gain_ref, wx_ref, wy_ref, recv_ref, seg_in, well_ref, held_ref, *rest, last
-):
+def sweep_kernel(p_in, coef_ref, wx_ref, wy_ref, recv_ref, seg_in, well_ref, held_ref, *rest, last):
     if last:
-        out_ref, seg_out, p_ref, term_ref = rest
+        out_ref, seg_out = rest
     else:
         p_ref, seg_ref, send_ref, face_ref, term_ref = rest
     unit, here, after, before = places()
@@ -252,42 +260,53 @@
         halves.append(cell)
     cell_p = jnp.concatenate(halves, axis=0)
     seg = well_update(rate, index, fm, seg_in[...], cell_p)
-    hots = spread_wells(index * (cell_p - seg), host, held_ref, term_ref)
+    flux = index * (cell_p - seg)
     half = 4 * PARTS + 32
-    for y in range(2):
-        west = rows_at(recv_ref, before + PARTS * y + 40)
-        west = jnp.where(unit == 0, F32(0.0), west)
-        east = rows_at(recv_ref, after + PARTS * y + 32)
-        east = jnp.where(unit == units - 1, F32(0.0), east)
-        for x in range(32):
-            block = p_in[32 * y + x]
-            tx, ty, tz = (field(fields_ref, which, y, x) for which in (2, 3, 4))
-            if y:
-                south, north = p_in[x, 7:8, :], recv_ref[half + 4 * PARTS + x : half + 4 * PARTS + x + 1, :]
-                edge = field(fields_ref, 3, 0, x)[7:8, :]
-            else:
-                south, north = recv_ref[4 * PARTS + x : 4 * PARTS + x + 1, :], p_in[32 + x, 0:1, :]
-                edge = wy_ref[x : x + 1, :]
-            total = field(fields_ref, 0, y, x) - term_ref[32 * y + x]
-            total = total + tx * (p_in[32 * y + x + 1] if x < 31 else east)
-            if x:
-                total = total + field(fields_ref, 2, y, x - 1) * p_in[32 * y + x - 1]
-            else:
-                total = total + wx_ref[y] * west
-            total = total + ty * y_moved(block, north, 1) + y_moved(ty, edge, -1) * y_moved(block, south, -1)
-            total = total + tz * z_shifted(block, 1) + z_shifted(tz, -1) * z_shifted(block, -1)
-            p_ref[32 * y + x] = F32(0.3) * block + gain_ref[32 * y + x] * total
+    lines = (slice(4 * PARTS, half), slice(half + 4 * PARTS, 2 * half))
+
+    def updated(y, x, term):
+        at = 32 * y + x
+        block = p_in[at]
+        if y:
+            south, north = p_in[x, 7:8, :], recv_ref[lines[1].start + x : lines[1].start + x + 1, :]
+        else:
+            south, north = recv_ref[lines[0].start + x : lines[0].start + x + 1, :], p_in[32 + x, 0:1, :]
+        if x < 31:
+            east = p_in[at + 1]
+        else:
+            east = rows_at(recv_ref, after + PARTS * y + 32)
+            east = jnp.where(unit == units - 1, F32(0.0), east)
+        if x:
+            west = p_in[at - 1]
+        else:
+            west = rows_at(recv_ref, before + PARTS * y + 40)
+            west = jnp.where(unit == 0, F32(0.0), west)
+        tx, ty, tz, gain, base = (coef_ref[which, at] for which in range(5))
+        edge = coef_ref[1, x, 7:8, :] if y else wy_ref[x : x + 1, :]
+        total = tx * east + (coef_ref[0, at - 1] if x else wx_ref[y]) * west
+        total = total + ty * y_moved(block, north, 1) + y_moved(ty, edge, -1) * y_moved(block, south, -1)
+        total = total + tz * pltpu.roll(block, 127, 1) + pltpu.roll(tz, 1, 1) * pltpu.roll(block, 1, 1)
+        return F32(0.3) * block + base + gain * (total - term)
+
     if last:
-        at = lax.axis_index("gx") % UNIT
+        place = lax.axis_index("gx") % UNIT
         core = lax.axis_index("gy") & 1
-        out_ref[...] = p_ref[pl.ds(32 * core + 8 * at, 8)]
-        mine = seg[6:8]
         for y in range(2):
-            for owner in range(UNIT):
-                start = 16 * y + 2 * (UNIT - 1 - owner)
-                mine = jnp.where((at == owner) & (core == y), seg[start : start + 2], mine)
-        seg_out[0] = mine
+            for block in range(UNIT):
+
+                @pl.when((place == block) & (core == y))
+                def _(y=y, block=block):
+                    term, _ = spread_block(flux, host, held_ref, y, block)
+                    for x in range(8):
+                        out_ref[x] = updated(y, 8 * block + x, term[8 * x : 8 * x + 8])
+                    start = 16 * y + 2 * (UNIT - 1 - block)
+                    seg_out[0] = seg[start : start + 2]
+
     else:
+        hots = spread_wells(flux, host, held_ref, term_ref)
+        for y in range(2):
+            for x in range(32):
+                p_ref[32 * y + x] = updated(y, x, term_ref[32 * y + x])
         seg_ref[...] = seg
         send_out(p_ref, held_ref, hots, send_ref, face_ref)
 
@@ -359,18 +378,17 @@
     message, edges, grid, wells = shape(96, 128), shape(32, 128), shape(64, 8, 128), shape(32, 128)
     send, face = call(share_kernel, [message, edges], among_chips(small))
     recv = exchanged(send, face)
-    p, gain, wx, wy, seg, well, held, send, face = call(
+    p, coef, wx, wy, seg, well, held, send, face = call(
         first_kernel,
-        [grid, grid, shape(2, 8, 128), edges, wells, shape(4, 32, 128), pltpu.VMEM((8, 8, 128), jnp.int32), message, edges],
-        fields, recv, scratch=[grid],
+        [grid, shape(5, 64, 8, 128), shape(2, 8, 128), edges, wells, shape(4, 32, 128), pltpu.VMEM((8, 8, 128), jnp.int32), message, edges],
+        fields, recv, scratch=[grid], placed=lambda value: value if value is fields else near(value),
     )
     for sweep in range(1, SWEEPS):
         last = sweep == SWEEPS - 1
         recv = exchanged(send, face)
         outs = [result(8, 8, 128), result(1, 2, 128)] if last else [grid, wells, message, edges]
         got = call(
-            sweep_kernel, outs, p, fields, gain, wx, wy, recv, seg, well, held,
-            scratch=[grid, grid] if last else [grid], last=last,
+            sweep_kernel, outs, p, coef, wx, wy, recv, seg, well, held, scratch=[] if last else [grid], last=last,
         )
         p, seg = got[:2]
         if not last:

time: 111 us -> 113 us (1.018)
  local copies, waits for them, and re-layouts: 2.43 us -> 3.7 us
    unnamed x4 -> x6, local copies, waits for them, and re-layouts: 2.43 us -> 3.7 us
where the time goes in v5:
time: 113 us; the launch traced here: 112 us
  blocking collectives  63.3 us (56%)
  starting transfers between devices  28 us (25%)
  Pallas kernels  15.7 us (14%)
  local copies, waits for them, and re-layouts  3.7 us (3%)
    all_gather x6, blocking collectives, exchanged(): lax.all_gather(send, ('gx', 'gy'), axis_index_groups=columns, tiled=True)  41.5 us
    ppermute x6, starting transfers between devices, exchanged(): edge = lax.ppermute(face, 'gy', facing)  23 us
    pallas_call x8, Pallas kernels, call(): pl.pallas_call(lambda *refs: body(*refs, **static), out_shape=outs, in_sp...  15.7 us
    all_gather x6, blocking collectives, exchanged(): return lax.all_gather(both, 'gy', axis_index_groups=mates, tiled=True)  11.8 us
    all_to_all x1, blocking collectives, among_chips(): lax.all_to_all(buffer, ('gx', 'gy'), 0, 0, tiled=True, axis_index_groups=...  9.95 us
    all_to_all x1, starting transfers between devices, among_chips(): lax.all_to_all(buffer, ('gx', 'gy'), 0, 0, tiled=True, axis_index_groups=...  4.98 us
    unnamed x6, local copies, waits for them, and re-layouts  3.7 us
  transfers between devices with their start and end apart: 7, of which 1 were waited for; matrix products, arithmetic and copies ran while one was open for 0% of the time, Pallas kernels for 0%

profile of v5, /device:TPU:25, one launch (start us, length us, event | category | flops | bytes accessed | tf_op | source)
XLA Modules:
  0.0 112.2 jit_solution(6953778108719930113)
XLA Ops:
  0.6 2.1 %shard_map.113 = (f32[8,24,128]{2,1,0:T(8,128)}, f32[8,328,128]{2,1,0:T(8,128)}) custom-call(f32[8,8,128]{2,1,0:T(8,128)} %refs_0_.1, f32[8,8,128]{2,1,0:T(8,128)} %refs_1_.1, f32[8,8,128]{2,1,0:T(8,128)} %refs_2_.1, f32[8,8,128]{2,1,0:T(8,128)} %refs_3_.1, f32[8,8,128]{2,1,0:T(8,128)} %refs_4_.1, s32[4,1,2,128]{3,2,1,0:T(2,128)} %refs_5_.1, ...), custom_call_target="tpu_custom_call" | custom-call | tf_op jit(solution)/shard_map/pallas_call | solution.py:356
  2.7 9.9 %all_to_all.10.refs_0_ = f32[8,24,128]{2,1,0:T(8,128)S(1)} all-to-all(f32[8,24,128]{2,1,0:T(8,128)} %get-tuple-element.32), channel_id=1, replica_groups={{0,1,16,17,32,33,48,49},{2,3,18,19,34,35,50,51},{4,5,20,21,36,37,52,53}..., dimensions={0} | all-to-all | bytes 196608 | tf_op jit(solution)/shard_map/all_to_all | solution.py:371
  12.6 5.0 %all-to-all-start = ((f32[8,328,128]{2,1,0:T(8,128)}), f32[8,328,128]{2,1,0:T(8,128)}, u32[]{:S(2)}, u32[]{:S(2)}) async-start(f32[8,328,128]{2,1,0:T(8,128)} %get-tuple-element.31), calls=%async_computation | async-start | bytes 2686976 | tf_op jit(solution)/shard_map/all_to_all | solution.py:371
  17.6 4.4 %collective-permute-start = (f32[32,128]{1,0:T(8,128)S(1)}, f32[32,128]{1,0:T(8,128)S(1)}, u32[]{:S(2)}, u32[]{:S(2)}) collective-permute-start(f32[32,128]{1,0:T(8,128)S(1)} %get-tuple-element.34), channel_id=1, source_target_pairs={{1,2},{3,4},{5,6},{7,8},{9,10},{11,12},{13,14},{2,1},{4,3},{6,5},{... | collective-permute-start | bytes 49160 | tf_op jit(solution)/shard_map/ppermute | solution.py:365
  22.1 11.3 %all_gather.36 = f32[192,128]{1,0:T(8,128)S(1)} all-gather(f32[96,128]{1,0:T(8,128)S(1)} %get-tuple-element.33), channel_id=1, replica_groups={{0,64},{16,80},{32,96},{48,112},{128,192},{144,208},{160,224},{176,240}..., dimensions={0}, use_global_device_ids=true | all-gather | bytes 147456 | tf_op jit(solution)/shard_map/all_gather | solution.py:366
  33.4 2.0 %all_gather.37.refs_1_ = f32[448,128]{1,0:T(8,128)S(1)} all-gather(f32[224,128]{1,0:T(8,128)S(1)} %pad_maximum_fusion), channel_id=1, replica_groups={{0,1},{2,3},{4,5},{6,7},{8,9},{10,11},{12,13},{14,15},{16,17},{18,19},{..., dimensions={0}, use_global_device_ids=true | all-gather | bytes 344064 | tf_op jit(solution)/shard_map/all_gather | solution.py:368
  36.0 3.5 %shard_map.115 = (f32[64,8,128]{2,1,0:T(8,128)S(1)}, f32[5,64,8,128]{3,2,1,0:T(8,128)S(1)}, f32[2,8,128]{2,1,0:T(8,128)S(1)}, f32[32,128]{1,0:T(8,128)S(1)}, f32...) custom-call(f32[8,328,128]{2,1,0:T(8,128)} %all-to-all-done.refs_0_,, ...), custom_call_target="tpu_custom_call" | custom-call | tf_op jit(solution)/shard_map/pallas_call | solution.py:356
  40.6 5.2 %collective-permute-start.1 = (f32[32,128]{1,0:T(8,128)S(1)}, f32[32,128]{1,0:T(8,128)S(1)}, u32[]{:S(2)}, u32[]{:S(2)}) collective-permute-start(f32[32,128]{1,0:T(8,128)S(1)} %get-tuple-element.40), channel_id=1, source_target_pairs={{1,2},{3,4},{5,6},{7,8},{9,10},{11,12},{13,14},{2,1},{4,3},{6,5},{... | collective-permute-start | bytes 49160 | tf_op jit(solution)/shard_map/ppermute | solution.py:365
  45.7 10.9 %all_gather.38 = f32[192,128]{1,0:T(8,128)S(1)} all-gather(f32[96,128]{1,0:T(8,128)S(1)} %get-tuple-element.39), channel_id=1, replica_groups={{0,64},{16,80},{32,96},{48,112},{128,192},{144,208},{160,224},{176,240}..., dimensions={0}, use_global_device_ids=true | all-gather | bytes 147456 | tf_op jit(solution)/shard_map/all_gather | solution.py:366
  59.9 2.3 %shard_map.116 = (f32[64,8,128]{2,1,0:T(8,128)S(1)}, f32[32,128]{1,0:T(8,128)S(1)}, f32[96,128]{1,0:T(8,128)S(1)}, f32[32,128]{1,0:T(8,128)S(1)}) custom-call(f32[64,8,128]{2,1,0:T(8,128)S(1)} %get-tuple-element.35.refs_0_, f32[5,64,8,128]{3,2,1,0:T(8,128)S(1)} %copy-done.1, f32[2,8,128]{2,1,0:T(8,128)S(1)} %get-tuple-element.37.refs_2_, ...), custom_call_target="tpu_custom_call" | custom-call | tf_op jit(solution)/shard_map/pallas_call | solution.py:356
  62.2 2.3 %collective-permute-start.2 = (f32[32,128]{1,0:T(8,128)S(1)}, f32[32,128]{1,0:T(8,128)S(1)}, u32[]{:S(2)}, u32[]{:S(2)}) collective-permute-start(f32[32,128]{1,0:T(8,128)S(1)} %get-tuple-element.46), channel_id=1, source_target_pairs={{1,2},{3,4},{5,6},{7,8},{9,10},{11,12},{13,14},{2,1},{4,3},{6,5},{... | collective-permute-start | bytes 49160 | tf_op jit(solution)/shard_map/ppermute | solution.py:365
  64.6 4.8 %all_gather.40 = f32[192,128]{1,0:T(8,128)S(1)} all-gather(f32[96,128]{1,0:T(8,128)S(1)} %get-tuple-element.45), channel_id=1, replica_groups={{0,64},{16,80},{32,96},{48,112},{128,192},{144,208},{160,224},{176,240}..., dimensions={0}, use_global_device_ids=true | all-gather | bytes 147456 | tf_op jit(solution)/shard_map/all_gather | solution.py:366
  69.4 2.0 %all_gather.41.refs_4_ = f32[448,128]{1,0:T(8,128)S(1)} all-gather(f32[224,128]{1,0:T(8,128)S(1)} %pad_maximum_fusion.2), channel_id=1, replica_groups={{0,1},{2,3},{4,5},{6,7},{8,9},{10,11},{12,13},{14,15},{16,17},{18,19},{..., dimensions={0}, use_global_device_ids=true | all-gather | bytes 344064 | tf_op jit(solution)/shard_map/all_gather | solution.py:368
  72.7 2.3 %shard_map.117 = (f32[64,8,128]{2,1,0:T(8,128)S(1)}, f32[32,128]{1,0:T(8,128)S(1)}, f32[96,128]{1,0:T(8,128)S(1)}, f32[32,128]{1,0:T(8,128)S(1)}) custom-call(f32[64,8,128]{2,1,0:T(8,128)S(1)} %get-tuple-element.44.refs_0_, f32[5,64,8,128]{3,2,1,0:T(8,128)S(1)} %copy-done.2, f32[2,8,128]{2,1,0:T(8,128)S(1)} %get-tuple-element.37.refs_2_, ...), custom_call_target="tpu_custom_call" | custom-call | tf_op jit(solution)/shard_map/pallas_call | solution.py:356
  75.0 4.4 %collective-permute-start.3 = (f32[32,128]{1,0:T(8,128)S(1)}, f32[32,128]{1,0:T(8,128)S(1)}, u32[]{:S(2)}, u32[]{:S(2)}) collective-permute-start(f32[32,128]{1,0:T(8,128)S(1)} %get-tuple-element.50), channel_id=1, source_target_pairs={{1,2},{3,4},{5,6},{7,8},{9,10},{11,12},{13,14},{2,1},{4,3},{6,5},{... | collective-permute-start | bytes 49160 | tf_op jit(solution)/shard_map/ppermute | solution.py:365
  79.4 4.8 %all_gather.42 = f32[192,128]{1,0:T(8,128)S(1)} all-gather(f32[96,128]{1,0:T(8,128)S(1)} %get-tuple-element.49), channel_id=1, replica_groups={{0,64},{16,80},{32,96},{48,112},{128,192},{144,208},{160,224},{176,240}..., dimensions={0}, use_global_device_ids=true | all-gather | bytes 147456 | tf_op jit(solution)/shard_map/all_gather | solution.py:366
  84.2 2.0 %all_gather.43.refs_4_ = f32[448,128]{1,0:T(8,128)S(1)} all-gather(f32[224,128]{1,0:T(8,128)S(1)} %pad_maximum_fusion.3), channel_id=1, replica_groups={{0,1},{2,3},{4,5},{6,7},{8,9},{10,11},{12,13},{14,15},{16,17},{18,19},{..., dimensions={0}, use_global_device_ids=true | all-gather | bytes 344064 | tf_op jit(solution)/shard_map/all_gather | solution.py:368
  86.2 2.3 %shard_map.118 = (f32[64,8,128]{2,1,0:T(8,128)S(1)}, f32[32,128]{1,0:T(8,128)S(1)}, f32[96,128]{1,0:T(8,128)S(1)}, f32[32,128]{1,0:T(8,128)S(1)}) custom-call(f32[64,8,128]{2,1,0:T(8,128)S(1)} %get-tuple-element.48.refs_0_, f32[5,64,8,128]{3,2,1,0:T(8,128)S(1)} %copy-done.2, f32[2,8,128]{2,1,0:T(8,128)S(1)} %get-tuple-element.37.refs_2_, ...), custom_call_target="tpu_custom_call" | custom-call | tf_op jit(solution)/shard_map/pallas_call | solution.py:356
  88.5 2.3 %collective-permute-start.4 = (f32[32,128]{1,0:T(8,128)S(1)}, f32[32,128]{1,0:T(8,128)S(1)}, u32[]{:S(2)}, u32[]{:S(2)}) collective-permute-start(f32[32,128]{1,0:T(8,128)S(1)} %get-tuple-element.54), channel_id=1, source_target_pairs={{1,2},{3,4},{5,6},{7,8},{9,10},{11,12},{13,14},{2,1},{4,3},{6,5},{... | collective-permute-start | bytes 49160 | tf_op jit(solution)/shard_map/ppermute | solution.py:365
  90.8 4.8 %all_gather.44 = f32[192,128]{1,0:T(8,128)S(1)} all-gather(f32[96,128]{1,0:T(8,128)S(1)} %get-tuple-element.53), channel_id=1, replica_groups={{0,64},{16,80},{32,96},{48,112},{128,192},{144,208},{160,224},{176,240}..., dimensions={0}, use_global_device_ids=true | all-gather | bytes 147456 | tf_op jit(solution)/shard_map/all_gather | solution.py:366
  95.6 2.0 %all_gather.45.refs_4_ = f32[448,128]{1,0:T(8,128)S(1)} all-gather(f32[224,128]{1,0:T(8,128)S(1)} %pad_maximum_fusion.4), channel_id=1, replica_groups={{0,1},{2,3},{4,5},{6,7},{8,9},{10,11},{12,13},{14,15},{16,17},{18,19},{..., dimensions={0}, use_global_device_ids=true | all-gather | bytes 344064 | tf_op jit(solution)/shard_map/all_gather | solution.py:368
  97.6 2.3 %shard_map.119 = (f32[64,8,128]{2,1,0:T(8,128)S(1)}, f32[32,128]{1,0:T(8,128)S(1)}, f32[96,128]{1,0:T(8,128)S(1)}, f32[32,128]{1,0:T(8,128)S(1)}) custom-call(f32[64,8,128]{2,1,0:T(8,128)S(1)} %get-tuple-element.52.refs_0_, f32[5,64,8,128]{3,2,1,0:T(8,128)S(1)} %copy-done.2, f32[2,8,128]{2,1,0:T(8,128)S(1)} %get-tuple-element.37.refs_2_, ...), custom_call_target="tpu_custom_call" | custom-call | tf_op jit(solution)/shard_map/pallas_call | solution.py:356
  99.9 4.4 %collective-permute-start.5 = (f32[32,128]{1,0:T(8,128)S(1)}, f32[32,128]{1,0:T(8,128)S(1)}, u32[]{:S(2)}, u32[]{:S(2)}) collective-permute-start(f32[32,128]{1,0:T(8,128)S(1)} %get-tuple-element.58), channel_id=1, source_target_pairs={{1,2},{3,4},{5,6},{7,8},{9,10},{11,12},{13,14},{2,1},{4,3},{6,5},{... | collective-permute-start | bytes 49160 | tf_op jit(solution)/shard_map/ppermute | solution.py:365
  104.3 4.8 %all_gather.46 = f32[192,128]{1,0:T(8,128)S(1)} all-gather(f32[96,128]{1,0:T(8,128)S(1)} %get-tuple-element.57), channel_id=1, replica_groups={{0,64},{16,80},{32,96},{48,112},{128,192},{144,208},{160,224},{176,240}..., dimensions={0}, use_global_device_ids=true | all-gather | bytes 147456 | tf_op jit(solution)/shard_map/all_gather | solution.py:366
  (23 shorter events, 9.4 us)
Async XLA Ops:
  12.6 23.4 %all-to-all-start = ((f32[8,328,128]{2,1,0:T(8,128)}), f32[8,328,128]{2,1,0:T(8,128)}, u32[]{:S(2)}, u32[]{:S(2)}) async-start(f32[8,328,128]{2,1,0:T(8,128)} %get-tuple-element.31), calls=%async_computation | async-start | bytes 2686976 | tf_op jit(solution)/shard_map/all_to_all | solution.py:371
  17.6 15.7 %collective-permute-start = (f32[32,128]{1,0:T(8,128)S(1)}, f32[32,128]{1,0:T(8,128)S(1)}, u32[]{:S(2)}, u32[]{:S(2)}) collective-permute-start(f32[32,128]{1,0:T(8,128)S(1)} %get-tuple-element.34), channel_id=1, source_target_pairs={{1,2},{3,4},{5,6},{7,8},{9,10},{11,12},{13,14},{2,1},{4,3},{6,5},{... | collective-permute-start | bytes 49160 | tf_op jit(solution)/shard_map/ppermute | solution.py:365
  39.5 1.1 copy-start
  40.6 16.1 %collective-permute-start.1 = (f32[32,128]{1,0:T(8,128)S(1)}, f32[32,128]{1,0:T(8,128)S(1)}, u32[]{:S(2)}, u32[]{:S(2)}) collective-permute-start(f32[32,128]{1,0:T(8,128)S(1)} %get-tuple-element.40), channel_id=1, source_target_pairs={{1,2},{3,4},{5,6},{7,8},{9,10},{11,12},{13,14},{2,1},{4,3},{6,5},{... | collective-permute-start | bytes 49160 | tf_op jit(solution)/shard_map/ppermute | solution.py:365
  58.6 1.3 %copy-start.1 = (f32[5,64,8,128]{3,2,1,0:T(8,128)S(1)}, f32[5,64,8,128]{3,2,1,0:T(8,128)}, u32[]{:S(2)}) copy-start(f32[5,64,8,128]{3,2,1,0:T(8,128)} %copy-done) | copy-start | bytes 3932164
  62.2 7.2 %collective-permute-start.2 = (f32[32,128]{1,0:T(8,128)S(1)}, f32[32,128]{1,0:T(8,128)S(1)}, u32[]{:S(2)}, u32[]{:S(2)}) collective-permute-start(f32[32,128]{1,0:T(8,128)S(1)} %get-tuple-element.46), channel_id=1, source_target_pairs={{1,2},{3,4},{5,6},{7,8},{9,10},{11,12},{13,14},{2,1},{4,3},{6,5},{... | collective-permute-start | bytes 49160 | tf_op jit(solution)/shard_map/ppermute | solution.py:365
  71.4 1.3 %copy-start.2 = (f32[5,64,8,128]{3,2,1,0:T(8,128)S(1)}, f32[5,64,8,128]{3,2,1,0:T(8,128)}, u32[]{:S(2)}) copy-start(f32[5,64,8,128]{3,2,1,0:T(8,128)} %copy-done) | copy-start | bytes 3932164
  75.0 9.2 %collective-permute-start.3 = (f32[32,128]{1,0:T(8,128)S(1)}, f32[32,128]{1,0:T(8,128)S(1)}, u32[]{:S(2)}, u32[]{:S(2)}) collective-permute-start(f32[32,128]{1,0:T(8,128)S(1)} %get-tuple-element.50), channel_id=1, source_target_pairs={{1,2},{3,4},{5,6},{7,8},{9,10},{11,12},{13,14},{2,1},{4,3},{6,5},{... | collective-permute-start | bytes 49160 | tf_op jit(solution)/shard_map/ppermute | solution.py:365
  88.5 7.2 %collective-permute-start.4 = (f32[32,128]{1,0:T(8,128)S(1)}, f32[32,128]{1,0:T(8,128)S(1)}, u32[]{:S(2)}, u32[]{:S(2)}) collective-permute-start(f32[32,128]{1,0:T(8,128)S(1)} %get-tuple-element.54), channel_id=1, source_target_pairs={{1,2},{3,4},{5,6},{7,8},{9,10},{11,12},{13,14},{2,1},{4,3},{6,5},{... | collective-permute-start | bytes 49160 | tf_op jit(solution)/shard_map/ppermute | solution.py:365
  99.9 9.2 %collective-permute-start.5 = (f32[32,128]{1,0:T(8,128)S(1)}, f32[32,128]{1,0:T(8,128)S(1)}, u32[]{:S(2)}, u32[]{:S(2)}) collective-permute-start(f32[32,128]{1,0:T(8,128)S(1)} %get-tuple-element.58), channel_id=1, source_target_pairs={{1,2},{3,4},{5,6},{7,8},{9,10},{11,12},{13,14},{2,1},{4,3},{6,5},{... | collective-permute-start | bytes 49160 | tf_op jit(solution)/shard_map/ppermute | solution.py:365

commit v6 on v5

--- a/solution.py
+++ b/solution.py
@@ -192,7 +192,7 @@
 
 
 def first_kernel(
-    fields_ref, recv_ref, p_ref, coef_ref, wx_ref, wy_ref, seg_ref, well_ref, held_ref, send_ref, face_ref, term_ref
+    fields_ref, recv_ref, p_ref, tx_out, ty_out, tz_out, gain_out, base_out, wx_ref, wy_ref, seg_ref, well_ref, held_ref, send_ref, face_ref, term_ref
 ):
     unit, here, after, before = places()
     own = iota((16, 128), 0) // 2
@@ -233,13 +233,14 @@
             gain = F32(0.7) / (field(fields_ref, 1, y, x) + tx + wx + ty + wy + tz + wz)
             base = gain * field(fields_ref, 0, y, x)
             at = 32 * y + x
-            for which, value in enumerate((tx, ty, inner, gain, base)):
-                coef_ref[which, at] = value
+            tx_out[at], ty_out[at], tz_out[at], gain_out[at], base_out[at] = tx, ty, inner, gain, base
             p_ref[at] = base - gain * term_ref[at]
     send_out(p_ref, held_ref, hots, send_ref, face_ref)
 
 
-def sweep_kernel(p_in, coef_ref, wx_ref, wy_ref, recv_ref, seg_in, well_ref, held_ref, *rest, last):
+def sweep_kernel(
+    p_in, tx_ref, ty_ref, tz_ref, gain_ref, base_ref, wx_ref, wy_ref, recv_ref, seg_in, well_ref, held_ref, *rest, last
+):
     if last:
         out_ref, seg_out = rest
     else:
@@ -281,12 +282,12 @@
         else:
             west = rows_at(recv_ref, before + PARTS * y + 40)
             west = jnp.where(unit == 0, F32(0.0), west)
-        tx, ty, tz, gain, base = (coef_ref[which, at] for which in range(5))
-        edge = coef_ref[1, x, 7:8, :] if y else wy_ref[x : x + 1, :]
-        total = tx * east + (coef_ref[0, at - 1] if x else wx_ref[y]) * west
+        tx, ty, tz = tx_ref[at], ty_ref[at], tz_ref[at]
+        edge = ty_ref[x, 7:8, :] if y else wy_ref[x : x + 1, :]
+        total = tx * east + (tx_ref[at - 1] if x else wx_ref[y]) * west
         total = total + ty * y_moved(block, north, 1) + y_moved(ty, edge, -1) * y_moved(block, south, -1)
         total = total + tz * pltpu.roll(block, 127, 1) + pltpu.roll(tz, 1, 1) * pltpu.roll(block, 1, 1)
-        return F32(0.3) * block + base + gain * (total - term)
+        return F32(0.3) * block + base_ref[at] + gain_ref[at] * (total - term)
 
     if last:
         place = lax.axis_index("gx") % UNIT
@@ -378,9 +379,9 @@
     message, edges, grid, wells = shape(96, 128), shape(32, 128), shape(64, 8, 128), shape(32, 128)
     send, face = call(share_kernel, [message, edges], among_chips(small))
     recv = exchanged(send, face)
-    p, coef, wx, wy, seg, well, held, send, face = call(
+    p, *kept, seg, well, held, send, face = call(
         first_kernel,
-        [grid, shape(5, 64, 8, 128), shape(2, 8, 128), edges, wells, shape(4, 32, 128), pltpu.VMEM((8, 8, 128), jnp.int32), message, edges],
+        [grid] * 6 + [shape(2, 8, 128), edges, wells, shape(4, 32, 128), pltpu.VMEM((8, 8, 128), jnp.int32), message, edges],
         fields, recv, scratch=[grid], placed=lambda value: value if value is fields else near(value),
     )
     for sweep in range(1, SWEEPS):
@@ -388,7 +389,7 @@
         recv = exchanged(send, face)
         outs = [result(8, 8, 128), result(1, 2, 128)] if last else [grid, wells, message, edges]
         got = call(
-            sweep_kernel, outs, p, coef, wx, wy, recv, seg, well, held, scratch=[] if last else [grid], last=last,
+            sweep_kernel, outs, p, *kept, recv, seg, well, held, scratch=[] if last else [grid], last=last,
         )
         p, seg = got[:2]
         if not last:

time: 113 us -> 109 us (0.965)
  local copies, waits for them, and re-layouts: 3.7 us -> 0 us
    unnamed x6 -> x0, local copies, waits for them, and re-layouts: 3.7 us -> none
where the time goes in v6:
time: 109 us; the launch traced here: 108 us
  blocking collectives  63.3 us (58%)
  starting transfers between devices  28 us (26%)
  Pallas kernels  15.7 us (14%)
    all_gather x6, blocking collectives, exchanged(): lax.all_gather(send, ('gx', 'gy'), axis_index_groups=columns, tiled=True)  41.5 us
    ppermute x6, starting transfers between devices, exchanged(): edge = lax.ppermute(face, 'gy', facing)  23 us
    pallas_call x8, Pallas kernels, call(): pl.pallas_call(lambda *refs: body(*refs, **static), out_shape=outs, in_sp...  15.7 us
    all_gather x6, blocking collectives, exchanged(): return lax.all_gather(both, 'gy', axis_index_groups=mates, tiled=True)  11.8 us
    all_to_all x1, blocking collectives, among_chips(): lax.all_to_all(buffer, ('gx', 'gy'), 0, 0, tiled=True, axis_index_groups=...  9.95 us
    all_to_all x1, starting transfers between devices, among_chips(): lax.all_to_all(buffer, ('gx', 'gy'), 0, 0, tiled=True, axis_index_groups=...  4.97 us
  transfers between devices with their start and end apart: 7, of which 1 were waited for; matrix products, arithmetic and copies ran while one was open for 0% of the time, Pallas kernels for 0%

profile of v6, /device:TPU:25, one launch (start us, length us, event | category | flops | bytes accessed | tf_op | source)
XLA Modules:
  0.0 108.5 jit_solution(10617737956140493493)
XLA Ops:
  0.6 2.0 %shard_map.113 = (f32[8,24,128]{2,1,0:T(8,128)}, f32[8,328,128]{2,1,0:T(8,128)}) custom-call(f32[8,8,128]{2,1,0:T(8,128)} %refs_0_.1, f32[8,8,128]{2,1,0:T(8,128)} %refs_1_.1, f32[8,8,128]{2,1,0:T(8,128)} %refs_2_.1, f32[8,8,128]{2,1,0:T(8,128)} %refs_3_.1, f32[8,8,128]{2,1,0:T(8,128)} %refs_4_.1, s32[4,1,2,128]{3,2,1,0:T(2,128)} %refs_5_.1, ...), custom_call_target="tpu_custom_call" | custom-call | tf_op jit(solution)/shard_map/pallas_call | solution.py:357
  2.7 9.9 %all_to_all.10.refs_0_ = f32[8,24,128]{2,1,0:T(8,128)S(1)} all-to-all(f32[8,24,128]{2,1,0:T(8,128)} %get-tuple-element.36), channel_id=1, replica_groups={{0,1,16,17,32,33,48,49},{2,3,18,19,34,35,50,51},{4,5,20,21,36,37,52,53}..., dimensions={0} | all-to-all | bytes 196608 | tf_op jit(solution)/shard_map/all_to_all | solution.py:372
  12.6 5.0 %all-to-all-start = ((f32[8,328,128]{2,1,0:T(8,128)}), f32[8,328,128]{2,1,0:T(8,128)}, u32[]{:S(2)}, u32[]{:S(2)}) async-start(f32[8,328,128]{2,1,0:T(8,128)} %get-tuple-element.35), calls=%async_computation | async-start | bytes 2686976 | tf_op jit(solution)/shard_map/all_to_all | solution.py:372
  17.6 4.4 %collective-permute-start = (f32[32,128]{1,0:T(8,128)S(1)}, f32[32,128]{1,0:T(8,128)S(1)}, u32[]{:S(2)}, u32[]{:S(2)}) collective-permute-start(f32[32,128]{1,0:T(8,128)S(1)} %get-tuple-element.38), channel_id=1, source_target_pairs={{1,2},{3,4},{5,6},{7,8},{9,10},{11,12},{13,14},{2,1},{4,3},{6,5},{... | collective-permute-start | bytes 49160 | tf_op jit(solution)/shard_map/ppermute | solution.py:366
  22.0 11.3 %all_gather.36 = f32[192,128]{1,0:T(8,128)S(1)} all-gather(f32[96,128]{1,0:T(8,128)S(1)} %get-tuple-element.37), channel_id=1, replica_groups={{0,64},{16,80},{32,96},{48,112},{128,192},{144,208},{160,224},{176,240}..., dimensions={0}, use_global_device_ids=true | all-gather | bytes 147456 | tf_op jit(solution)/shard_map/all_gather | solution.py:367
  33.3 2.0 %all_gather.37.refs_1_ = f32[448,128]{1,0:T(8,128)S(1)} all-gather(f32[224,128]{1,0:T(8,128)S(1)} %pad_maximum_fusion), channel_id=1, replica_groups={{0,1},{2,3},{4,5},{6,7},{8,9},{10,11},{12,13},{14,15},{16,17},{18,19},{..., dimensions={0}, use_global_device_ids=true | all-gather | bytes 344064 | tf_op jit(solution)/shard_map/all_gather | solution.py:369
  36.0 3.5 %shard_map.115 = (f32[64,8,128]{2,1,0:T(8,128)S(1)}, f32[64,8,128]{2,1,0:T(8,128)S(1)}, f32[64,8,128]{2,1,0:T(8,128)S(1)}, f32[64,8,128]{2,1,0:T(8,128)S(1)}, f3...) custom-call(f32[8,328,128]{2,1,0:T(8,128)} %all-to-all-done.refs_0_,, ...), custom_call_target="tpu_custom_call" | custom-call | tf_op jit(solution)/shard_map/pallas_call | solution.py:357
  39.4 5.2 %collective-permute-start.1 = (f32[32,128]{1,0:T(8,128)S(1)}, f32[32,128]{1,0:T(8,128)S(1)}, u32[]{:S(2)}, u32[]{:S(2)}) collective-permute-start(f32[32,128]{1,0:T(8,128)S(1)} %get-tuple-element.48), channel_id=1, source_target_pairs={{1,2},{3,4},{5,6},{7,8},{9,10},{11,12},{13,14},{2,1},{4,3},{6,5},{... | collective-permute-start | bytes 49160 | tf_op jit(solution)/shard_map/ppermute | solution.py:366
  44.6 10.9 %all_gather.38 = f32[192,128]{1,0:T(8,128)S(1)} all-gather(f32[96,128]{1,0:T(8,128)S(1)} %get-tuple-element.47), channel_id=1, replica_groups={{0,64},{16,80},{32,96},{48,112},{128,192},{144,208},{160,224},{176,240}..., dimensions={0}, use_global_device_ids=true | all-gather | bytes 147456 | tf_op jit(solution)/shard_map/all_gather | solution.py:367
  55.5 2.0 %all_gather.39.refs_8_ = f32[448,128]{1,0:T(8,128)S(1)} all-gather(f32[224,128]{1,0:T(8,128)S(1)} %pad_maximum_fusion.1), channel_id=1, replica_groups={{0,1},{2,3},{4,5},{6,7},{8,9},{10,11},{12,13},{14,15},{16,17},{18,19},{..., dimensions={0}, use_global_device_ids=true | all-gather | bytes 344064 | tf_op jit(solution)/shard_map/all_gather | solution.py:369
  57.5 2.3 %shard_map.116 = (f32[64,8,128]{2,1,0:T(8,128)S(1)}, f32[32,128]{1,0:T(8,128)S(1)}, f32[96,128]{1,0:T(8,128)S(1)}, f32[32,128]{1,0:T(8,128)S(1)}) custom-call(f32[64,8,128]{2,1,0:T(8,128)S(1)} %get-tuple-element.39.refs_0_, f32[64,8,128]{2,1,0:T(8,128)S(1)} %get-tuple-element.40.refs_1_, f32[64,8,128]{2,1,0:T(8,128)S(1)} %get-tuple-element.41.refs_2_, ...), custom_call_target="tpu_custom_call" | custom-call | tf_op jit(solution)/shard_map/pallas_call | solution.py:357
  59.8 2.3 %collective-permute-start.2 = (f32[32,128]{1,0:T(8,128)S(1)}, f32[32,128]{1,0:T(8,128)S(1)}, u32[]{:S(2)}, u32[]{:S(2)}) collective-permute-start(f32[32,128]{1,0:T(8,128)S(1)} %get-tuple-element.54), channel_id=1, source_target_pairs={{1,2},{3,4},{5,6},{7,8},{9,10},{11,12},{13,14},{2,1},{4,3},{6,5},{... | collective-permute-start | bytes 49160 | tf_op jit(solution)/shard_map/ppermute | solution.py:366
  62.1 4.8 %all_gather.40 = f32[192,128]{1,0:T(8,128)S(1)} all-gather(f32[96,128]{1,0:T(8,128)S(1)} %get-tuple-element.53), channel_id=1, replica_groups={{0,64},{16,80},{32,96},{48,112},{128,192},{144,208},{160,224},{176,240}..., dimensions={0}, use_global_device_ids=true | all-gather | bytes 147456 | tf_op jit(solution)/shard_map/all_gather | solution.py:367
  67.0 2.0 %all_gather.41.refs_8_ = f32[448,128]{1,0:T(8,128)S(1)} all-gather(f32[224,128]{1,0:T(8,128)S(1)} %pad_maximum_fusion.2), channel_id=1, replica_groups={{0,1},{2,3},{4,5},{6,7},{8,9},{10,11},{12,13},{14,15},{16,17},{18,19},{..., dimensions={0}, use_global_device_ids=true | all-gather | bytes 344064 | tf_op jit(solution)/shard_map/all_gather | solution.py:369
  69.0 2.3 %shard_map.117 = (f32[64,8,128]{2,1,0:T(8,128)S(1)}, f32[32,128]{1,0:T(8,128)S(1)}, f32[96,128]{1,0:T(8,128)S(1)}, f32[32,128]{1,0:T(8,128)S(1)}) custom-call(f32[64,8,128]{2,1,0:T(8,128)S(1)} %get-tuple-element.52.refs_0_, f32[64,8,128]{2,1,0:T(8,128)S(1)} %get-tuple-element.40.refs_1_, f32[64,8,128]{2,1,0:T(8,128)S(1)} %get-tuple-element.41.refs_2_, ...), custom_call_target="tpu_custom_call" | custom-call | tf_op jit(solution)/shard_map/pallas_call | solution.py:357
  71.3 4.4 %collective-permute-start.3 = (f32[32,128]{1,0:T(8,128)S(1)}, f32[32,128]{1,0:T(8,128)S(1)}, u32[]{:S(2)}, u32[]{:S(2)}) collective-permute-start(f32[32,128]{1,0:T(8,128)S(1)} %get-tuple-element.58), channel_id=1, source_target_pairs={{1,2},{3,4},{5,6},{7,8},{9,10},{11,12},{13,14},{2,1},{4,3},{6,5},{... | collective-permute-start | bytes 49160 | tf_op jit(solution)/shard_map/ppermute | solution.py:366
  75.6 4.8 %all_gather.42 = f32[192,128]{1,0:T(8,128)S(1)} all-gather(f32[96,128]{1,0:T(8,128)S(1)} %get-tuple-element.57), channel_id=1, replica_groups={{0,64},{16,80},{32,96},{48,112},{128,192},{144,208},{160,224},{176,240}..., dimensions={0}, use_global_device_ids=true | all-gather | bytes 147456 | tf_op jit(solution)/shard_map/all_gather | solution.py:367
  80.5 2.0 %all_gather.43.refs_8_ = f32[448,128]{1,0:T(8,128)S(1)} all-gather(f32[224,128]{1,0:T(8,128)S(1)} %pad_maximum_fusion.3), channel_id=1, replica_groups={{0,1},{2,3},{4,5},{6,7},{8,9},{10,11},{12,13},{14,15},{16,17},{18,19},{..., dimensions={0}, use_global_device_ids=true | all-gather | bytes 344064 | tf_op jit(solution)/shard_map/all_gather | solution.py:369
  82.5 2.3 %shard_map.118 = (f32[64,8,128]{2,1,0:T(8,128)S(1)}, f32[32,128]{1,0:T(8,128)S(1)}, f32[96,128]{1,0:T(8,128)S(1)}, f32[32,128]{1,0:T(8,128)S(1)}) custom-call(f32[64,8,128]{2,1,0:T(8,128)S(1)} %get-tuple-element.56.refs_0_, f32[64,8,128]{2,1,0:T(8,128)S(1)} %get-tuple-element.40.refs_1_, f32[64,8,128]{2,1,0:T(8,128)S(1)} %get-tuple-element.41.refs_2_, ...), custom_call_target="tpu_custom_call" | custom-call | tf_op jit(solution)/shard_map/pallas_call | solution.py:357
  84.8 2.3 %collective-permute-start.4 = (f32[32,128]{1,0:T(8,128)S(1)}, f32[32,128]{1,0:T(8,128)S(1)}, u32[]{:S(2)}, u32[]{:S(2)}) collective-permute-start(f32[32,128]{1,0:T(8,128)S(1)} %get-tuple-element.62), channel_id=1, source_target_pairs={{1,2},{3,4},{5,6},{7,8},{9,10},{11,12},{13,14},{2,1},{4,3},{6,5},{... | collective-permute-start | bytes 49160 | tf_op jit(solution)/shard_map/ppermute | solution.py:366
  87.1 4.8 %all_gather.44 = f32[192,128]{1,0:T(8,128)S(1)} all-gather(f32[96,128]{1,0:T(8,128)S(1)} %get-tuple-element.61), channel_id=1, replica_groups={{0,64},{16,80},{32,96},{48,112},{128,192},{144,208},{160,224},{176,240}..., dimensions={0}, use_global_device_ids=true | all-gather | bytes 147456 | tf_op jit(solution)/shard_map/all_gather | solution.py:367
  93.9 2.3 %shard_map.119 = (f32[64,8,128]{2,1,0:T(8,128)S(1)}, f32[32,128]{1,0:T(8,128)S(1)}, f32[96,128]{1,0:T(8,128)S(1)}, f32[32,128]{1,0:T(8,128)S(1)}) custom-call(f32[64,8,128]{2,1,0:T(8,128)S(1)} %get-tuple-element.60.refs_0_, f32[64,8,128]{2,1,0:T(8,128)S(1)} %get-tuple-element.40.refs_1_, f32[64,8,128]{2,1,0:T(8,128)S(1)} %get-tuple-element.41.refs_2_, ...), custom_call_target="tpu_custom_call" | custom-call | tf_op jit(solution)/shard_map/pallas_call | solution.py:357
  96.2 4.4 %collective-permute-start.5 = (f32[32,128]{1,0:T(8,128)S(1)}, f32[32,128]{1,0:T(8,128)S(1)}, u32[]{:S(2)}, u32[]{:S(2)}) collective-permute-start(f32[32,128]{1,0:T(8,128)S(1)} %get-tuple-element.66), channel_id=1, source_target_pairs={{1,2},{3,4},{5,6},{7,8},{9,10},{11,12},{13,14},{2,1},{4,3},{6,5},{... | collective-permute-start | bytes 49160 | tf_op jit(solution)/shard_map/ppermute | solution.py:366
  100.6 4.8 %all_gather.46 = f32[192,128]{1,0:T(8,128)S(1)} all-gather(f32[96,128]{1,0:T(8,128)S(1)} %get-tuple-element.65), channel_id=1, replica_groups={{0,64},{16,80},{32,96},{48,112},{128,192},{144,208},{160,224},{176,240}..., dimensions={0}, use_global_device_ids=true | all-gather | bytes 147456 | tf_op jit(solution)/shard_map/all_gather | solution.py:367
  (17 shorter events, 5.7 us)
Async XLA Ops:
  12.6 23.3 %all-to-all-start = ((f32[8,328,128]{2,1,0:T(8,128)}), f32[8,328,128]{2,1,0:T(8,128)}, u32[]{:S(2)}, u32[]{:S(2)}) async-start(f32[8,328,128]{2,1,0:T(8,128)} %get-tuple-element.35), calls=%async_computation | async-start | bytes 2686976 | tf_op jit(solution)/shard_map/all_to_all | solution.py:372
  17.6 15.7 %collective-permute-start = (f32[32,128]{1,0:T(8,128)S(1)}, f32[32,128]{1,0:T(8,128)S(1)}, u32[]{:S(2)}, u32[]{:S(2)}) collective-permute-start(f32[32,128]{1,0:T(8,128)S(1)} %get-tuple-element.38), channel_id=1, source_target_pairs={{1,2},{3,4},{5,6},{7,8},{9,10},{11,12},{13,14},{2,1},{4,3},{6,5},{... | collective-permute-start | bytes 49160 | tf_op jit(solution)/shard_map/ppermute | solution.py:366
  39.4 16.1 %collective-permute-start.1 = (f32[32,128]{1,0:T(8,128)S(1)}, f32[32,128]{1,0:T(8,128)S(1)}, u32[]{:S(2)}, u32[]{:S(2)}) collective-permute-start(f32[32,128]{1,0:T(8,128)S(1)} %get-tuple-element.48), channel_id=1, source_target_pairs={{1,2},{3,4},{5,6},{7,8},{9,10},{11,12},{13,14},{2,1},{4,3},{6,5},{... | collective-permute-start | bytes 49160 | tf_op jit(solution)/shard_map/ppermute | solution.py:366
  59.8 7.2 %collective-permute-start.2 = (f32[32,128]{1,0:T(8,128)S(1)}, f32[32,128]{1,0:T(8,128)S(1)}, u32[]{:S(2)}, u32[]{:S(2)}) collective-permute-start(f32[32,128]{1,0:T(8,128)S(1)} %get-tuple-element.54), channel_id=1, source_target_pairs={{1,2},{3,4},{5,6},{7,8},{9,10},{11,12},{13,14},{2,1},{4,3},{6,5},{... | collective-permute-start | bytes 49160 | tf_op jit(solution)/shard_map/ppermute | solution.py:366
  71.3 9.2 %collective-permute-start.3 = (f32[32,128]{1,0:T(8,128)S(1)}, f32[32,128]{1,0:T(8,128)S(1)}, u32[]{:S(2)}, u32[]{:S(2)}) collective-permute-start(f32[32,128]{1,0:T(8,128)S(1)} %get-tuple-element.58), channel_id=1, source_target_pairs={{1,2},{3,4},{5,6},{7,8},{9,10},{11,12},{13,14},{2,1},{4,3},{6,5},{... | collective-permute-start | bytes 49160 | tf_op jit(solution)/shard_map/ppermute | solution.py:366
  84.8 7.2 %collective-permute-start.4 = (f32[32,128]{1,0:T(8,128)S(1)}, f32[32,128]{1,0:T(8,128)S(1)}, u32[]{:S(2)}, u32[]{:S(2)}) collective-permute-start(f32[32,128]{1,0:T(8,128)S(1)} %get-tuple-element.62), channel_id=1, source_target_pairs={{1,2},{3,4},{5,6},{7,8},{9,10},{11,12},{13,14},{2,1},{4,3},{6,5},{... | collective-permute-start | bytes 49160 | tf_op jit(solution)/shard_map/ppermute | solution.py:366
  96.2 9.2 %collective-permute-start.5 = (f32[32,128]{1,0:T(8,128)S(1)}, f32[32,128]{1,0:T(8,128)S(1)}, u32[]{:S(2)}, u32[]{:S(2)}) collective-permute-start(f32[32,128]{1,0:T(8,128)S(1)} %get-tuple-element.66), channel_id=1, source_target_pairs={{1,2},{3,4},{5,6},{7,8},{9,10},{11,12},{13,14},{2,1},{4,3},{6,5},{... | collective-permute-start | bytes 49160 | tf_op jit(solution)/shard_map/ppermute | solution.py:366

commit v7 on v6

--- a/solution.py
+++ b/solution.py
@@ -10,12 +10,9 @@
 BF16 = jnp.bfloat16
 
 
-def split3(value):
+def split(value):
     high = value.astype(BF16)
-    rest = value - high.astype(F32)
-    middle = rest.astype(BF16)
-    low = (rest - middle.astype(F32)).astype(BF16)
-    return high, middle, low
+    return high, (value - high.astype(F32)).astype(BF16)
 
 
 def iota(shape, dim):
@@ -38,7 +35,7 @@
 
 
 def scatter(flux, idx, lane_hot, count, lanes):
-    parts = [part.astype(F32) for part in split3(flux)]
+    parts = [part.astype(F32) for part in split(flux)]
     columns = []
     for row in range(idx.shape[0]):
         hit = row_hit(idx, row, lanes, count)
@@ -52,16 +49,16 @@
     out = lax.dot_general(
         spread, lane_hot, (((1,), (1,)), ((), ())), preferred_element_type=F32
     )
-    return out[:count] + out[count : 2 * count] + out[2 * count :]
+    return out[:count] + out[count:]
 
 
 def gather(cells, idx, lane_hot, lanes):
     count = cells.shape[0]
-    stacked = jnp.concatenate(split3(cells), axis=0)
+    stacked = jnp.concatenate(split(cells), axis=0)
     picked = lax.dot_general(
         stacked, lane_hot, (((1,), (0,)), ((), ())), preferred_element_type=F32
     )
-    picked = picked[:count] + picked[count : 2 * count] + picked[2 * count :]
+    picked = picked[:count] + picked[count:]
     slots = idx.shape[1]
     out = jnp.zeros(idx.shape, F32)
     for row in range(idx.shape[0]):
@@ -192,8 +189,13 @@
 
 
 def first_kernel(
-    fields_ref, recv_ref, p_ref, tx_out, ty_out, tz_out, gain_out, base_out, wx_ref, wy_ref, seg_ref, well_ref, held_ref, send_ref, face_ref, term_ref
+    shared_ref, recv_ref, p_ref, tx_out, ty_out, tz_out, gain_out, base_out, wx_ref, wy_ref, seg_ref, well_ref, held_ref, send_ref, face_ref, term_ref, fields_ref, sem
 ):
+    tail, body = pl.ds(320, 8), pl.ds(0, 320)
+    late = pltpu.make_async_copy(shared_ref.at[:, tail], fields_ref.at[:, tail], sem.at[0])
+    main = pltpu.make_async_copy(shared_ref.at[:, body], fields_ref.at[:, body], sem.at[1])
+    late.start()
+    main.start()
     unit, here, after, before = places()
     own = iota((16, 128), 0) // 2
     groups = []
@@ -214,10 +216,12 @@
     zero = jnp.zeros(cond.shape, F32)
     seg = well_update(rate, index, fm, zero, zero)
     seg_ref[...] = seg
+    late.wait()
     for m in range(2 * UNIT):
         held_ref[m] = fields_ref[m, 320:328, :].astype(jnp.int32)
     hots = spread_wells(F32(0.0) - index * seg, host, held_ref, term_ref)
     wy_ref[...] = recv_ref[4 * PARTS : 4 * PARTS + 32, :]
+    main.wait()
     top = iota((8, 128), 1) == 127
     for y in range(2):
         west = rows_at(recv_ref, before + PARTS * y + 40)
@@ -353,11 +357,11 @@
 
     vmem = pl.BlockSpec(memory_space=pltpu.VMEM)
 
-    def call(body, outs, *args, placed=near, scratch=(), **static):
+    def call(body, outs, *args, placed=near, scratch=(), specs=None, **static):
         return pl.pallas_call(
             lambda *refs: body(*refs, **static),
             out_shape=outs,
-            in_specs=[vmem] * len(args),
+            in_specs=[vmem] * len(args) if specs is None else specs,
             out_specs=[vmem] * len(outs),
             scratch_shapes=scratch,
         )(*map(placed, args))
@@ -382,7 +386,8 @@
     p, *kept, seg, well, held, send, face = call(
         first_kernel,
         [grid] * 6 + [shape(2, 8, 128), edges, wells, shape(4, 32, 128), pltpu.VMEM((8, 8, 128), jnp.int32), message, edges],
-        fields, recv, scratch=[grid], placed=lambda value: value if value is fields else near(value),
+        fields, recv, scratch=[grid, shape(8, 328, 128), pltpu.SemaphoreType.DMA((2,))],
+        specs=[pl.BlockSpec(memory_space=pl.ANY), vmem], placed=lambda value: value if value is fields else near(value),
     )
     for sweep in range(1, SWEEPS):
         last = sweep == SWEEPS - 1

time: 109 us -> 107 us (0.982)
  Pallas kernels: 15.7 us -> 13.6 us
    pallas_call x8, Pallas kernels: 15.7 us -> 13.6 us  [call(): pl.pallas_call(lambda *refs: body(*refs, **static), out_shape=outs, in_sp...]
where the time goes in v7:
time: 107 us; the launch traced here: 106 us
  blocking collectives  63.3 us (59%)
  starting transfers between devices  28 us (26%)
  Pallas kernels  13.6 us (13%)
    all_gather x6, blocking collectives, exchanged(): lax.all_gather(send, ('gx', 'gy'), axis_index_groups=columns, tiled=True)  41.5 us
    ppermute x6, starting transfers between devices, exchanged(): edge = lax.ppermute(face, 'gy', facing)  23 us
    pallas_call x8, Pallas kernels, call(): pl.pallas_call(lambda *refs: body(*refs, **static), out_shape=outs, in_sp...  13.6 us
    all_gather x6, blocking collectives, exchanged(): return lax.all_gather(both, 'gy', axis_index_groups=mates, tiled=True)  11.8 us
    all_to_all x1, blocking collectives, among_chips(): lax.all_to_all(buffer, ('gx', 'gy'), 0, 0, tiled=True, axis_index_groups=...  9.95 us
    all_to_all x1, starting transfers between devices, among_chips(): lax.all_to_all(buffer, ('gx', 'gy'), 0, 0, tiled=True, axis_index_groups=...  4.97 us
  transfers between devices with their start and end apart: 7, of which 1 were waited for; matrix products, arithmetic and copies ran while one was open for 0% of the time, Pallas kernels for 0%

profile of v7, /device:TPU:25, one launch (start us, length us, event | category | flops | bytes accessed | tf_op | source)
XLA Modules:
  0.0 106.3 jit_solution(4986790086383978256)
XLA Ops:
  0.6 2.0 %shard_map.113 = (f32[8,24,128]{2,1,0:T(8,128)}, f32[8,328,128]{2,1,0:T(8,128)}) custom-call(f32[8,8,128]{2,1,0:T(8,128)} %refs_0_.1, f32[8,8,128]{2,1,0:T(8,128)} %refs_1_.1, f32[8,8,128]{2,1,0:T(8,128)} %refs_2_.1, f32[8,8,128]{2,1,0:T(8,128)} %refs_3_.1, f32[8,8,128]{2,1,0:T(8,128)} %refs_4_.1, s32[4,1,2,128]{3,2,1,0:T(2,128)} %refs_5_.1, ...), custom_call_target="tpu_custom_call" | custom-call | tf_op jit(solution)/shard_map/pallas_call | solution.py:361
  2.7 9.9 %all_to_all.10.refs_0_ = f32[8,24,128]{2,1,0:T(8,128)S(1)} all-to-all(f32[8,24,128]{2,1,0:T(8,128)} %get-tuple-element.36), channel_id=1, replica_groups={{0,1,16,17,32,33,48,49},{2,3,18,19,34,35,50,51},{4,5,20,21,36,37,52,53}..., dimensions={0} | all-to-all | bytes 196608 | tf_op jit(solution)/shard_map/all_to_all | solution.py:376
  12.6 5.0 %all-to-all-start = ((f32[8,328,128]{2,1,0:T(8,128)}), f32[8,328,128]{2,1,0:T(8,128)}, u32[]{:S(2)}, u32[]{:S(2)}) async-start(f32[8,328,128]{2,1,0:T(8,128)} %get-tuple-element.35), calls=%async_computation | async-start | bytes 2686976 | tf_op jit(solution)/shard_map/all_to_all | solution.py:376
  17.6 4.4 %collective-permute-start = (f32[32,128]{1,0:T(8,128)S(1)}, f32[32,128]{1,0:T(8,128)S(1)}, u32[]{:S(2)}, u32[]{:S(2)}) collective-permute-start(f32[32,128]{1,0:T(8,128)S(1)} %get-tuple-element.38), channel_id=1, source_target_pairs={{1,2},{3,4},{5,6},{7,8},{9,10},{11,12},{13,14},{2,1},{4,3},{6,5},{... | collective-permute-start | bytes 49160 | tf_op jit(solution)/shard_map/ppermute | solution.py:370
  22.0 11.3 %all_gather.36 = f32[192,128]{1,0:T(8,128)S(1)} all-gather(f32[96,128]{1,0:T(8,128)S(1)} %get-tuple-element.37), channel_id=1, replica_groups={{0,64},{16,80},{32,96},{48,112},{128,192},{144,208},{160,224},{176,240}..., dimensions={0}, use_global_device_ids=true | all-gather | bytes 147456 | tf_op jit(solution)/shard_map/all_gather | solution.py:371
  33.3 2.0 %all_gather.37.refs_1_ = f32[448,128]{1,0:T(8,128)S(1)} all-gather(f32[224,128]{1,0:T(8,128)S(1)} %pad_maximum_fusion), channel_id=1, replica_groups={{0,1},{2,3},{4,5},{6,7},{8,9},{10,11},{12,13},{14,15},{16,17},{18,19},{..., dimensions={0}, use_global_device_ids=true | all-gather | bytes 344064 | tf_op jit(solution)/shard_map/all_gather | solution.py:373
  36.0 2.7 %shard_map.115 = (f32[64,8,128]{2,1,0:T(8,128)S(1)}, f32[64,8,128]{2,1,0:T(8,128)S(1)}, f32[64,8,128]{2,1,0:T(8,128)S(1)}, f32[64,8,128]{2,1,0:T(8,128)S(1)}, f3...) custom-call(f32[8,328,128]{2,1,0:T(8,128)} %all-to-all-done.refs_0_,, ...), custom_call_target="tpu_custom_call" | custom-call | tf_op jit(solution)/shard_map/pallas_call | solution.py:361
  38.6 5.2 %collective-permute-start.1 = (f32[32,128]{1,0:T(8,128)S(1)}, f32[32,128]{1,0:T(8,128)S(1)}, u32[]{:S(2)}, u32[]{:S(2)}) collective-permute-start(f32[32,128]{1,0:T(8,128)S(1)} %get-tuple-element.48), channel_id=1, source_target_pairs={{1,2},{3,4},{5,6},{7,8},{9,10},{11,12},{13,14},{2,1},{4,3},{6,5},{... | collective-permute-start | bytes 49160 | tf_op jit(solution)/shard_map/ppermute | solution.py:370
  43.8 10.9 %all_gather.38 = f32[192,128]{1,0:T(8,128)S(1)} all-gather(f32[96,128]{1,0:T(8,128)S(1)} %get-tuple-element.47), channel_id=1, replica_groups={{0,64},{16,80},{32,96},{48,112},{128,192},{144,208},{160,224},{176,240}..., dimensions={0}, use_global_device_ids=true | all-gather | bytes 147456 | tf_op jit(solution)/shard_map/all_gather | solution.py:371
  54.7 2.0 %all_gather.39.refs_8_ = f32[448,128]{1,0:T(8,128)S(1)} all-gather(f32[224,128]{1,0:T(8,128)S(1)} %pad_maximum_fusion.1), channel_id=1, replica_groups={{0,1},{2,3},{4,5},{6,7},{8,9},{10,11},{12,13},{14,15},{16,17},{18,19},{..., dimensions={0}, use_global_device_ids=true | all-gather | bytes 344064 | tf_op jit(solution)/shard_map/all_gather | solution.py:373
  56.7 2.0 %shard_map.116 = (f32[64,8,128]{2,1,0:T(8,128)S(1)}, f32[32,128]{1,0:T(8,128)S(1)}, f32[96,128]{1,0:T(8,128)S(1)}, f32[32,128]{1,0:T(8,128)S(1)}) custom-call(f32[64,8,128]{2,1,0:T(8,128)S(1)} %get-tuple-element.39.refs_0_, f32[64,8,128]{2,1,0:T(8,128)S(1)} %get-tuple-element.40.refs_1_, f32[64,8,128]{2,1,0:T(8,128)S(1)} %get-tuple-element.41.refs_2_, ...), custom_call_target="tpu_custom_call" | custom-call | tf_op jit(solution)/shard_map/pallas_call | solution.py:361
  58.7 2.3 %collective-permute-start.2 = (f32[32,128]{1,0:T(8,128)S(1)}, f32[32,128]{1,0:T(8,128)S(1)}, u32[]{:S(2)}, u32[]{:S(2)}) collective-permute-start(f32[32,128]{1,0:T(8,128)S(1)} %get-tuple-element.54), channel_id=1, source_target_pairs={{1,2},{3,4},{5,6},{7,8},{9,10},{11,12},{13,14},{2,1},{4,3},{6,5},{... | collective-permute-start | bytes 49160 | tf_op jit(solution)/shard_map/ppermute | solution.py:370
  61.0 4.8 %all_gather.40 = f32[192,128]{1,0:T(8,128)S(1)} all-gather(f32[96,128]{1,0:T(8,128)S(1)} %get-tuple-element.53), channel_id=1, replica_groups={{0,64},{16,80},{32,96},{48,112},{128,192},{144,208},{160,224},{176,240}..., dimensions={0}, use_global_device_ids=true | all-gather | bytes 147456 | tf_op jit(solution)/shard_map/all_gather | solution.py:371
  65.9 2.0 %all_gather.41.refs_8_ = f32[448,128]{1,0:T(8,128)S(1)} all-gather(f32[224,128]{1,0:T(8,128)S(1)} %pad_maximum_fusion.2), channel_id=1, replica_groups={{0,1},{2,3},{4,5},{6,7},{8,9},{10,11},{12,13},{14,15},{16,17},{18,19},{..., dimensions={0}, use_global_device_ids=true | all-gather | bytes 344064 | tf_op jit(solution)/shard_map/all_gather | solution.py:373
  67.9 2.0 %shard_map.117 = (f32[64,8,128]{2,1,0:T(8,128)S(1)}, f32[32,128]{1,0:T(8,128)S(1)}, f32[96,128]{1,0:T(8,128)S(1)}, f32[32,128]{1,0:T(8,128)S(1)}) custom-call(f32[64,8,128]{2,1,0:T(8,128)S(1)} %get-tuple-element.52.refs_0_, f32[64,8,128]{2,1,0:T(8,128)S(1)} %get-tuple-element.40.refs_1_, f32[64,8,128]{2,1,0:T(8,128)S(1)} %get-tuple-element.41.refs_2_, ...), custom_call_target="tpu_custom_call" | custom-call | tf_op jit(solution)/shard_map/pallas_call | solution.py:361
  69.8 4.4 %collective-permute-start.3 = (f32[32,128]{1,0:T(8,128)S(1)}, f32[32,128]{1,0:T(8,128)S(1)}, u32[]{:S(2)}, u32[]{:S(2)}) collective-permute-start(f32[32,128]{1,0:T(8,128)S(1)} %get-tuple-element.58), channel_id=1, source_target_pairs={{1,2},{3,4},{5,6},{7,8},{9,10},{11,12},{13,14},{2,1},{4,3},{6,5},{... | collective-permute-start | bytes 49160 | tf_op jit(solution)/shard_map/ppermute | solution.py:370
  74.2 4.8 %all_gather.42 = f32[192,128]{1,0:T(8,128)S(1)} all-gather(f32[96,128]{1,0:T(8,128)S(1)} %get-tuple-element.57), channel_id=1, replica_groups={{0,64},{16,80},{32,96},{48,112},{128,192},{144,208},{160,224},{176,240}..., dimensions={0}, use_global_device_ids=true | all-gather | bytes 147456 | tf_op jit(solution)/shard_map/all_gather | solution.py:371
  79.0 2.0 %all_gather.43.refs_8_ = f32[448,128]{1,0:T(8,128)S(1)} all-gather(f32[224,128]{1,0:T(8,128)S(1)} %pad_maximum_fusion.3), channel_id=1, replica_groups={{0,1},{2,3},{4,5},{6,7},{8,9},{10,11},{12,13},{14,15},{16,17},{18,19},{..., dimensions={0}, use_global_device_ids=true | all-gather | bytes 344064 | tf_op jit(solution)/shard_map/all_gather | solution.py:373
  83.0 2.3 %collective-permute-start.4 = (f32[32,128]{1,0:T(8,128)S(1)}, f32[32,128]{1,0:T(8,128)S(1)}, u32[]{:S(2)}, u32[]{:S(2)}) collective-permute-start(f32[32,128]{1,0:T(8,128)S(1)} %get-tuple-element.62), channel_id=1, source_target_pairs={{1,2},{3,4},{5,6},{7,8},{9,10},{11,12},{13,14},{2,1},{4,3},{6,5},{... | collective-permute-start | bytes 49160 | tf_op jit(solution)/shard_map/ppermute | solution.py:370
  85.3 4.8 %all_gather.44 = f32[192,128]{1,0:T(8,128)S(1)} all-gather(f32[96,128]{1,0:T(8,128)S(1)} %get-tuple-element.61), channel_id=1, replica_groups={{0,64},{16,80},{32,96},{48,112},{128,192},{144,208},{160,224},{176,240}..., dimensions={0}, use_global_device_ids=true | all-gather | bytes 147456 | tf_op jit(solution)/shard_map/all_gather | solution.py:371
  90.2 2.0 %all_gather.45.refs_8_ = f32[448,128]{1,0:T(8,128)S(1)} all-gather(f32[224,128]{1,0:T(8,128)S(1)} %pad_maximum_fusion.4), channel_id=1, replica_groups={{0,1},{2,3},{4,5},{6,7},{8,9},{10,11},{12,13},{14,15},{16,17},{18,19},{..., dimensions={0}, use_global_device_ids=true | all-gather | bytes 344064 | tf_op jit(solution)/shard_map/all_gather | solution.py:373
  94.1 4.4 %collective-permute-start.5 = (f32[32,128]{1,0:T(8,128)S(1)}, f32[32,128]{1,0:T(8,128)S(1)}, u32[]{:S(2)}, u32[]{:S(2)}) collective-permute-start(f32[32,128]{1,0:T(8,128)S(1)} %get-tuple-element.66), channel_id=1, source_target_pairs={{1,2},{3,4},{5,6},{7,8},{9,10},{11,12},{13,14},{2,1},{4,3},{6,5},{... | collective-permute-start | bytes 49160 | tf_op jit(solution)/shard_map/ppermute | solution.py:370
  98.5 4.8 %all_gather.46 = f32[192,128]{1,0:T(8,128)S(1)} all-gather(f32[96,128]{1,0:T(8,128)S(1)} %get-tuple-element.65), channel_id=1, replica_groups={{0,64},{16,80},{32,96},{48,112},{128,192},{144,208},{160,224},{176,240}..., dimensions={0}, use_global_device_ids=true | all-gather | bytes 147456 | tf_op jit(solution)/shard_map/all_gather | solution.py:371
  103.4 2.0 %all_gather.47.refs_8_ = f32[448,128]{1,0:T(8,128)S(1)} all-gather(f32[224,128]{1,0:T(8,128)S(1)} %pad_maximum_fusion.5), channel_id=1, replica_groups={{0,1},{2,3},{4,5},{6,7},{8,9},{10,11},{12,13},{14,15},{16,17},{18,19},{..., dimensions={0}, use_global_device_ids=true | all-gather | bytes 344064 | tf_op jit(solution)/shard_map/all_gather | solution.py:373
  (17 shorter events, 5.7 us)
Async XLA Ops:
  12.6 23.3 %all-to-all-start = ((f32[8,328,128]{2,1,0:T(8,128)}), f32[8,328,128]{2,1,0:T(8,128)}, u32[]{:S(2)}, u32[]{:S(2)}) async-start(f32[8,328,128]{2,1,0:T(8,128)} %get-tuple-element.35), calls=%async_computation | async-start | bytes 2686976 | tf_op jit(solution)/shard_map/all_to_all | solution.py:376
  17.6 15.7 %collective-permute-start = (f32[32,128]{1,0:T(8,128)S(1)}, f32[32,128]{1,0:T(8,128)S(1)}, u32[]{:S(2)}, u32[]{:S(2)}) collective-permute-start(f32[32,128]{1,0:T(8,128)S(1)} %get-tuple-element.38), channel_id=1, source_target_pairs={{1,2},{3,4},{5,6},{7,8},{9,10},{11,12},{13,14},{2,1},{4,3},{6,5},{... | collective-permute-start | bytes 49160 | tf_op jit(solution)/shard_map/ppermute | solution.py:370
  38.6 16.1 %collective-permute-start.1 = (f32[32,128]{1,0:T(8,128)S(1)}, f32[32,128]{1,0:T(8,128)S(1)}, u32[]{:S(2)}, u32[]{:S(2)}) collective-permute-start(f32[32,128]{1,0:T(8,128)S(1)} %get-tuple-element.48), channel_id=1, source_target_pairs={{1,2},{3,4},{5,6},{7,8},{9,10},{11,12},{13,14},{2,1},{4,3},{6,5},{... | collective-permute-start | bytes 49160 | tf_op jit(solution)/shard_map/ppermute | solution.py:370
  58.7 7.2 %collective-permute-start.2 = (f32[32,128]{1,0:T(8,128)S(1)}, f32[32,128]{1,0:T(8,128)S(1)}, u32[]{:S(2)}, u32[]{:S(2)}) collective-permute-start(f32[32,128]{1,0:T(8,128)S(1)} %get-tuple-element.54), channel_id=1, source_target_pairs={{1,2},{3,4},{5,6},{7,8},{9,10},{11,12},{13,14},{2,1},{4,3},{6,5},{... | collective-permute-start | bytes 49160 | tf_op jit(solution)/shard_map/ppermute | solution.py:370
  69.8 9.2 %collective-permute-start.3 = (f32[32,128]{1,0:T(8,128)S(1)}, f32[32,128]{1,0:T(8,128)S(1)}, u32[]{:S(2)}, u32[]{:S(2)}) collective-permute-start(f32[32,128]{1,0:T(8,128)S(1)} %get-tuple-element.58), channel_id=1, source_target_pairs={{1,2},{3,4},{5,6},{7,8},{9,10},{11,12},{13,14},{2,1},{4,3},{6,5},{... | collective-permute-start | bytes 49160 | tf_op jit(solution)/shard_map/ppermute | solution.py:370
  83.0 7.2 %collective-permute-start.4 = (f32[32,128]{1,0:T(8,128)S(1)}, f32[32,128]{1,0:T(8,128)S(1)}, u32[]{:S(2)}, u32[]{:S(2)}) collective-permute-start(f32[32,128]{1,0:T(8,128)S(1)} %get-tuple-element.62), channel_id=1, source_target_pairs={{1,2},{3,4},{5,6},{7,8},{9,10},{11,12},{13,14},{2,1},{4,3},{6,5},{... | collective-permute-start | bytes 49160 | tf_op jit(solution)/shard_map/ppermute | solution.py:370
  94.1 9.2 %collective-permute-start.5 = (f32[32,128]{1,0:T(8,128)S(1)}, f32[32,128]{1,0:T(8,128)S(1)}, u32[]{:S(2)}, u32[]{:S(2)}) collective-permute-start(f32[32,128]{1,0:T(8,128)S(1)} %get-tuple-element.66), channel_id=1, source_target_pairs={{1,2},{3,4},{5,6},{7,8},{9,10},{11,12},{13,14},{2,1},{4,3},{6,5},{... | collective-permute-start | bytes 49160 | tf_op jit(solution)/shard_map/ppermute | solution.py:370

commit v8 on v7

--- a/solution.py
+++ b/solution.py
@@ -165,20 +165,22 @@
         [host_ref[0].astype(F32), index_ref[0], cond_ref[0], rate_ref[0]], axis=0
     )
     edge = jnp.concatenate([ty_ref[x, 7:8, :] for x in range(8)], axis=0)
+    held = held_ref[...].reshape(8, 128).astype(F32)
     for m in range(members):
         small_ref[m, 0:8, :] = pack
+        small_ref[m, 24:32, :] = held
+        large_ref[m, 320:328, :] = held
         small_ref[m, 8:16, :] = tx_ref[7]
         small_ref[m, 16:24, :] = edge
     for which, ref in enumerate((rhs_ref, acc_ref, tx_ref, ty_ref, tz_ref)):
         whole = ref[...].reshape(64, 128)
         for m in range(members):
             large_ref[m, 64 * which : 64 * which + 64, :] = whole
-    held = held_ref[...].reshape(8, 128).astype(F32)
-    for m in range(members):
-        large_ref[m, 320:328, :] = held
-
-
-def share_kernel(small_ref, send_ref, face_ref):
+
+
+def share_kernel(small_ref, send_ref, face_ref, held_ref):
+    for m in range(2 * UNIT):
+        held_ref[m] = small_ref[m, 24:32, :].astype(jnp.int32)
     for y in range(2):
         for block in range(UNIT):
             send_ref[pl.ds(PARTS * y + 8 * block, 8), :] = small_ref[2 * block + y, 0:8, :]
@@ -188,14 +190,7 @@
         face_ref[pl.ds(8 * block, 8), :] = small_ref[2 * block + 1, 16:24, :]
 
 
-def first_kernel(
-    shared_ref, recv_ref, p_ref, tx_out, ty_out, tz_out, gain_out, base_out, wx_ref, wy_ref, seg_ref, well_ref, held_ref, send_ref, face_ref, term_ref, fields_ref, sem
-):
-    tail, body = pl.ds(320, 8), pl.ds(0, 320)
-    late = pltpu.make_async_copy(shared_ref.at[:, tail], fields_ref.at[:, tail], sem.at[0])
-    main = pltpu.make_async_copy(shared_ref.at[:, body], fields_ref.at[:, body], sem.at[1])
-    late.start()
-    main.start()
+def wells_kernel(recv_ref, held_ref, wx_ref, wy_ref, seg_ref, well_ref, term_ref):
     unit, here, after, before = places()
     own = iota((16, 128), 0) // 2
     groups = []
@@ -216,21 +211,33 @@
     zero = jnp.zeros(cond.shape, F32)
     seg = well_update(rate, index, fm, zero, zero)
     seg_ref[...] = seg
-    late.wait()
-    for m in range(2 * UNIT):
-        held_ref[m] = fields_ref[m, 320:328, :].astype(jnp.int32)
-    hots = spread_wells(F32(0.0) - index * seg, host, held_ref, term_ref)
+    spread_wells(F32(0.0) - index * seg, host, held_ref, term_ref)
     wy_ref[...] = recv_ref[4 * PARTS : 4 * PARTS + 32, :]
-    main.wait()
-    top = iota((8, 128), 1) == 127
     for y in range(2):
         west = rows_at(recv_ref, before + PARTS * y + 40)
-        west = jnp.where(unit == 0, F32(0.0), west)
-        wx_ref[y] = west
-        for x in range(32):
+        wx_ref[y] = jnp.where(unit == 0, F32(0.0), west)
+
+
+def first_kernel(
+    shared_ref, wx_ref, wy_ref, held_ref, term_ref, p_ref, tx_out, ty_out, tz_out, gain_out, base_out, send_ref, face_ref,
+    fields_ref, sem,
+):
+    members = 2 * UNIT
+    loads = [
+        pltpu.make_async_copy(shared_ref.at[m, pl.ds(0, 320)], fields_ref.at[m], sem.at[m]) for m in range(members)
+    ]
+    for load in loads:
+        load.start()
+    hots = [lane_onehot(held_ref[2 * block + y], 128) for y in range(2) for block in range(UNIT)]
+    top = iota((8, 128), 1) == 127
+    for x in range(32):
+        if x % 8 == 0:
+            loads[x // 4].wait()
+            loads[x // 4 + 1].wait()
+        for y in range(2):
             tx, ty, tz = (field(fields_ref, which, y, x) for which in (2, 3, 4))
-            edge = field(fields_ref, 3, 0, x)[7:8, :] if y else recv_ref[4 * PARTS + x : 4 * PARTS + x + 1, :]
-            wx = field(fields_ref, 2, y, x - 1) if x else west
+            edge = field(fields_ref, 3, 0, x)[7:8, :] if y else wy_ref[x : x + 1, :]
+            wx = field(fields_ref, 2, y, x - 1) if x else wx_ref[y]
             wy = y_moved(ty, edge, -1)
             inner = jnp.where(top, F32(0.0), tz)
             wz = pltpu.roll(inner, 1, 1)
@@ -376,19 +383,25 @@
         return lax.all_to_all(buffer, ("gx", "gy"), 0, 0, tiled=True, axis_index_groups=chips)
 
     small, large = call(
-        pack_kernel, [result(8, 24, 128), result(8, 328, 128)], rhs_field, accumulation, trans_x, trans_y, trans_z,
+        pack_kernel, [result(8, 32, 128), result(8, 328, 128)], rhs_field, accumulation, trans_x, trans_y, trans_z,
         held_cells, perf_host, well_index, seg_cond, seg_rate, placed=lambda value: value,
     )
     fields = among_chips(large)
     message, edges, grid, wells = shape(96, 128), shape(32, 128), shape(64, 8, 128), shape(32, 128)
-    send, face = call(share_kernel, [message, edges], among_chips(small))
+    send, face, held = call(
+        share_kernel, [message, edges, pltpu.VMEM((8, 8, 128), jnp.int32)], among_chips(small)
+    )
     recv = exchanged(send, face)
-    p, *kept, seg, well, held, send, face = call(
-        first_kernel,
-        [grid] * 6 + [shape(2, 8, 128), edges, wells, shape(4, 32, 128), pltpu.VMEM((8, 8, 128), jnp.int32), message, edges],
-        fields, recv, scratch=[grid, shape(8, 328, 128), pltpu.SemaphoreType.DMA((2,))],
-        specs=[pl.BlockSpec(memory_space=pl.ANY), vmem], placed=lambda value: value if value is fields else near(value),
-    )
+    wx, wy, seg, well, term = call(
+        wells_kernel, [shape(2, 8, 128), edges, wells, shape(4, 32, 128), grid], recv, held
+    )
+    p, *kept, send, face = call(
+        first_kernel, [grid] * 6 + [message, edges], fields, wx, wy, held, term,
+        placed=lambda value: value if value is fields else near(value),
+        specs=[pl.BlockSpec(memory_space=pl.ANY)] + [vmem] * 4,
+        scratch=[shape(8, 320, 128), pltpu.SemaphoreType.DMA((8,))],
+    )
+    kept += [wx, wy]
     for sweep in range(1, SWEEPS):
         last = sweep == SWEEPS - 1
         recv = exchanged(send, face)

time: 107 us -> 107 us (level)
    pallas_call x8 -> x9, Pallas kernels: 13.6 us -> 14.1 us  [call(): pl.pallas_call(lambda *refs: body(*refs, **static), out_shape=outs, in_sp...]
  transfers between devices with their start and end apart: 7 -> 7, of which waited for: 1 -> 0; matrix products, arithmetic and copies ran while one was open for 0% -> 0% of each run, Pallas kernels for 0% -> 1%
where the time goes in v8:
time: 107 us; the launch traced here: 106 us
  blocking collectives  63.6 us (59%)
  starting transfers between devices  27.8 us (26%)
  Pallas kernels  14.1 us (13%)
    all_gather x6, blocking collectives, exchanged(): lax.all_gather(send, ('gx', 'gy'), axis_index_groups=columns, tiled=True)  41.5 us
    ppermute x6, starting transfers between devices, exchanged(): edge = lax.ppermute(face, 'gy', facing)  22.8 us
    pallas_call x9, Pallas kernels, call(): pl.pallas_call(lambda *refs: body(*refs, **static), out_shape=outs, in_sp...  14.1 us
    all_gather x6, blocking collectives, exchanged(): return lax.all_gather(both, 'gy', axis_index_groups=mates, tiled=True)  11.8 us
    all_to_all x1, blocking collectives, among_chips(): lax.all_to_all(buffer, ('gx', 'gy'), 0, 0, tiled=True, axis_index_groups=...  10.2 us
    all_to_all x1, starting transfers between devices, among_chips(): lax.all_to_all(buffer, ('gx', 'gy'), 0, 0, tiled=True, axis_index_groups=...  5.02 us
  transfers between devices with their start and end apart: 7, of which 0 were waited for; matrix products, arithmetic and copies ran while one was open for 0% of the time, Pallas kernels for 1%

profile of v8, /device:TPU:25, one launch (start us, length us, event | category | flops | bytes accessed | tf_op | source)
XLA Modules:
  0.0 106.3 jit_solution(16285458096318270476)
XLA Ops:
  0.6 2.1 %shard_map.113 = (f32[8,32,128]{2,1,0:T(8,128)}, f32[8,328,128]{2,1,0:T(8,128)}) custom-call(f32[8,8,128]{2,1,0:T(8,128)} %refs_0_.1, f32[8,8,128]{2,1,0:T(8,128)} %refs_1_.1, f32[8,8,128]{2,1,0:T(8,128)} %refs_2_.1, f32[8,8,128]{2,1,0:T(8,128)} %refs_3_.1, f32[8,8,128]{2,1,0:T(8,128)} %refs_4_.1, s32[4,1,2,128]{3,2,1,0:T(2,128)} %refs_5_.1, ...), custom_call_target="tpu_custom_call" | custom-call | tf_op jit(solution)/shard_map/pallas_call | solution.py:368
  2.7 10.2 %all_to_all.10.refs_0_ = f32[8,32,128]{2,1,0:T(8,128)S(1)} all-to-all(f32[8,32,128]{2,1,0:T(8,128)} %get-tuple-element.37), channel_id=1, replica_groups={{0,1,16,17,32,33,48,49},{2,3,18,19,34,35,50,51},{4,5,20,21,36,37,52,53}..., dimensions={0} | all-to-all | bytes 262144 | tf_op jit(solution)/shard_map/all_to_all | solution.py:383
  12.9 5.0 %all-to-all-start = ((f32[8,328,128]{2,1,0:T(8,128)}), f32[8,328,128]{2,1,0:T(8,128)}, u32[]{:S(2)}, u32[]{:S(2)}) async-start(f32[8,328,128]{2,1,0:T(8,128)} %get-tuple-element.36), calls=%async_computation | async-start | bytes 2686976 | tf_op jit(solution)/shard_map/all_to_all | solution.py:383
  18.0 4.4 %collective-permute-start = (f32[32,128]{1,0:T(8,128)S(1)}, f32[32,128]{1,0:T(8,128)S(1)}, u32[]{:S(2)}, u32[]{:S(2)}) collective-permute-start(f32[32,128]{1,0:T(8,128)S(1)} %get-tuple-element.39), channel_id=1, source_target_pairs={{1,2},{3,4},{5,6},{7,8},{9,10},{11,12},{13,14},{2,1},{4,3},{6,5},{... | collective-permute-start | bytes 49160 | tf_op jit(solution)/shard_map/ppermute | solution.py:377
  22.4 11.3 %all_gather.36 = f32[192,128]{1,0:T(8,128)S(1)} all-gather(f32[96,128]{1,0:T(8,128)S(1)} %get-tuple-element.38), channel_id=1, replica_groups={{0,64},{16,80},{32,96},{48,112},{128,192},{144,208},{160,224},{176,240}..., dimensions={0}, use_global_device_ids=true | all-gather | bytes 147456 | tf_op jit(solution)/shard_map/all_gather | solution.py:378
  33.7 2.0 %all_gather.37.refs_0_ = f32[448,128]{1,0:T(8,128)S(1)} all-gather(f32[224,128]{1,0:T(8,128)S(1)} %pad_maximum_fusion), channel_id=1, replica_groups={{0,1},{2,3},{4,5},{6,7},{8,9},{10,11},{12,13},{14,15},{16,17},{18,19},{..., dimensions={0}, use_global_device_ids=true | all-gather | bytes 344064 | tf_op jit(solution)/shard_map/all_gather | solution.py:380
  36.6 2.2 %shard_map.116 = (f32[64,8,128]{2,1,0:T(8,128)S(1)}, f32[64,8,128]{2,1,0:T(8,128)S(1)}, f32[64,8,128]{2,1,0:T(8,128)S(1)}, f32[64,8,128]{2,1,0:T(8,128)S(1)}, f3...) custom-call(f32[8,328,128]{2,1,0:T(8,128)} %all-to-all-done.refs_0_, ...), custom_call_target="tpu_custom_call" | custom-call | tf_op jit(solution)/shard_map/pallas_call | solution.py:368
  38.8 4.9 %collective-permute-start.1 = (f32[32,128]{1,0:T(8,128)S(1)}, f32[32,128]{1,0:T(8,128)S(1)}, u32[]{:S(2)}, u32[]{:S(2)}) collective-permute-start(f32[32,128]{1,0:T(8,128)S(1)} %get-tuple-element.51), channel_id=1, source_target_pairs={{1,2},{3,4},{5,6},{7,8},{9,10},{11,12},{13,14},{2,1},{4,3},{6,5},{... | collective-permute-start | bytes 49160 | tf_op jit(solution)/shard_map/ppermute | solution.py:377
  43.8 10.9 %all_gather.38 = f32[192,128]{1,0:T(8,128)S(1)} all-gather(f32[96,128]{1,0:T(8,128)S(1)} %get-tuple-element.50), channel_id=1, replica_groups={{0,64},{16,80},{32,96},{48,112},{128,192},{144,208},{160,224},{176,240}..., dimensions={0}, use_global_device_ids=true | all-gather | bytes 147456 | tf_op jit(solution)/shard_map/all_gather | solution.py:378
  56.6 2.0 %shard_map.117 = (f32[64,8,128]{2,1,0:T(8,128)S(1)}, f32[32,128]{1,0:T(8,128)S(1)}, f32[96,128]{1,0:T(8,128)S(1)}, f32[32,128]{1,0:T(8,128)S(1)}) custom-call(f32[64,8,128]{2,1,0:T(8,128)S(1)} %get-tuple-element.44.refs_0_, f32[64,8,128]{2,1,0:T(8,128)S(1)} %get-tuple-element.45.refs_1_, f32[64,8,128]{2,1,0:T(8,128)S(1)} %get-tuple-element.46.refs_2_, ...), custom_call_target="tpu_custom_call" | custom-call | tf_op jit(solution)/shard_map/pallas_call | solution.py:368
  58.6 2.3 %collective-permute-start.2 = (f32[32,128]{1,0:T(8,128)S(1)}, f32[32,128]{1,0:T(8,128)S(1)}, u32[]{:S(2)}, u32[]{:S(2)}) collective-permute-start(f32[32,128]{1,0:T(8,128)S(1)} %get-tuple-element.56), channel_id=1, source_target_pairs={{1,2},{3,4},{5,6},{7,8},{9,10},{11,12},{13,14},{2,1},{4,3},{6,5},{... | collective-permute-start | bytes 49160 | tf_op jit(solution)/shard_map/ppermute | solution.py:377
  61.0 4.8 %all_gather.40 = f32[192,128]{1,0:T(8,128)S(1)} all-gather(f32[96,128]{1,0:T(8,128)S(1)} %get-tuple-element.55), channel_id=1, replica_groups={{0,64},{16,80},{32,96},{48,112},{128,192},{144,208},{160,224},{176,240}..., dimensions={0}, use_global_device_ids=true | all-gather | bytes 147456 | tf_op jit(solution)/shard_map/all_gather | solution.py:378
  65.8 2.0 %all_gather.41.refs_8_ = f32[448,128]{1,0:T(8,128)S(1)} all-gather(f32[224,128]{1,0:T(8,128)S(1)} %pad_maximum_fusion.2), channel_id=1, replica_groups={{0,1},{2,3},{4,5},{6,7},{8,9},{10,11},{12,13},{14,15},{16,17},{18,19},{..., dimensions={0}, use_global_device_ids=true | all-gather | bytes 344064 | tf_op jit(solution)/shard_map/all_gather | solution.py:380
  67.8 2.0 %shard_map.118 = (f32[64,8,128]{2,1,0:T(8,128)S(1)}, f32[32,128]{1,0:T(8,128)S(1)}, f32[96,128]{1,0:T(8,128)S(1)}, f32[32,128]{1,0:T(8,128)S(1)}) custom-call(f32[64,8,128]{2,1,0:T(8,128)S(1)} %get-tuple-element.54.refs_0_, f32[64,8,128]{2,1,0:T(8,128)S(1)} %get-tuple-element.45.refs_1_, f32[64,8,128]{2,1,0:T(8,128)S(1)} %get-tuple-element.46.refs_2_, ...), custom_call_target="tpu_custom_call" | custom-call | tf_op jit(solution)/shard_map/pallas_call | solution.py:368
  69.8 4.4 %collective-permute-start.3 = (f32[32,128]{1,0:T(8,128)S(1)}, f32[32,128]{1,0:T(8,128)S(1)}, u32[]{:S(2)}, u32[]{:S(2)}) collective-permute-start(f32[32,128]{1,0:T(8,128)S(1)} %get-tuple-element.60), channel_id=1, source_target_pairs={{1,2},{3,4},{5,6},{7,8},{9,10},{11,12},{13,14},{2,1},{4,3},{6,5},{... | collective-permute-start | bytes 49160 | tf_op jit(solution)/shard_map/ppermute | solution.py:377
  74.1 4.8 %all_gather.42 = f32[192,128]{1,0:T(8,128)S(1)} all-gather(f32[96,128]{1,0:T(8,128)S(1)} %get-tuple-element.59), channel_id=1, replica_groups={{0,64},{16,80},{32,96},{48,112},{128,192},{144,208},{160,224},{176,240}..., dimensions={0}, use_global_device_ids=true | all-gather | bytes 147456 | tf_op jit(solution)/shard_map/all_gather | solution.py:378
  81.0 2.0 %shard_map.119 = (f32[64,8,128]{2,1,0:T(8,128)S(1)}, f32[32,128]{1,0:T(8,128)S(1)}, f32[96,128]{1,0:T(8,128)S(1)}, f32[32,128]{1,0:T(8,128)S(1)}) custom-call(f32[64,8,128]{2,1,0:T(8,128)S(1)} %get-tuple-element.58.refs_0_, f32[64,8,128]{2,1,0:T(8,128)S(1)} %get-tuple-element.45.refs_1_, f32[64,8,128]{2,1,0:T(8,128)S(1)} %get-tuple-element.46.refs_2_, ...), custom_call_target="tpu_custom_call" | custom-call | tf_op jit(solution)/shard_map/pallas_call | solution.py:368
  82.9 2.3 %collective-permute-start.4 = (f32[32,128]{1,0:T(8,128)S(1)}, f32[32,128]{1,0:T(8,128)S(1)}, u32[]{:S(2)}, u32[]{:S(2)}) collective-permute-start(f32[32,128]{1,0:T(8,128)S(1)} %get-tuple-element.64), channel_id=1, source_target_pairs={{1,2},{3,4},{5,6},{7,8},{9,10},{11,12},{13,14},{2,1},{4,3},{6,5},{... | collective-permute-start | bytes 49160 | tf_op jit(solution)/shard_map/ppermute | solution.py:377
  85.3 4.8 %all_gather.44 = f32[192,128]{1,0:T(8,128)S(1)} all-gather(f32[96,128]{1,0:T(8,128)S(1)} %get-tuple-element.63), channel_id=1, replica_groups={{0,64},{16,80},{32,96},{48,112},{128,192},{144,208},{160,224},{176,240}..., dimensions={0}, use_global_device_ids=true | all-gather | bytes 147456 | tf_op jit(solution)/shard_map/all_gather | solution.py:378
  90.1 2.0 %all_gather.45.refs_8_ = f32[448,128]{1,0:T(8,128)S(1)} all-gather(f32[224,128]{1,0:T(8,128)S(1)} %pad_maximum_fusion.4), channel_id=1, replica_groups={{0,1},{2,3},{4,5},{6,7},{8,9},{10,11},{12,13},{14,15},{16,17},{18,19},{..., dimensions={0}, use_global_device_ids=true | all-gather | bytes 344064 | tf_op jit(solution)/shard_map/all_gather | solution.py:380
  92.1 2.0 %shard_map.120 = (f32[64,8,128]{2,1,0:T(8,128)S(1)}, f32[32,128]{1,0:T(8,128)S(1)}, f32[96,128]{1,0:T(8,128)S(1)}, f32[32,128]{1,0:T(8,128)S(1)}) custom-call(f32[64,8,128]{2,1,0:T(8,128)S(1)} %get-tuple-element.62.refs_0_, f32[64,8,128]{2,1,0:T(8,128)S(1)} %get-tuple-element.45.refs_1_, f32[64,8,128]{2,1,0:T(8,128)S(1)} %get-tuple-element.46.refs_2_, ...), custom_call_target="tpu_custom_call" | custom-call | tf_op jit(solution)/shard_map/pallas_call | solution.py:368
  94.1 4.4 %collective-permute-start.5 = (f32[32,128]{1,0:T(8,128)S(1)}, f32[32,128]{1,0:T(8,128)S(1)}, u32[]{:S(2)}, u32[]{:S(2)}) collective-permute-start(f32[32,128]{1,0:T(8,128)S(1)} %get-tuple-element.68), channel_id=1, source_target_pairs={{1,2},{3,4},{5,6},{7,8},{9,10},{11,12},{13,14},{2,1},{4,3},{6,5},{... | collective-permute-start | bytes 49160 | tf_op jit(solution)/shard_map/ppermute | solution.py:377
  98.5 4.8 %all_gather.46 = f32[192,128]{1,0:T(8,128)S(1)} all-gather(f32[96,128]{1,0:T(8,128)S(1)} %get-tuple-element.67), channel_id=1, replica_groups={{0,64},{16,80},{32,96},{48,112},{128,192},{144,208},{160,224},{176,240}..., dimensions={0}, use_global_device_ids=true | all-gather | bytes 147456 | tf_op jit(solution)/shard_map/all_gather | solution.py:378
  103.3 2.0 %all_gather.47.refs_8_ = f32[448,128]{1,0:T(8,128)S(1)} all-gather(f32[224,128]{1,0:T(8,128)S(1)} %pad_maximum_fusion.5), channel_id=1, replica_groups={{0,1},{2,3},{4,5},{6,7},{8,9},{10,11},{12,13},{14,15},{16,17},{18,19},{..., dimensions={0}, use_global_device_ids=true | all-gather | bytes 344064 | tf_op jit(solution)/shard_map/all_gather | solution.py:380
  (18 shorter events, 5.9 us)
Async XLA Ops:
  12.9 23.7 %all-to-all-start = ((f32[8,328,128]{2,1,0:T(8,128)}), f32[8,328,128]{2,1,0:T(8,128)}, u32[]{:S(2)}, u32[]{:S(2)}) async-start(f32[8,328,128]{2,1,0:T(8,128)} %get-tuple-element.36), calls=%async_computation | async-start | bytes 2686976 | tf_op jit(solution)/shard_map/all_to_all | solution.py:383
  18.0 15.7 %collective-permute-start = (f32[32,128]{1,0:T(8,128)S(1)}, f32[32,128]{1,0:T(8,128)S(1)}, u32[]{:S(2)}, u32[]{:S(2)}) collective-permute-start(f32[32,128]{1,0:T(8,128)S(1)} %get-tuple-element.39), channel_id=1, source_target_pairs={{1,2},{3,4},{5,6},{7,8},{9,10},{11,12},{13,14},{2,1},{4,3},{6,5},{... | collective-permute-start | bytes 49160 | tf_op jit(solution)/shard_map/ppermute | solution.py:377
  38.8 15.8 %collective-permute-start.1 = (f32[32,128]{1,0:T(8,128)S(1)}, f32[32,128]{1,0:T(8,128)S(1)}, u32[]{:S(2)}, u32[]{:S(2)}) collective-permute-start(f32[32,128]{1,0:T(8,128)S(1)} %get-tuple-element.51), channel_id=1, source_target_pairs={{1,2},{3,4},{5,6},{7,8},{9,10},{11,12},{13,14},{2,1},{4,3},{6,5},{... | collective-permute-start | bytes 49160 | tf_op jit(solution)/shard_map/ppermute | solution.py:377
  58.6 7.2 %collective-permute-start.2 = (f32[32,128]{1,0:T(8,128)S(1)}, f32[32,128]{1,0:T(8,128)S(1)}, u32[]{:S(2)}, u32[]{:S(2)}) collective-permute-start(f32[32,128]{1,0:T(8,128)S(1)} %get-tuple-element.56), channel_id=1, source_target_pairs={{1,2},{3,4},{5,6},{7,8},{9,10},{11,12},{13,14},{2,1},{4,3},{6,5},{... | collective-permute-start | bytes 49160 | tf_op jit(solution)/shard_map/ppermute | solution.py:377
  69.8 9.2 %collective-permute-start.3 = (f32[32,128]{1,0:T(8,128)S(1)}, f32[32,128]{1,0:T(8,128)S(1)}, u32[]{:S(2)}, u32[]{:S(2)}) collective-permute-start(f32[32,128]{1,0:T(8,128)S(1)} %get-tuple-element.60), channel_id=1, source_target_pairs={{1,2},{3,4},{5,6},{7,8},{9,10},{11,12},{13,14},{2,1},{4,3},{6,5},{... | collective-permute-start | bytes 49160 | tf_op jit(solution)/shard_map/ppermute | solution.py:377
  82.9 7.2 %collective-permute-start.4 = (f32[32,128]{1,0:T(8,128)S(1)}, f32[32,128]{1,0:T(8,128)S(1)}, u32[]{:S(2)}, u32[]{:S(2)}) collective-permute-start(f32[32,128]{1,0:T(8,128)S(1)} %get-tuple-element.64), channel_id=1, source_target_pairs={{1,2},{3,4},{5,6},{7,8},{9,10},{11,12},{13,14},{2,1},{4,3},{6,5},{... | collective-permute-start | bytes 49160 | tf_op jit(solution)/shard_map/ppermute | solution.py:377
  94.1 9.2 %collective-permute-start.5 = (f32[32,128]{1,0:T(8,128)S(1)}, f32[32,128]{1,0:T(8,128)S(1)}, u32[]{:S(2)}, u32[]{:S(2)}) collective-permute-start(f32[32,128]{1,0:T(8,128)S(1)} %get-tuple-element.68), channel_id=1, source_target_pairs={{1,2},{3,4},{5,6},{7,8},{9,10},{11,12},{13,14},{2,1},{4,3},{6,5},{... | collective-permute-start | bytes 49160 | tf_op jit(solution)/shard_map/ppermute | solution.py:377

commit v9 on v7

--- a/solution.py
+++ b/solution.py
@@ -158,9 +158,16 @@
 
 
 def pack_kernel(
-    rhs_ref, acc_ref, tx_ref, ty_ref, tz_ref, held_ref, host_ref, index_ref, cond_ref, rate_ref, small_ref, large_ref
+    rhs_ref, acc_ref, tx_ref, ty_ref, tz_ref, held_ref, host_ref, index_ref, cond_ref, rate_ref, small_ref, large_ref,
+    whole_ref, sem
 ):
     members = large_ref.shape[0]
+    for which, ref in enumerate((rhs_ref, acc_ref, tx_ref, ty_ref, tz_ref)):
+        whole_ref[64 * which : 64 * which + 64, :] = ref[...].reshape(64, 128)
+    whole_ref[320:328, :] = held_ref[...].reshape(8, 128).astype(F32)
+    copies = [pltpu.make_async_copy(whole_ref, large_ref.at[m], sem.at[m]) for m in range(members)]
+    for copy in copies:
+        copy.start()
     pack = jnp.concatenate(
         [host_ref[0].astype(F32), index_ref[0], cond_ref[0], rate_ref[0]], axis=0
     )
@@ -169,13 +176,8 @@
         small_ref[m, 0:8, :] = pack
         small_ref[m, 8:16, :] = tx_ref[7]
         small_ref[m, 16:24, :] = edge
-    for which, ref in enumerate((rhs_ref, acc_ref, tx_ref, ty_ref, tz_ref)):
-        whole = ref[...].reshape(64, 128)
-        for m in range(members):
-            large_ref[m, 64 * which : 64 * which + 64, :] = whole
-    held = held_ref[...].reshape(8, 128).astype(F32)
-    for m in range(members):
-        large_ref[m, 320:328, :] = held
+    for copy in copies:
+        copy.wait()
 
 
 def share_kernel(small_ref, send_ref, face_ref):
@@ -357,12 +359,12 @@
 
     vmem = pl.BlockSpec(memory_space=pltpu.VMEM)
 
-    def call(body, outs, *args, placed=near, scratch=(), specs=None, **static):
+    def call(body, outs, *args, placed=near, scratch=(), specs=None, places_out=None, **static):
         return pl.pallas_call(
             lambda *refs: body(*refs, **static),
             out_shape=outs,
             in_specs=[vmem] * len(args) if specs is None else specs,
-            out_specs=[vmem] * len(outs),
+            out_specs=[vmem] * len(outs) if places_out is None else places_out,
             scratch_shapes=scratch,
         )(*map(placed, args))
 
@@ -378,6 +380,8 @@
     small, large = call(
         pack_kernel, [result(8, 24, 128), result(8, 328, 128)], rhs_field, accumulation, trans_x, trans_y, trans_z,
         held_cells, perf_host, well_index, seg_cond, seg_rate, placed=lambda value: value,
+        places_out=[vmem, pl.BlockSpec(memory_space=pl.ANY)],
+        scratch=[shape(328, 128), pltpu.SemaphoreType.DMA((8,))],
     )
     fields = among_chips(large)
     message, edges, grid, wells = shape(96, 128), shape(32, 128), shape(64, 8, 128), shape(32, 128)

time: 107 us -> 108 us (level)
  no operation moved by 1% of the time
where the time goes in v9:
time: 108 us; the launch traced here: 107 us
  blocking collectives  63.3 us (59%)
  starting transfers between devices  28 us (26%)
  Pallas kernels  14.2 us (13%)
    all_gather x6, blocking collectives, exchanged(): lax.all_gather(send, ('gx', 'gy'), axis_index_groups=columns, tiled=True)  41.5 us
    ppermute x6, starting transfers between devices, exchanged(): edge = lax.ppermute(face, 'gy', facing)  23 us
    pallas_call x8, Pallas kernels, call(): pl.pallas_call(lambda *refs: body(*refs, **static), out_shape=outs, in_sp...  14.2 us
    all_gather x6, blocking collectives, exchanged(): return lax.all_gather(both, 'gy', axis_index_groups=mates, tiled=True)  11.8 us
    all_to_all x1, blocking collectives, among_chips(): lax.all_to_all(buffer, ('gx', 'gy'), 0, 0, tiled=True, axis_index_groups=...  9.96 us
    all_to_all x1, starting transfers between devices, among_chips(): lax.all_to_all(buffer, ('gx', 'gy'), 0, 0, tiled=True, axis_index_groups=...  4.97 us
  transfers between devices with their start and end apart: 7, of which 1 were waited for; matrix products, arithmetic and copies ran while one was open for 0% of the time, Pallas kernels for 0%

profile of v9, /device:TPU:25, one launch (start us, length us, event | category | flops | bytes accessed | tf_op | source)
XLA Modules:
  0.0 107.0 jit_solution(10807752064252640982)
XLA Ops:
  0.6 2.7 %shard_map.113 = (f32[8,24,128]{2,1,0:T(8,128)}, f32[8,328,128]{2,1,0:T(8,128)}) custom-call(f32[8,8,128]{2,1,0:T(8,128)} %refs_0_.1, f32[8,8,128]{2,1,0:T(8,128)} %refs_1_.1, f32[8,8,128]{2,1,0:T(8,128)} %refs_2_.1, f32[8,8,128]{2,1,0:T(8,128)} %refs_3_.1, f32[8,8,128]{2,1,0:T(8,128)} %refs_4_.1, s32[4,1,2,128]{3,2,1,0:T(2,128)} %refs_5_.1, ...), custom_call_target="tpu_custom_call" | custom-call | tf_op jit(solution)/shard_map/pallas_call | solution.py:363
  3.3 10.0 %all_to_all.10.refs_0_ = f32[8,24,128]{2,1,0:T(8,128)S(1)} all-to-all(f32[8,24,128]{2,1,0:T(8,128)} %get-tuple-element.36), channel_id=1, replica_groups={{0,1,16,17,32,33,48,49},{2,3,18,19,34,35,50,51},{4,5,20,21,36,37,52,53}..., dimensions={0} | all-to-all | bytes 196608 | tf_op jit(solution)/shard_map/all_to_all | solution.py:378
  13.3 5.0 %all-to-all-start = ((f32[8,328,128]{2,1,0:T(8,128)}), f32[8,328,128]{2,1,0:T(8,128)}, u32[]{:S(2)}, u32[]{:S(2)}) async-start(f32[8,328,128]{2,1,0:T(8,128)} %get-tuple-element.35), calls=%async_computation | async-start | bytes 2686976 | tf_op jit(solution)/shard_map/all_to_all | solution.py:378
  18.2 4.4 %collective-permute-start = (f32[32,128]{1,0:T(8,128)S(1)}, f32[32,128]{1,0:T(8,128)S(1)}, u32[]{:S(2)}, u32[]{:S(2)}) collective-permute-start(f32[32,128]{1,0:T(8,128)S(1)} %get-tuple-element.38), channel_id=1, source_target_pairs={{1,2},{3,4},{5,6},{7,8},{9,10},{11,12},{13,14},{2,1},{4,3},{6,5},{... | collective-permute-start | bytes 49160 | tf_op jit(solution)/shard_map/ppermute | solution.py:372
  22.7 11.3 %all_gather.36 = f32[192,128]{1,0:T(8,128)S(1)} all-gather(f32[96,128]{1,0:T(8,128)S(1)} %get-tuple-element.37), channel_id=1, replica_groups={{0,64},{16,80},{32,96},{48,112},{128,192},{144,208},{160,224},{176,240}..., dimensions={0}, use_global_device_ids=true | all-gather | bytes 147456 | tf_op jit(solution)/shard_map/all_gather | solution.py:373
  34.0 2.0 %all_gather.37.refs_1_ = f32[448,128]{1,0:T(8,128)S(1)} all-gather(f32[224,128]{1,0:T(8,128)S(1)} %pad_maximum_fusion), channel_id=1, replica_groups={{0,1},{2,3},{4,5},{6,7},{8,9},{10,11},{12,13},{14,15},{16,17},{18,19},{..., dimensions={0}, use_global_device_ids=true | all-gather | bytes 344064 | tf_op jit(solution)/shard_map/all_gather | solution.py:375
  36.6 2.7 %shard_map.115 = (f32[64,8,128]{2,1,0:T(8,128)S(1)}, f32[64,8,128]{2,1,0:T(8,128)S(1)}, f32[64,8,128]{2,1,0:T(8,128)S(1)}, f32[64,8,128]{2,1,0:T(8,128)S(1)}, f3...) custom-call(f32[8,328,128]{2,1,0:T(8,128)} %all-to-all-done.refs_0_,, ...), custom_call_target="tpu_custom_call" | custom-call | tf_op jit(solution)/shard_map/pallas_call | solution.py:363
  39.3 5.2 %collective-permute-start.1 = (f32[32,128]{1,0:T(8,128)S(1)}, f32[32,128]{1,0:T(8,128)S(1)}, u32[]{:S(2)}, u32[]{:S(2)}) collective-permute-start(f32[32,128]{1,0:T(8,128)S(1)} %get-tuple-element.48), channel_id=1, source_target_pairs={{1,2},{3,4},{5,6},{7,8},{9,10},{11,12},{13,14},{2,1},{4,3},{6,5},{... | collective-permute-start | bytes 49160 | tf_op jit(solution)/shard_map/ppermute | solution.py:372
  44.5 10.9 %all_gather.38 = f32[192,128]{1,0:T(8,128)S(1)} all-gather(f32[96,128]{1,0:T(8,128)S(1)} %get-tuple-element.47), channel_id=1, replica_groups={{0,64},{16,80},{32,96},{48,112},{128,192},{144,208},{160,224},{176,240}..., dimensions={0}, use_global_device_ids=true | all-gather | bytes 147456 | tf_op jit(solution)/shard_map/all_gather | solution.py:373
  55.4 2.0 %all_gather.39.refs_8_ = f32[448,128]{1,0:T(8,128)S(1)} all-gather(f32[224,128]{1,0:T(8,128)S(1)} %pad_maximum_fusion.1), channel_id=1, replica_groups={{0,1},{2,3},{4,5},{6,7},{8,9},{10,11},{12,13},{14,15},{16,17},{18,19},{..., dimensions={0}, use_global_device_ids=true | all-gather | bytes 344064 | tf_op jit(solution)/shard_map/all_gather | solution.py:375
  57.4 2.0 %shard_map.116 = (f32[64,8,128]{2,1,0:T(8,128)S(1)}, f32[32,128]{1,0:T(8,128)S(1)}, f32[96,128]{1,0:T(8,128)S(1)}, f32[32,128]{1,0:T(8,128)S(1)}) custom-call(f32[64,8,128]{2,1,0:T(8,128)S(1)} %get-tuple-element.39.refs_0_, f32[64,8,128]{2,1,0:T(8,128)S(1)} %get-tuple-element.40.refs_1_, f32[64,8,128]{2,1,0:T(8,128)S(1)} %get-tuple-element.41.refs_2_, ...), custom_call_target="tpu_custom_call" | custom-call | tf_op jit(solution)/shard_map/pallas_call | solution.py:363
  59.3 2.3 %collective-permute-start.2 = (f32[32,128]{1,0:T(8,128)S(1)}, f32[32,128]{1,0:T(8,128)S(1)}, u32[]{:S(2)}, u32[]{:S(2)}) collective-permute-start(f32[32,128]{1,0:T(8,128)S(1)} %get-tuple-element.54), channel_id=1, source_target_pairs={{1,2},{3,4},{5,6},{7,8},{9,10},{11,12},{13,14},{2,1},{4,3},{6,5},{... | collective-permute-start | bytes 49160 | tf_op jit(solution)/shard_map/ppermute | solution.py:372
  61.7 4.8 %all_gather.40 = f32[192,128]{1,0:T(8,128)S(1)} all-gather(f32[96,128]{1,0:T(8,128)S(1)} %get-tuple-element.53), channel_id=1, replica_groups={{0,64},{16,80},{32,96},{48,112},{128,192},{144,208},{160,224},{176,240}..., dimensions={0}, use_global_device_ids=true | all-gather | bytes 147456 | tf_op jit(solution)/shard_map/all_gather | solution.py:373
  66.5 2.0 %all_gather.41.refs_8_ = f32[448,128]{1,0:T(8,128)S(1)} all-gather(f32[224,128]{1,0:T(8,128)S(1)} %pad_maximum_fusion.2), channel_id=1, replica_groups={{0,1},{2,3},{4,5},{6,7},{8,9},{10,11},{12,13},{14,15},{16,17},{18,19},{..., dimensions={0}, use_global_device_ids=true | all-gather | bytes 344064 | tf_op jit(solution)/shard_map/all_gather | solution.py:375
  68.5 2.0 %shard_map.117 = (f32[64,8,128]{2,1,0:T(8,128)S(1)}, f32[32,128]{1,0:T(8,128)S(1)}, f32[96,128]{1,0:T(8,128)S(1)}, f32[32,128]{1,0:T(8,128)S(1)}) custom-call(f32[64,8,128]{2,1,0:T(8,128)S(1)} %get-tuple-element.52.refs_0_, f32[64,8,128]{2,1,0:T(8,128)S(1)} %get-tuple-element.40.refs_1_, f32[64,8,128]{2,1,0:T(8,128)S(1)} %get-tuple-element.41.refs_2_, ...), custom_call_target="tpu_custom_call" | custom-call | tf_op jit(solution)/shard_map/pallas_call | solution.py:363
  70.5 4.4 %collective-permute-start.3 = (f32[32,128]{1,0:T(8,128)S(1)}, f32[32,128]{1,0:T(8,128)S(1)}, u32[]{:S(2)}, u32[]{:S(2)}) collective-permute-start(f32[32,128]{1,0:T(8,128)S(1)} %get-tuple-element.58), channel_id=1, source_target_pairs={{1,2},{3,4},{5,6},{7,8},{9,10},{11,12},{13,14},{2,1},{4,3},{6,5},{... | collective-permute-start | bytes 49160 | tf_op jit(solution)/shard_map/ppermute | solution.py:372
  74.9 4.8 %all_gather.42 = f32[192,128]{1,0:T(8,128)S(1)} all-gather(f32[96,128]{1,0:T(8,128)S(1)} %get-tuple-element.57), channel_id=1, replica_groups={{0,64},{16,80},{32,96},{48,112},{128,192},{144,208},{160,224},{176,240}..., dimensions={0}, use_global_device_ids=true | all-gather | bytes 147456 | tf_op jit(solution)/shard_map/all_gather | solution.py:373
  79.7 2.0 %all_gather.43.refs_8_ = f32[448,128]{1,0:T(8,128)S(1)} all-gather(f32[224,128]{1,0:T(8,128)S(1)} %pad_maximum_fusion.3), channel_id=1, replica_groups={{0,1},{2,3},{4,5},{6,7},{8,9},{10,11},{12,13},{14,15},{16,17},{18,19},{..., dimensions={0}, use_global_device_ids=true | all-gather | bytes 344064 | tf_op jit(solution)/shard_map/all_gather | solution.py:375
  83.6 2.3 %collective-permute-start.4 = (f32[32,128]{1,0:T(8,128)S(1)}, f32[32,128]{1,0:T(8,128)S(1)}, u32[]{:S(2)}, u32[]{:S(2)}) collective-permute-start(f32[32,128]{1,0:T(8,128)S(1)} %get-tuple-element.62), channel_id=1, source_target_pairs={{1,2},{3,4},{5,6},{7,8},{9,10},{11,12},{13,14},{2,1},{4,3},{6,5},{... | collective-permute-start | bytes 49160 | tf_op jit(solution)/shard_map/ppermute | solution.py:372
  86.0 4.8 %all_gather.44 = f32[192,128]{1,0:T(8,128)S(1)} all-gather(f32[96,128]{1,0:T(8,128)S(1)} %get-tuple-element.61), channel_id=1, replica_groups={{0,64},{16,80},{32,96},{48,112},{128,192},{144,208},{160,224},{176,240}..., dimensions={0}, use_global_device_ids=true | all-gather | bytes 147456 | tf_op jit(solution)/shard_map/all_gather | solution.py:373
  90.8 2.0 %all_gather.45.refs_8_ = f32[448,128]{1,0:T(8,128)S(1)} all-gather(f32[224,128]{1,0:T(8,128)S(1)} %pad_maximum_fusion.4), channel_id=1, replica_groups={{0,1},{2,3},{4,5},{6,7},{8,9},{10,11},{12,13},{14,15},{16,17},{18,19},{..., dimensions={0}, use_global_device_ids=true | all-gather | bytes 344064 | tf_op jit(solution)/shard_map/all_gather | solution.py:375
  94.8 4.4 %collective-permute-start.5 = (f32[32,128]{1,0:T(8,128)S(1)}, f32[32,128]{1,0:T(8,128)S(1)}, u32[]{:S(2)}, u32[]{:S(2)}) collective-permute-start(f32[32,128]{1,0:T(8,128)S(1)} %get-tuple-element.66), channel_id=1, source_target_pairs={{1,2},{3,4},{5,6},{7,8},{9,10},{11,12},{13,14},{2,1},{4,3},{6,5},{... | collective-permute-start | bytes 49160 | tf_op jit(solution)/shard_map/ppermute | solution.py:372
  99.2 4.8 %all_gather.46 = f32[192,128]{1,0:T(8,128)S(1)} all-gather(f32[96,128]{1,0:T(8,128)S(1)} %get-tuple-element.65), channel_id=1, replica_groups={{0,64},{16,80},{32,96},{48,112},{128,192},{144,208},{160,224},{176,240}..., dimensions={0}, use_global_device_ids=true | all-gather | bytes 147456 | tf_op jit(solution)/shard_map/all_gather | solution.py:373
  104.0 2.0 %all_gather.47.refs_8_ = f32[448,128]{1,0:T(8,128)S(1)} all-gather(f32[224,128]{1,0:T(8,128)S(1)} %pad_maximum_fusion.5), channel_id=1, replica_groups={{0,1},{2,3},{4,5},{6,7},{8,9},{10,11},{12,13},{14,15},{16,17},{18,19},{..., dimensions={0}, use_global_device_ids=true | all-gather | bytes 344064 | tf_op jit(solution)/shard_map/all_gather | solution.py:375
  (17 shorter events, 5.7 us)
Async XLA Ops:
  13.3 23.3 %all-to-all-start = ((f32[8,328,128]{2,1,0:T(8,128)}), f32[8,328,128]{2,1,0:T(8,128)}, u32[]{:S(2)}, u32[]{:S(2)}) async-start(f32[8,328,128]{2,1,0:T(8,128)} %get-tuple-element.35), calls=%async_computation | async-start | bytes 2686976 | tf_op jit(solution)/shard_map/all_to_all | solution.py:378
  18.2 15.7 %collective-permute-start = (f32[32,128]{1,0:T(8,128)S(1)}, f32[32,128]{1,0:T(8,128)S(1)}, u32[]{:S(2)}, u32[]{:S(2)}) collective-permute-start(f32[32,128]{1,0:T(8,128)S(1)} %get-tuple-element.38), channel_id=1, source_target_pairs={{1,2},{3,4},{5,6},{7,8},{9,10},{11,12},{13,14},{2,1},{4,3},{6,5},{... | collective-permute-start | bytes 49160 | tf_op jit(solution)/shard_map/ppermute | solution.py:372
  39.3 16.1 %collective-permute-start.1 = (f32[32,128]{1,0:T(8,128)S(1)}, f32[32,128]{1,0:T(8,128)S(1)}, u32[]{:S(2)}, u32[]{:S(2)}) collective-permute-start(f32[32,128]{1,0:T(8,128)S(1)} %get-tuple-element.48), channel_id=1, source_target_pairs={{1,2},{3,4},{5,6},{7,8},{9,10},{11,12},{13,14},{2,1},{4,3},{6,5},{... | collective-permute-start | bytes 49160 | tf_op jit(solution)/shard_map/ppermute | solution.py:372
  59.3 7.2 %collective-permute-start.2 = (f32[32,128]{1,0:T(8,128)S(1)}, f32[32,128]{1,0:T(8,128)S(1)}, u32[]{:S(2)}, u32[]{:S(2)}) collective-permute-start(f32[32,128]{1,0:T(8,128)S(1)} %get-tuple-element.54), channel_id=1, source_target_pairs={{1,2},{3,4},{5,6},{7,8},{9,10},{11,12},{13,14},{2,1},{4,3},{6,5},{... | collective-permute-start | bytes 49160 | tf_op jit(solution)/shard_map/ppermute | solution.py:372
  70.5 9.2 %collective-permute-start.3 = (f32[32,128]{1,0:T(8,128)S(1)}, f32[32,128]{1,0:T(8,128)S(1)}, u32[]{:S(2)}, u32[]{:S(2)}) collective-permute-start(f32[32,128]{1,0:T(8,128)S(1)} %get-tuple-element.58), channel_id=1, source_target_pairs={{1,2},{3,4},{5,6},{7,8},{9,10},{11,12},{13,14},{2,1},{4,3},{6,5},{... | collective-permute-start | bytes 49160 | tf_op jit(solution)/shard_map/ppermute | solution.py:372
  83.6 7.2 %collective-permute-start.4 = (f32[32,128]{1,0:T(8,128)S(1)}, f32[32,128]{1,0:T(8,128)S(1)}, u32[]{:S(2)}, u32[]{:S(2)}) collective-permute-start(f32[32,128]{1,0:T(8,128)S(1)} %get-tuple-element.62), channel_id=1, source_target_pairs={{1,2},{3,4},{5,6},{7,8},{9,10},{11,12},{13,14},{2,1},{4,3},{6,5},{... | collective-permute-start | bytes 49160 | tf_op jit(solution)/shard_map/ppermute | solution.py:372
  94.8 9.2 %collective-permute-start.5 = (f32[32,128]{1,0:T(8,128)S(1)}, f32[32,128]{1,0:T(8,128)S(1)}, u32[]{:S(2)}, u32[]{:S(2)}) collective-permute-start(f32[32,128]{1,0:T(8,128)S(1)} %get-tuple-element.66), channel_id=1, source_target_pairs={{1,2},{3,4},{5,6},{7,8},{9,10},{11,12},{13,14},{2,1},{4,3},{6,5},{... | collective-permute-start | bytes 49160 | tf_op jit(solution)/shard_map/ppermute | solution.py:372
